TPU v7x, 256 devices: a whole 4x4x8 slice. The times are simulated.
256 devices in a mesh: ctx: 64 (over y, z, core), head: 4 (over x).
Axes of the slice: x: 4, y: 4, z: 8, core: 2. Of those that a mesh axis runs over, the one named last changes fastest.
Arguments:
- lin_query: bfloat16 [8192, 6144], P('ctx', 'head'), may hold values from -6 to 6
- lin_key: bfloat16 [8192, 6144], P('ctx', 'head'), may hold values from -6 to 6
- lin_value: bfloat16 [8192, 6144], P('ctx', 'head'), may hold values from -6 to 6
- soft_query: bfloat16 [8192, 6144], P('ctx', 'head'), may hold values from -6 to 6
- soft_key: bfloat16 [8192, 6144], P('ctx', 'head'), may hold values from -6 to 6
- soft_value: bfloat16 [8192, 6144], P('ctx', 'head'), may hold values from -6 to 6
- upstream: bfloat16 [8192, 6144], P('ctx', 'head'), may hold values from -6 to 6
- doc_lengths: int32 [42], replicated, may hold values from 1 to 384, 8192 in all
- doc_domain: int32 [42], replicated, may hold values from 0 to 7
- domain_weight: float32 [8], replicated, may hold values from 0.25 to 4
Outputs:
- lin_dq: bfloat16 [8192, 6144], P('ctx', 'head')
- lin_dk: bfloat16 [8192, 6144], P('ctx', 'head')
- lin_dv: bfloat16 [8192, 6144], P('ctx', 'head')
- soft_dq: bfloat16 [8192, 6144], P('ctx', 'head')
- soft_dk: bfloat16 [8192, 6144], P('ctx', 'head')
- soft_dv: bfloat16 [8192, 6144], P('ctx', 'head')
- domain_loss: float32 [8], replicated
Inputs may be any that keep to these rules, and one draw needn't show every extreme that they name: `doc_lengths`: whole documents fill the sequence in order; the longest has exactly 384 tokens.
All inputs are finite; a program needn't handle non-finite values.
Results may differ from a plain program's by a relative error of at most 0.029.
Values may be sent and summed in bfloat16 or wider, within the bound.
No kernel may reach another device: no remote copies, remote signals or barrier semaphores. Data moves between devices by JAX's collectives and lax.ppermute only.
A program may use at most 192 MiB of HBM per device.

v0:
```python
import jax
import jax.numpy as jnp
from jax import lax
from jax.sharding import PartitionSpec as P

HD = 128
REACH = 3
DOC_MOST = 384


def prefix(part, axis, combine, identity, reverse):
    count = lax.axis_size(axis)
    place = lax.axis_index(axis)
    ahead = count - 1 - place if reverse else place
    gathered = jax.tree.map(lambda a: lax.all_gather(a, axis), part)
    state = jax.tree.map(lambda a, e: jnp.zeros_like(a) + jnp.asarray(e, a.dtype), part, identity)

    def one(lap, state):
        source = count - 1 - lap if reverse else lap
        return combine(
            state, jax.tree.map(lambda a: lax.dynamic_index_in_dim(a, source, 0, False), gathered)
        )

    return lax.fori_loop(0, ahead, one, state)


def passed_along(x, axis, by):
    length = lax.axis_size(axis)
    pairs = [(i, i + by) for i in range(length) if 0 <= i + by < length]
    return lax.ppermute(x, axis, pairs)


def token_docs(doc_lengths, positions):
    doc_ends = jnp.cumsum(doc_lengths)
    doc_starts = doc_ends - doc_lengths
    inside = (doc_starts[None, :] <= positions[:, None]) & (positions[:, None] < doc_ends[None, :])
    numbers = jnp.arange(1, doc_lengths.shape[0] + 1, dtype=jnp.int32)
    doc_index = jnp.sum(jnp.where(inside, numbers[None, :], 0), axis=1) - 1
    doc_begin = jnp.sum(jnp.where(inside, doc_starts[None, :], 0), axis=1)
    doc_finish = jnp.sum(jnp.where(inside, doc_ends[None, :], 0), axis=1)
    return (inside, doc_index, doc_begin, doc_finish)


def token_weights(inside, doc_domain, domain_weight):
    domain_of = jnp.sum(jnp.where(inside, doc_domain[None, :], 0), axis=1)
    domain_ids = jnp.arange(domain_weight.shape[0], dtype=jnp.int32)
    domain_hot = (domain_of[:, None] == domain_ids[None, :]).astype(jnp.float32)
    return (jnp.sum(domain_hot * domain_weight[None, :], axis=1), domain_hot)


def combine(earlier, later):
    return (later[0] + (1.0 - later[1]) * earlier[0], jnp.maximum(earlier[1], later[1]))


def on_device(
    lin_query,
    lin_key,
    lin_value,
    soft_query,
    soft_key,
    soft_value,
    upstream,
    doc_lengths,
    doc_domain,
    domain_weight,
):
    tok_rows, feat_cols = lin_query.shape
    head_count = feat_cols // HD
    linear_scale = (HD * DOC_MOST) ** (-0.5)
    soft_scale = HD ** (-0.5)
    highest_index = lax.Precision.HIGHEST
    row_start = lax.axis_index("ctx") * tok_rows
    row_end = row_start + tok_rows
    order = jnp.arange(tok_rows, dtype=jnp.int32)
    positions = row_start + order
    inside, doc_index, doc_begin, doc_finish = token_docs(doc_lengths, positions)
    weights, domain_hot = token_weights(inside, doc_domain, domain_weight)
    grad_flat = (weights[:, None] * upstream.astype(jnp.float32)).astype(jnp.bfloat16)

    def heads_of(array):
        return array.reshape(array.shape[0], head_count, HD)

    query_rows, key_rows, value_rows, gradient_heads = (
        heads_of(lin_query),
        heads_of(lin_key),
        heads_of(lin_value),
        heads_of(grad_flat),
    )
    last_onehot = (doc_index == doc_index[tok_rows - 1]).astype(jnp.bfloat16)[:, None, None]
    local_state = jnp.einsum(
        "lzd,lzj->zdj", key_rows * last_onehot, value_rows, preferred_element_type=jnp.float32
    )
    flag_left = (doc_begin[tok_rows - 1] >= row_start).astype(jnp.float32)
    first_onehot = (doc_index == doc_index[0]).astype(jnp.bfloat16)[:, None, None]
    later_local = jnp.einsum(
        "cis,ciy->isy",
        query_rows * first_onehot,
        gradient_heads,
        preferred_element_type=jnp.float32,
    )
    flag_right = (doc_finish[0] <= row_end).astype(jnp.float32)
    identity = (jnp.zeros((head_count, HD, HD), jnp.float32), jnp.zeros((), jnp.float32))
    preceding_state, _ = prefix((local_state, flag_left), "ctx", combine, identity, False)
    subsequent_state, _ = prefix((later_local, flag_right), "ctx", combine, identity, True)
    allowed = (doc_index[:, None] == doc_index[None, :]) & (order[None, :] <= order[:, None])
    lin_scores = jnp.where(
        allowed[None],
        linear_scale
        * jnp.einsum("thd,shd->hts", query_rows, key_rows, preferred_element_type=jnp.float32),
        0.0,
    ).astype(jnp.bfloat16)
    lin_back = jnp.where(
        allowed[None],
        linear_scale
        * jnp.einsum(
            "thd,shd->hts", gradient_heads, value_rows, preferred_element_type=jnp.float32
        ),
        0.0,
    ).astype(jnp.bfloat16)
    carried_along = (doc_begin < row_start).astype(jnp.float32)[:, None, None]
    extended_rows = (doc_finish > row_end).astype(jnp.float32)[:, None, None]
    inner = jnp.einsum("hts,shd->thd", lin_scores, value_rows, preferred_element_type=jnp.float32)
    outer_product = (
        linear_scale
        * carried_along
        * jnp.einsum(
            "jlb,lbw->jlw", query_rows.astype(jnp.float32), preceding_state, precision=highest_index
        )
    )
    lin_out = (inner + outer_product).astype(jnp.bfloat16).reshape(tok_rows, feat_cols)
    dq_inner = jnp.einsum("hts,shd->thd", lin_back, key_rows, preferred_element_type=jnp.float32)
    outer_query_gradient = (
        linear_scale
        * carried_along
        * jnp.einsum(
            "nmu,meu->nme",
            gradient_heads.astype(jnp.float32),
            preceding_state,
            precision=highest_index,
        )
    )
    lin_dq = (dq_inner + outer_query_gradient).astype(jnp.bfloat16).reshape(tok_rows, feat_cols)
    dk_inner = jnp.einsum("hts,thd->shd", lin_back, query_rows, preferred_element_type=jnp.float32)
    outer_key_gradient = (
        linear_scale
        * extended_rows
        * jnp.einsum(
            "mdx,dwx->mdw",
            value_rows.astype(jnp.float32),
            subsequent_state,
            precision=highest_index,
        )
    )
    lin_dk = (dk_inner + outer_key_gradient).astype(jnp.bfloat16).reshape(tok_rows, feat_cols)
    dv_inner = jnp.einsum(
        "hts,thd->shd", lin_scores, gradient_heads, preferred_element_type=jnp.float32
    )
    outer_value_gradient = (
        linear_scale
        * extended_rows
        * jnp.einsum(
            "nzt,zti->nzi", key_rows.astype(jnp.float32), subsequent_state, precision=highest_index
        )
    )
    lin_dv = (dv_inner + outer_value_gradient).astype(jnp.bfloat16).reshape(tok_rows, feat_cols)
    fetched = [
        passed_along((soft_key, soft_value), "ctx", offset) for offset in range(1, REACH + 1)
    ]
    key_window = jnp.concatenate(
        [fetched[REACH - 1 - offset][0] for offset in range(REACH)] + [soft_key], axis=0
    )
    value_window = jnp.concatenate(
        [fetched[REACH - 1 - offset][1] for offset in range(REACH)] + [soft_value], axis=0
    )
    window_rows = key_window.shape[0]
    key_heads = heads_of(key_window)
    value_heads = heads_of(value_window)
    soft_heads_q = heads_of(soft_query)
    positions_k = row_start - REACH * tok_rows + jnp.arange(window_rows, dtype=jnp.int32)
    _, key_docs, _, _ = token_docs(doc_lengths, positions_k)
    allowed_keys = (
        (key_docs[None, :] == doc_index[:, None])
        & (positions_k[None, :] <= positions[:, None])
        & (positions_k[None, :] >= 0)
    )
    scores = soft_scale * jnp.einsum(
        "thd,shd->hts", soft_heads_q, key_heads, preferred_element_type=jnp.float32
    )
    scores = jnp.where(allowed_keys[None], scores, -jnp.inf)
    row_max = jnp.max(scores, axis=2, keepdims=True)
    log_total = row_max + jnp.log(jnp.sum(jnp.exp(scores - row_max), axis=2, keepdims=True))
    soft_prob = jnp.exp(scores - log_total)
    soft_weights = soft_prob.astype(jnp.bfloat16)
    soft_out = jnp.einsum(
        "hts,shd->thd", soft_weights, value_heads, preferred_element_type=jnp.float32
    ).astype(jnp.bfloat16)
    delta = jnp.sum(gradient_heads.astype(jnp.float32) * soft_out.astype(jnp.float32), axis=2)
    grad_prob = jnp.einsum(
        "thd,shd->hts", gradient_heads, value_heads, preferred_element_type=jnp.float32
    )
    soft_ds = (soft_prob * (grad_prob - delta.T[:, :, None]) * soft_scale).astype(jnp.bfloat16)
    soft_dq = (
        jnp.einsum("hts,shd->thd", soft_ds, key_heads, preferred_element_type=jnp.float32)
        .astype(jnp.bfloat16)
        .reshape(tok_rows, feat_cols)
    )
    key_grad = jnp.einsum(
        "hts,thd->shd", soft_ds, soft_heads_q, preferred_element_type=jnp.float32
    ).reshape(REACH + 1, tok_rows, feat_cols)
    value_grad = jnp.einsum(
        "hts,thd->shd", soft_weights, gradient_heads, preferred_element_type=jnp.float32
    ).reshape(REACH + 1, tok_rows, feat_cols)
    returned = [
        passed_along((key_grad[REACH - offset], value_grad[REACH - offset]), "ctx", -offset)
        for offset in range(1, REACH + 1)
    ]
    key_total = key_grad[REACH]
    value_total = value_grad[REACH]
    for pieces in returned:
        key_total = key_total + pieces[0]
        value_total = value_total + pieces[1]
    soft_dk = key_total.astype(jnp.bfloat16)
    soft_dv = value_total.astype(jnp.bfloat16)
    soft_flat = soft_out.reshape(tok_rows, feat_cols)
    contrib = weights * jnp.sum(
        upstream.astype(jnp.float32)
        * (lin_out.astype(jnp.float32) + soft_flat.astype(jnp.float32)),
        axis=1,
    )
    partial_loss = jnp.sum(contrib[:, None] * domain_hot, axis=0)
    domain_loss = lax.psum(partial_loss, ("ctx", "head"))
    return (lin_dq, lin_dk, lin_dv, soft_dq, soft_dk, soft_dv, domain_loss)


def solution(mesh):
    placed = (
        P("ctx", "head"),
        P("ctx", "head"),
        P("ctx", "head"),
        P("ctx", "head"),
        P("ctx", "head"),
        P("ctx", "head"),
        P("ctx", "head"),
        P(),
        P(),
        P(),
    )
    return jax.shard_map(
        on_device,
        mesh=mesh,
        in_specs=placed,
        out_specs=(
            P("ctx", "head"),
            P("ctx", "head"),
            P("ctx", "head"),
            P("ctx", "head"),
            P("ctx", "head"),
            P("ctx", "head"),
            P(),
        ),
        check_vma=False,
    )
```

profile of v0, /device:TPU:1, one launch (start us, length us, event | category | flops | bytes accessed | tf_op | source)
XLA Modules:
  0.0 871.8 jit_solution(14858116202687606455)
XLA Ops:
  13.9 1.9 compare_convert_fusion
  17.3 4.9 collective-permute-start.5
  22.3 4.3 collective-permute-start.4
  26.8 1.9 collective-permute-start.2
  28.8 3.1 collective-permute-start.1
  31.9 6.4 collective-permute-start
  39.2 1.6 and_and_fusion
  49.0 158.0 %all-reduce.2 = (f32[64]{0:T(128)}, f32[64]{0:T(128)}) all-reduce(f32[64]{0:T(128)S(1)} %dynamic-update-slice, f32[64]{0:T(128)S(1)} %dynamic-update-slice.1), channel_id=1, replica_groups=mesh['ctx'=64,'head'=4] {'ctx'}, use_global_device_ids=true, to_apply=%add | all-reduce | flops 128 | bytes 1024
  211.4 1.6 pad_maximum_fusion
  214.5 14.3 %collective-permute-done.3 = bf16[128,1536]{0,1:T(8,128)(2,1)S(1)} collective-permute-done((bf16[128,1536]{0,1:T(8,128)(2,1)S(1)}, bf16[128,1536]{0,1:T(8,128)(2,1)S(1)}, u32[]{:S(2)}, u32[]{:S(2)}) %collective-permute-start.3) | collective-permute-done | bytes 393248 | tf_op jit(solution)/shard_map/ppermute | solution.py:30
  231.3 1.9 fusion.19
  233.2 15.3 %all-gather.5.cloned.1.call-done = f32[768,128,128]{2,1,0:T(8,128)} async-done(((f32[12,128,128]{2,1,0:T(8,128)}), f32[768,128,128]{2,1,0:T(8,128)}) %all-gather.5.cloned.1.call-update) | async-done | bytes 50331664 | tf_op jit(solution)/shard_map/all_gather | solution.py:15
  248.6 2.7 while.26
  249.8 1.4 bitcast_add_fusion.4
  252.1 2.6 fusion.15
  254.7 2.3 copy.198
  257.0 2.5 fusion.21
  260.8 2.3 fusion.22
  265.8 237.8 %psum.7 = f32[8]{0:T(128)} all-reduce(f32[8]{0:T(128)S(1)} %select_reduce_fusion.5), channel_id=1, replica_groups=mesh['ctx'=64,'head'=4] {'ctx','head'}, use_global_device_ids=true, to_apply=%region_16.17 | all-reduce | flops 8 | bytes 64 | tf_op jit(solution)/shard_map/psum | solution.py:231
  504.8 3.7 multiply_convert_fusion
  509.9 1.9 copy.202
  511.8 3.0 convolution_bitcast_fusion
  514.8 1.8 fusion.35
  516.6 2.4 copy.192
  519.1 2.4 copy.195
  521.5 2.3 copy.194
  526.4 3.0 collective-permute-start.9
  529.4 1.6 convolution_bitcast_fusion.1
  531.0 1.6 fusion.36
  532.6 2.3 copy.187
  534.9 2.4 copy.190
  542.6 19.2 %collective-permute-done.10 = f32[128,1536]{1,0:T(8,128)} collective-permute-done((f32[128,1536]{1,0:T(8,128)}, f32[128,1536]{1,0:T(8,128)}, u32[]{:S(2)}, u32[]{:S(2)}) %collective-permute-start.10) | collective-permute-done | bytes 786464 | tf_op jit(solution)/shard_map/ppermute | solution.py:30
  561.8 4.3 collective-permute-start.6
  569.0 37.6 %collective-permute-done.11 = f32[128,1536]{1,0:T(8,128)} collective-permute-done((f32[128,1536]{1,0:T(8,128)}, f32[128,1536]{1,0:T(8,128)}, u32[]{:S(2)}, u32[]{:S(2)}) %collective-permute-start.11) | collective-permute-done | bytes 786464 | tf_op jit(solution)/shard_map/ppermute | solution.py:30
  606.6 2.8 add_convert_fusion
  609.4 28.3 %collective-permute-done.7 = f32[128,1536]{1,0:T(8,128)} collective-permute-done((f32[128,1536]{1,0:T(8,128)}, f32[128,1536]{1,0:T(8,128)}, u32[]{:S(2)}, u32[]{:S(2)}) %collective-permute-start.7) | collective-permute-done | bytes 786464 | tf_op jit(solution)/shard_map/ppermute | solution.py:30
  637.7 59.9 %collective-permute-done.8 = f32[128,1536]{1,0:T(8,128)} collective-permute-done((f32[128,1536]{1,0:T(8,128)}, f32[128,1536]{1,0:T(8,128)}, u32[]{:S(2)}, u32[]{:S(2)}) %collective-permute-start.8) | collective-permute-done | bytes 786464 | tf_op jit(solution)/shard_map/ppermute | solution.py:30
  697.6 2.5 add_convert_fusion.1
  700.2 161.0 %while.27 = (s32[]{:T(128)}, f32[12,128,128]{2,1,0:T(8,128)S(1)}, s32[]{:T(128)}, f32[64,12,128,128]{3,2,1,0:T(8,128)}, f32[64]{0:T(128)S(1)}, /*index=5*/s32[]{...) while((s32[]{:T(128)}, f32[12,128,128]{2,1,0:T(8,128)S(1)}, s32[]{:T(128)}, ...), condition=%wide.region_9.10_spmd, body=%wide.region_8.9_spmd.sunk | while | flops 393223 | bytes 2359483 | solution.py:24
  701.3 1.4 bitcast_add_fusion.5
  703.9 1.4 bitcast_add_fusion.5
  709.1 1.4 bitcast_add_fusion.5
  714.3 1.4 bitcast_add_fusion.5
  719.5 1.4 bitcast_add_fusion.5
  722.1 1.4 bitcast_add_fusion.5
  727.3 1.4 bitcast_add_fusion.5
  732.5 1.4 bitcast_add_fusion.5
  735.1 1.4 bitcast_add_fusion.5
  (247 shorter events, 157.9 us)
Async XLA Ops:
  7.2 9.9 %copy-start.15 = (bf16[128,1536]{1,0:T(8,128)(2,1)S(1)}, bf16[128,1536]{1,0:T(8,128)(2,1)}, u32[]{:S(2)}) copy-start(bf16[128,1536]{1,0:T(8,128)(2,1)} %param.19) | copy-start | bytes 1179652
  7.2 19.4 %copy-start.16 = (bf16[128,1536]{1,0:T(8,128)(2,1)S(1)}, bf16[128,1536]{1,0:T(8,128)(2,1)}, u32[]{:S(2)}) copy-start(bf16[128,1536]{1,0:T(8,128)(2,1)} %param.18) | copy-start | bytes 1179652
  7.2 37.3 %copy-start.17 = (bf16[128,1536]{1,0:T(8,128)(2,1)S(1)}, bf16[128,1536]{1,0:T(8,128)(2,1)}, u32[]{:S(2)}) copy-start(bf16[128,1536]{1,0:T(8,128)(2,1)} %param.14) | copy-start | bytes 1179652
  7.2 241.3 %all-gather.5.cloned.1.call-start = ((), (), s32[]{:S(2)}) async-start(), calls=%async_computation | async-start | bytes 51118080 | tf_op jit(solution)/shard_map/all_gather | solution.py:15
  7.3 3.0 copy-start.25
  10.3 0.5 copy-start.21
  17.1 683.0 %all-gather.7.cloned.1.call-start = ((), (), s32[]{:S(2)}) async-start(), calls=%async_computation.1 | async-start | bytes 51118080 | tf_op jit(solution)/shard_map/all_gather | solution.py:15
  17.3 197.2 %collective-permute-start.5 = (bf16[128,1536]{0,1:T(8,128)(2,1)S(1)}, bf16[128,1536]{0,1:T(8,128)(2,1)}, u32[]{:S(2)}, u32[]{:S(2)}) collective-permute-start(bf16[128,1536]{0,1:T(8,128)(2,1)S(1)} %copy.177), channel_id=1, source_target_pairs={{0,4},{4,8},{8,12},{12,16},{16,20},{20,24},{24,28},{28,32},{32,36}... | collective-permute-start | bytes 1179656 | tf_op jit(solution)/shard_map/ppermute | solution.py:30
  22.3 192.3 %collective-permute-start.4 = (bf16[128,1536]{0,1:T(8,128)(2,1)S(1)}, bf16[128,1536]{0,1:T(8,128)(2,1)}, u32[]{:S(2)}, u32[]{:S(2)}) collective-permute-start(bf16[128,1536]{0,1:T(8,128)(2,1)S(1)} %copy.177), channel_id=1, source_target_pairs={{0,8},{4,12},{8,16},{12,20},{16,24},{20,28},{24,32},{28,36},{32,40... | collective-permute-start | bytes 1179656 | tf_op jit(solution)/shard_map/ppermute | solution.py:30
  26.8 183.9 %copy-start.8 = (bf16[128,1536]{0,1:T(8,128)(2,1)}, bf16[128,1536]{0,1:T(8,128)(2,1)S(1)}, u32[]{:S(2)}) copy-start(bf16[128,1536]{0,1:T(8,128)(2,1)S(1)} %copy.170) | copy-start | bytes 1179652
  26.8 182.5 %collective-permute-start.2 = (bf16[128,1536]{0,1:T(8,128)(2,1)S(1)}, bf16[128,1536]{0,1:T(8,128)(2,1)S(1)}, u32[]{:S(2)}, u32[]{:S(2)}) collective-permute-start(bf16[128,1536]{0,1:T(8,128)(2,1)S(1)} %copy.170), channel_id=1, source_target_pairs={{0,4},{4,8},{8,12},{12,16},{16,20},{20,24},{24,28},{28,32},{32,36}... | collective-permute-start | bytes 1179656 | tf_op jit(solution)/shard_map/ppermute | solution.py:30
  28.8 181.9 %collective-permute-start.1 = (bf16[128,1536]{0,1:T(8,128)(2,1)S(1)}, bf16[128,1536]{0,1:T(8,128)(2,1)S(1)}, u32[]{:S(2)}, u32[]{:S(2)}) collective-permute-start(bf16[128,1536]{0,1:T(8,128)(2,1)S(1)} %copy.170), channel_id=1, source_target_pairs={{0,8},{4,12},{8,16},{12,20},{16,24},{20,28},{24,32},{28,36},{32,40... | collective-permute-start | bytes 1179656 | tf_op jit(solution)/shard_map/ppermute | solution.py:30
  31.9 179.6 %collective-permute-start = (bf16[128,1536]{0,1:T(8,128)(2,1)S(1)}, bf16[128,1536]{0,1:T(8,128)(2,1)}, u32[]{:S(2)}, u32[]{:S(2)}) collective-permute-start(bf16[128,1536]{0,1:T(8,128)(2,1)S(1)} %copy.170), channel_id=1, source_target_pairs={{0,12},{4,16},{8,20},{12,24},{16,28},{20,32},{24,36},{28,40},{32,4... | collective-permute-start | bytes 1179656 | tf_op jit(solution)/shard_map/ppermute | solution.py:30
  39.2 174.7 %copy-start.19 = (pred[128,128]{1,0:T(8,128)(4,1)}, pred[128,128]{1,0:T(8,128)(4,1)S(1)}, u32[]{:S(2)}) copy-start(pred[128,128]{1,0:T(8,128)(4,1)S(1)} %fusion.28) | copy-start | bytes 49156
  44.8 206.5 %copy-start.3 = (bf16[128,1536]{0,1:T(8,128)(2,1)}, bf16[128,1536]{0,1:T(8,128)(2,1)S(1)}, u32[]{:S(2)}) copy-start(bf16[128,1536]{0,1:T(8,128)(2,1)S(1)} %copy.163) | copy-start | bytes 1179652
  46.1 167.7 %copy-start.5 = (bf16[128,1536]{0,1:T(8,128)(2,1)}, bf16[128,1536]{0,1:T(8,128)(2,1)S(1)}, u32[]{:S(2)}) copy-start(bf16[128,1536]{0,1:T(8,128)(2,1)S(1)} %copy.174) | copy-start | bytes 1179652
  207.0 6.0 copy-start.12
  209.3 1.3 copy-start.13
  209.3 19.5 %collective-permute-start.3 = (bf16[128,1536]{0,1:T(8,128)(2,1)S(1)}, bf16[128,1536]{0,1:T(8,128)(2,1)S(1)}, u32[]{:S(2)}, u32[]{:S(2)}) collective-permute-start(bf16[128,1536]{0,1:T(8,128)(2,1)S(1)} %copy.177), channel_id=1, source_target_pairs={{0,12},{4,16},{8,20},{12,24},{16,28},{20,32},{24,36},{28,40},{32,4... | collective-permute-start | bytes 1179656 | tf_op jit(solution)/shard_map/ppermute | solution.py:30
  210.7 0.7 copy-start.14
  213.8 16.3 %copy-start = (f32[12,512,128]{2,1,0:T(8,128)}, f32[12,512,128]{2,1,0:T(8,128)S(1)}, u32[]{:S(2)}) copy-start(f32[12,512,128]{2,1,0:T(8,128)S(1)} %get-tuple-element.206) | copy-start | bytes 9437188
  230.1 1.2 copy-start.7
  231.3 17.2 %copy-start.28 = (f32[64]{0:T(128)S(1)}, f32[64]{0:T(128)}, u32[]{:S(2)}) copy-start(f32[64]{0:T(128)} %get-tuple-element.275) | copy-start | bytes 772
  248.6 2.7 copy-start.22
  251.3 5.7 copy-start.26
  252.1 4.9 copy-start.18
  252.1 8.7 copy-start.24
  508.5 1.3 copy-start.1
  516.6 12.7 %copy-start.2 = (bf16[12,128,512]{1,2,0:T(8,128)(2,1)S(1)}, bf16[12,128,512]{1,2,0:T(8,128)(2,1)}, u32[]{:S(2)}) copy-start(bf16[12,128,512]{1,2,0:T(8,128)(2,1)} %copy-done.1) | copy-start | bytes 4718596
  523.8 38.1 %collective-permute-start.10 = (f32[128,1536]{1,0:T(8,128)}, f32[128,1536]{1,0:T(8,128)}, u32[]{:S(2)}, u32[]{:S(2)}) collective-permute-start(f32[128,1536]{1,0:T(8,128)} %copy.194), channel_id=1, source_target_pairs={{8,0},{12,4},{16,8},{20,12},{24,16},{28,20},{32,24},{36,28},{40,32... | collective-permute-start | bytes 2359304 | tf_op jit(solution)/shard_map/ppermute | solution.py:30
  525.1 81.5 %collective-permute-start.11 = (f32[128,1536]{1,0:T(8,128)}, f32[128,1536]{1,0:T(8,128)}, u32[]{:S(2)}, u32[]{:S(2)}) collective-permute-start(f32[128,1536]{1,0:T(8,128)} %copy.195), channel_id=1, source_target_pairs={{12,0},{16,4},{20,8},{24,12},{28,16},{32,20},{36,24},{40,28},{44,3... | collective-permute-start | bytes 2359304 | tf_op jit(solution)/shard_map/ppermute | solution.py:30
  526.4 80.2 %collective-permute-start.9 = (f32[128,1536]{1,0:T(8,128)}, f32[128,1536]{1,0:T(8,128)}, u32[]{:S(2)}, u32[]{:S(2)}) collective-permute-start(f32[128,1536]{1,0:T(8,128)} %copy.192), channel_id=1, source_target_pairs={{4,0},{8,4},{12,8},{16,12},{20,16},{24,20},{28,24},{32,28},{36,32}... | collective-permute-start | bytes 2359304 | tf_op jit(solution)/shard_map/ppermute | solution.py:30
  532.6 8.6 copy-start.20
  538.4 29.1 %copy-start.6 = (f32[128,12,128]{0,2,1:T(8,128)S(1)}, f32[128,12,128]{0,2,1:T(8,128)}, u32[]{:S(2)}) copy-start(f32[128,12,128]{0,2,1:T(8,128)} %get-tuple-element.194) | copy-start | bytes 2359300
  538.4 99.3 %collective-permute-start.7 = (f32[128,1536]{1,0:T(8,128)}, f32[128,1536]{1,0:T(8,128)}, u32[]{:S(2)}, u32[]{:S(2)}) collective-permute-start(f32[128,1536]{1,0:T(8,128)} %copy.189), channel_id=1, source_target_pairs={{8,0},{12,4},{16,8},{20,12},{24,16},{28,20},{32,24},{36,28},{40,32... | collective-permute-start | bytes 2359304 | tf_op jit(solution)/shard_map/ppermute | solution.py:30
  539.9 157.7 %collective-permute-start.8 = (f32[128,1536]{1,0:T(8,128)}, f32[128,1536]{1,0:T(8,128)}, u32[]{:S(2)}, u32[]{:S(2)}) collective-permute-start(f32[128,1536]{1,0:T(8,128)} %copy.190), channel_id=1, source_target_pairs={{12,0},{16,4},{20,8},{24,12},{28,16},{32,20},{36,24},{40,28},{44,3... | collective-permute-start | bytes 2359304 | tf_op jit(solution)/shard_map/ppermute | solution.py:30
  541.5 25.1 %copy-start.10 = (bf16[12,128,128]{2,1,0:T(8,128)(2,1)}, bf16[12,128,128]{2,1,0:T(8,128)(2,1)S(1)}, u32[]{:S(2)}) copy-start(bf16[12,128,128]{2,1,0:T(8,128)(2,1)S(1)} %fusion.11) | copy-start | bytes 1179652
  561.8 135.7 %collective-permute-start.6 = (f32[128,1536]{1,0:T(8,128)}, f32[128,1536]{1,0:T(8,128)}, u32[]{:S(2)}, u32[]{:S(2)}) collective-permute-start(f32[128,1536]{1,0:T(8,128)} %copy.187), channel_id=1, source_target_pairs={{4,0},{8,4},{12,8},{16,12},{20,16},{24,20},{28,24},{32,28},{36,32}... | collective-permute-start | bytes 2359304 | tf_op jit(solution)/shard_map/ppermute | solution.py:30
  568.9 131.2 %copy-start.27 = (f32[64]{0:T(128)S(1)}, f32[64]{0:T(128)}, u32[]{:S(2)}) copy-start(f32[64]{0:T(128)} %get-tuple-element.302) | copy-start | bytes 772
  700.2 161.1 %copy-start.23 = (f32[128]{0:T(128)S(1)}, f32[128]{0:T(128)}, u32[]{:S(2)}) copy-start(f32[128]{0:T(128)} %compare_select_fusion) | copy-start | bytes 1540
  861.2 1.3 copy-start.4
  861.3 1.3 copy-start.11
  861.3 1.6 copy-start.9
Sparse Core Ops, SparseCore 0:
  17.2 231.2 all-gather.4
  263.3 421.5 all-gather.6
where the time goes:
time: 878 us; the launch traced here: 872 us
  blocking collectives  396 us (45%)
  waiting for transfers between devices  175 us (20%)
  other arithmetic  115 us (13%)
  local copies, waits for them, and re-layouts  73.9 us (8%)
  loops' own time  37.7 us (4%)
  starting transfers between devices  34.6 us (4%)
  matrix products  24.1 us (3%)
  between operations  16.1 us (2%)
    psum x1, blocking collectives, on_device(): domain_loss = lax.psum(partial_loss, ('ctx', 'head'))  238 us
    ppermute x12, waiting for transfers between devices, passed_along(): return lax.ppermute(x, axis, pairs)  159 us
    unnamed x1, blocking collectives  158 us
    add x63, other arithmetic, combine(): later[0] + (1.0 - later[1]) * earlier[0]  90.8 us
    another operation x2, loops' own time, prefix(): return lax.fori_loop(0, ahead, one, state)  37.7 us
    dynamic_slice x63, local copies, waits for them, and re-layouts, one(): lax.dynamic_index_in_dim(a, source, 0, False)  35.3 us
    ppermute x12, starting transfers between devices, passed_along(): return lax.ppermute(x, axis, pairs)  34.5 us
  transfers between devices with their start and end apart: 14, of which 6 were waited for; matrix products, arithmetic and copies ran while one was open for 7% of the time, Pallas kernels for 0%

commit v1 on v0

v1 whole, which is shorter than its diff:
```python
import functools

import jax
import jax.numpy as jnp
from jax import lax
from jax.experimental import pallas as pl
from jax.experimental.pallas import tpu as pltpu
from jax.sharding import PartitionSpec as P

HD = 128
DOC_MOST = 384
NDOM = 8
LIN_SCALE = (HD * DOC_MOST) ** (-0.5)
SOFT_SCALE = HD ** (-0.5)
LOG2E = 1.4426950408889634
NEG = -1e30
HEADS_STEP = 4
VMEM = 40 * 1024 * 1024

F32 = jnp.float32
BF16 = jnp.bfloat16


def nn(a, b):
    return lax.dot_general(a, b, (((1,), (0,)), ((), ())), preferred_element_type=F32)


def nt(a, b):
    return lax.dot_general(a, b, (((1,), (1,)), ((), ())), preferred_element_type=F32)


def tn(a, b):
    return lax.dot_general(a, b, (((0,), (0,)), ((), ())), preferred_element_type=F32)


def iota(shape, dim):
    return lax.broadcasted_iota(jnp.int32, shape, dim).astype(F32)


def cols(h):
    return slice(h * HD, (h + 1) * HD)


def pack_kernel(lens, doms, wts, place, lq, lk, lv, sq, sk, sv, up, f_out, b_out, mr, mc):
    rows = lq.shape[0]

    @pl.when(pl.program_id(0) == 0)
    def _():
        first = place[0] * rows
        pos = first + lax.broadcasted_iota(jnp.int32, (1, HD), 1)

        def one(i, carry):
            start, begin, end, dom, wt = carry
            stop = start + lens[i]
            inside = (pos >= start) & (pos < stop)
            begin = jnp.where(inside, start.astype(F32), begin)
            end = jnp.where(inside, stop.astype(F32), end)
            dom = jnp.where(inside, doms[i].astype(F32), dom)
            wt = jnp.where(inside, wts[doms[i]], wt)
            return stop, begin, end, dom, wt

        zero = jnp.zeros((1, HD), F32)
        _, begin, end, dom, wt = lax.fori_loop(
            0, lens.shape[0], one, (jnp.int32(0), zero, zero, zero, zero)
        )
        mr[0:1, :] = begin
        mr[1:2, :] = end
        mr[2:3, :] = dom
        mr[3:4, :] = wt
        mr[4:8, :] = jnp.zeros((4, HD), F32)
        square = (rows, HD)
        mc[0:rows, :] = jnp.broadcast_to(begin, square).T
        mc[rows : 2 * rows, :] = jnp.broadcast_to(end, square).T
        mc[2 * rows : 3 * rows, :] = jnp.broadcast_to(wt, square).T

    begin_c = mc[0:rows, :]
    weight = mc[2 * rows : 3 * rows, :]
    in_last = (begin_c == begin_c[rows - 1 : rows, :]).astype(BF16)
    in_first = (begin_c == begin_c[0:1, :]).astype(BF16)
    f_out[0:rows, :] = sk[...]
    f_out[rows : 2 * rows, :] = sv[...]
    b_out[0:rows, :] = sq[...]
    for h in range(HEADS_STEP):
        c = cols(h)
        grad = (weight * up[:, c].astype(F32)).astype(BF16)
        b_out[rows : 2 * rows, c] = grad
        f_out[2 * rows : 3 * rows, c] = tn(lk[:, c] * in_last, lv[:, c]).astype(BF16)
        b_out[2 * rows : 3 * rows, c] = tn(lq[:, c] * in_first, grad).astype(BF16)


def query_kernel(place, mr, mc, f_own, b_own, lq, lk, lv, wr, wa, wx, sdq, ldq, stats, bias, cm, acc, soft):
    rows = lq.shape[0]
    step = pl.program_id(0)
    block = place[0]
    odd = block % 2
    offs = (2, jnp.where(odd == 1, 3, 1), jnp.where(odd == 1, 1, 3))
    square = (rows, HD)

    @pl.when(step == 0)
    def _():
        begin = mr[0:1, :]
        sub, lane = iota(square, 0), iota(square, 1)
        for i, o in enumerate(offs):
            pos = ((block - o) * rows).astype(F32) + sub
            bias[i * rows : (i + 1) * rows, :] = jnp.where(pos >= begin, 0.0, NEG)
        own = (block * rows).astype(F32) + sub
        bias[3 * rows : 4 * rows, :] = jnp.where((own >= begin) & (sub <= lane), 0.0, NEG)
        cm[...] = jnp.where((mc[0:rows, :] == begin) & (sub <= lane), LIN_SCALE, 0.0)
        acc[...] = jnp.zeros(square, F32)
        soft[...] = jnp.zeros((8, HD), F32)
        stats[...] = jnp.zeros_like(stats)

    begin_c = mc[0:rows, :]
    carried = jnp.where(begin_c < (block * rows).astype(F32), LIN_SCALE, 0.0)
    begin0 = begin_c[0:1, :]
    coef = [jnp.where(begin0 < ((block - o + 1) * rows).astype(F32), 1.0, 0.0) for o in offs]
    for h in range(HEADS_STEP):
        c = cols(h)
        q = b_own[0:rows, c]
        grad = b_own[rows : 2 * rows, c]
        keys = jnp.concatenate([wr[0:rows, c], wa[0:rows, c], wx[0:rows, c], f_own[0:rows, c]], axis=0)
        vals = jnp.concatenate(
            [w[rows : 2 * rows, c] for w in (wr, wa, wx, f_own)], axis=0
        )
        s = nt(keys, q) * (SOFT_SCALE * LOG2E) + bias[...]
        gp = nt(vals, grad)
        top = jnp.max(s, axis=0, keepdims=True)
        e = jnp.exp2(s - top)
        total = jnp.sum(e, axis=0, keepdims=True)
        prob = e * (1.0 / total)
        delta = jnp.sum(prob * gp, axis=0, keepdims=True)
        ds = (prob * (gp - delta) * SOFT_SCALE).astype(BF16)
        sdq[:, c] = tn(ds, keys).astype(BF16)
        row = step * HEADS_STEP + h
        stats[pl.ds(row, 1), :] = top + jnp.log2(total)
        stats[pl.ds(16 + row, 1), :] = delta
        soft[0:1, :] += delta
        prior = (
            coef[0] * wr[2 * rows : 3 * rows, c].astype(F32)
            + coef[1] * wa[2 * rows : 3 * rows, c].astype(F32)
            + coef[2] * wx[2 * rows : 3 * rows, c].astype(F32)
        ).astype(BF16)
        back = (cm[...] * nt(lv[:, c], grad)).astype(BF16)
        dq = tn(back, lk[:, c]) + carried * nt(grad, prior)
        ldq[:, c] = dq.astype(BF16)
        acc[...] += dq * lq[:, c].astype(F32)

    @pl.when(step == pl.num_programs(0) - 1)
    def _():
        r = jnp.sum(acc[...].T, axis=0, keepdims=True) + soft[0:1, :]
        stats[32:40, :] = jnp.where(mr[2:3, :] == iota((NDOM, HD), 0), r, 0.0)


def lin_key_kernel(place, mr, mc, b_own, lq, lk, lv, wr, wa, wx, ldk, ldv, cm):
    rows = lq.shape[0]
    block = place[0]
    odd = block % 2
    offs = (2, jnp.where(odd == 1, 1, 3), jnp.where(odd == 1, 3, 1))
    square = (rows, HD)

    @pl.when(pl.program_id(0) == 0)
    def _():
        sub, lane = iota(square, 0), iota(square, 1)
        cm[...] = jnp.where((mc[0:rows, :] == mr[0:1, :]) & (sub <= lane), LIN_SCALE, 0.0)

    end_c = mc[rows : 2 * rows, :]
    extended = jnp.where(end_c > ((block + 1) * rows).astype(F32), LIN_SCALE, 0.0)
    last = end_c[rows - 1 : rows, :]
    coef = [jnp.where(last > ((block + o) * rows).astype(F32), 1.0, 0.0) for o in offs]
    for h in range(HEADS_STEP):
        c = cols(h)
        grad = b_own[rows : 2 * rows, c]
        later = (
            coef[0] * wr[2 * rows : 3 * rows, c].astype(F32)
            + coef[1] * wa[2 * rows : 3 * rows, c].astype(F32)
            + coef[2] * wx[2 * rows : 3 * rows, c].astype(F32)
        ).astype(BF16)
        k, v, q = lk[:, c], lv[:, c], lq[:, c]
        scores = (cm[...] * nt(k, q)).astype(BF16)
        back = (cm[...] * nt(v, grad)).astype(BF16)
        ldk[:, c] = (nn(back, q) + extended * nt(v, later)).astype(BF16)
        ldv[:, c] = (nn(scores, grad) + extended * nn(k, later)).astype(BF16)


def soft_key_kernel(place, mc, f_own, b_own, wr, wa, wx, s0, s1, s2, s3, sdk, sdv, bias):
    rows = f_own.shape[0] // 3
    step = pl.program_id(0)
    block = place[0]
    odd = block % 2
    offs = (2, jnp.where(odd == 1, 1, 3), jnp.where(odd == 1, 3, 1))
    square = (rows, HD)

    @pl.when(step == 0)
    def _():
        end_c = mc[rows : 2 * rows, :]
        sub, lane = iota(square, 0), iota(square, 1)
        for i, o in enumerate(offs):
            pos = ((block + o) * rows).astype(F32) + lane
            bias[:, cols(i)] = jnp.where(pos < end_c, 0.0, NEG)
        own = (block * rows).astype(F32) + lane
        bias[:, cols(3)] = jnp.where((own < end_c) & (sub <= lane), 0.0, NEG)

    def stat(row):
        near, far = s1[pl.ds(row, 1), :], s3[pl.ds(row, 1), :]
        parts = [
            s2[pl.ds(row, 1), :],
            jnp.where(odd == 1, near, far),
            jnp.where(odd == 1, far, near),
            s0[pl.ds(row, 1), :],
        ]
        return jnp.concatenate(parts, axis=1)

    for h in range(HEADS_STEP):
        c = cols(h)
        k, v = f_own[0:rows, c], f_own[rows : 2 * rows, c]
        queries = jnp.concatenate([w[0:rows, c] for w in (wr, wa, wx, b_own)], axis=0)
        grads = jnp.concatenate([w[rows : 2 * rows, c] for w in (wr, wa, wx, b_own)], axis=0)
        row = step * HEADS_STEP + h
        s = nt(k, queries) * (SOFT_SCALE * LOG2E) + bias[...]
        prob = jnp.exp2(s - stat(row))
        gp = nt(v, grads)
        ds = (prob * (gp - stat(16 + row)) * SOFT_SCALE).astype(BF16)
        sdk[:, c] = nn(ds, queries).astype(BF16)
        sdv[:, c] = nn(prob.astype(BF16), grads).astype(BF16)


def on_device(lin_query, lin_key, lin_value, soft_query, soft_key, soft_value, upstream, doc_lengths, doc_domain, domain_weight):
    rows, feats = lin_query.shape
    wide = HEADS_STEP * HD
    steps = feats // wide
    count = lax.axis_size("ctx")
    block = lax.axis_index("ctx")
    place = block.astype(jnp.int32).reshape(1)

    smem = pl.BlockSpec(memory_space=pltpu.SMEM)

    def tall(n):
        return pl.BlockSpec((n * rows, wide), lambda i: (0, i))

    def whole(n):
        return pl.BlockSpec((n, HD), lambda i: (0, 0))

    params = pltpu.CompilerParams(dimension_semantics=("arbitrary",), vmem_limit_bytes=VMEM)
    one = jax.ShapeDtypeStruct((rows, feats), BF16)
    three = jax.ShapeDtypeStruct((3 * rows, feats), BF16)
    unit = rows * feats * 2
    mm = 2 * rows * HD * feats

    def call(kernel, name, in_specs, out_specs, out_shape, scratch, flops, traffic, *args):
        return pl.pallas_call(
            kernel,
            name=name,
            grid=(steps,),
            in_specs=in_specs,
            out_specs=out_specs,
            out_shape=out_shape,
            scratch_shapes=scratch,
            compiler_params=params,
            cost_estimate=pl.CostEstimate(flops=flops, bytes_accessed=traffic, transcendentals=0),
        )(*args)

    fwd, bwd, mr, mc = call(
        pack_kernel, "pack", [smem] * 4 + [tall(1)] * 7,
        [tall(3), tall(3), whole(8), whole(3 * rows)],
        [three, three, jax.ShapeDtypeStruct((8, HD), F32), jax.ShapeDtypeStruct((3 * rows, HD), F32)],
        [], 2 * mm, 13 * unit,
        doc_lengths, doc_domain, domain_weight, place,
        lin_query, lin_key, lin_value, soft_query, soft_key, soft_value, upstream,
    )

    def shift(x, by):
        return lax.ppermute(x, "ctx", [(i, i + by) for i in range(count) if 0 <= i + by < count])

    def around(x, by):
        return lax.ppermute(x, "ctx", [(i, (i + by) % count) for i in range(count)])

    def swap(x):
        return lax.ppermute(x, "ctx", [(i, i ^ 1) for i in range(count)])

    odd = block % 2 == 1
    fr = shift(fwd, 2)
    br = shift(bwd, -2)
    fa = swap(fr)
    fx = shift(jnp.where(odd, fr, fwd), 1)
    ba = swap(br)
    bx = shift(jnp.where(odd, bwd, br), -1)

    soft_dq, lin_dq, stats = call(
        query_kernel, "queries", [smem, whole(8), whole(3 * rows), tall(3), tall(3)] + [tall(1)] * 3 + [tall(3)] * 3,
        [tall(1), tall(1), whole(40)],
        [one, one, jax.ShapeDtypeStruct((40, HD), F32)],
        [pltpu.VMEM((4 * rows, HD), F32), pltpu.VMEM((rows, HD), F32), pltpu.VMEM((rows, HD), F32), pltpu.VMEM((8, HD), F32)],
        16 * mm, 20 * unit,
        place, mr, mc, fwd, bwd, lin_query, lin_key, lin_value, fr, fa, fx,
    )
    s1, s2, s3 = (around(stats, -o) for o in (1, 2, 3))

    lin_dk, lin_dv = call(
        lin_key_kernel, "lin_keys", [smem, whole(8), whole(3 * rows), tall(3)] + [tall(1)] * 3 + [tall(3)] * 3,
        [tall(1), tall(1)], [one, one], [pltpu.VMEM((rows, HD), F32)],
        6 * mm, 17 * unit,
        place, mr, mc, bwd, lin_query, lin_key, lin_value, br, ba, bx,
    )
    soft_dk, soft_dv = call(
        soft_key_kernel, "soft_keys", [smem, whole(3 * rows), tall(3), tall(3)] + [tall(3)] * 3 + [whole(40)] * 4,
        [tall(1), tall(1)], [one, one], [pltpu.VMEM((rows, 4 * HD), F32)],
        16 * mm, 17 * unit,
        place, mc, fwd, bwd, br, ba, bx, stats, s1, s2, s3,
    )

    loss = stats[32:40] + s1[32:40] + s2[32:40] + s3[32:40]
    for stride in (4, 16):
        loss = loss + sum(around(loss, stride * k) for k in (1, 2, 3))
    heads = lax.axis_size("head")
    loss = loss + sum(
        lax.ppermute(loss, "head", [(i, (i + k) % heads) for i in range(heads)]) for k in range(1, heads)
    )
    domain_loss = jnp.sum(loss, axis=1)
    return (lin_dq, lin_dk, lin_dv, soft_dq, soft_dk, soft_dv, domain_loss)


def solution(mesh):
    spec = P("ctx", "head")
    return jax.shard_map(
        on_device,
        mesh=mesh,
        in_specs=(spec,) * 7 + (P(),) * 3,
        out_specs=(spec,) * 6 + (P(),),
        check_vma=False,
    )
```

time: 878 us -> 112 us (0.13)
  the two profiles are of different devices: /device:TPU:1 before, /device:TPU:10 now
where the time goes in v1:
time: 112 us; the launch traced here: 111 us
  waiting for transfers between devices  42.8 us (38%)
  starting transfers between devices  36.7 us (33%)
  Pallas kernels  20.3 us (18%)
  local copies, waits for them, and re-layouts  9.62 us (9%)
    ppermute x4, waiting for transfers between devices, shift(): lax.ppermute(x, 'ctx', [(i, i + by) for i in range(count) if 0 <= i + by...  35.7 us
    pallas_call x4, Pallas kernels, call(): pl.pallas_call(kernel, name=name, grid=(steps,), in_specs=in_specs, out_s...  20.3 us
    ppermute x4, starting transfers between devices, shift(): lax.ppermute(x, 'ctx', [(i, i + by) for i in range(count) if 0 <= i + by...  17.4 us
    ppermute x9, starting transfers between devices, around(): return lax.ppermute(x, 'ctx', [(i, (i + by) % count) for i in range(count)])  14.3 us
    unnamed x30, local copies, waits for them, and re-layouts  9.62 us
    ppermute x9, waiting for transfers between devices, around(): return lax.ppermute(x, 'ctx', [(i, (i + by) % count) for i in range(count)])  7.03 us
    ppermute x3, starting transfers between devices, on_device(): lax.ppermute(loss, 'head', [(i, (i + k) % heads) for i in range(heads)])  4.83 us
  transfers between devices with their start and end apart: 18, of which 6 were waited for; matrix products, arithmetic and copies ran while one was open for 0% of the time, Pallas kernels for 16%

profile of v1, /device:TPU:10, one launch (start us, length us, event | category | flops | bytes accessed | tf_op | source)
XLA Modules:
  0.0 111.2 jit_solution(4305573472877462097)
XLA Ops:
  0.6 0.0 copy-start
  0.7 1.0 copy-done
  1.6 1.0 copy-done.2
  2.6 1.0 copy-done.4
  3.6 1.0 copy-done.8
  4.6 1.0 copy-done.9
  5.6 1.0 copy-done.10
  6.6 1.0 copy-done.11
  7.6 0.7 copy-done.12
  8.3 0.7 copy-done.13
  8.9 0.7 copy-done.14
  9.6 2.3 %pack.1 = (bf16[384,1536]{1,0:T(8,128)(2,1)S(1)}, bf16[384,1536]{1,0:T(8,128)(2,1)S(1)}, f32[8,128]{1,0:T(8,128)S(1)}, f32[384,128]{1,0:T(8,128)S(1)}) custom-call(s32[42]{0:T(128)S(1)} %copy-done.12, s32[42]{0:T(128)S(1)} %copy-done.13, f32[8]{0:T(128)S(1)} %copy-done.14, s32[1]{0:T(128)} %bitcast.place, bf16[128,1536]{1,0:T(8,128)(2,1)S(1)} %copy-done, ...), custom_call_target="tpu_custom_call" | custom-call | flops 100663296 | bytes 5111808 | tf_op jit(solution)/shard_map/pack/pallas_call | solution.py:250
  11.9 0.0 copy-start.6
  11.9 0.7 copy-done.6
  12.6 3.8 %collective-permute-start = (bf16[384,1536]{1,0:T(8,128)(2,1)S(1)}, bf16[384,1536]{1,0:T(8,128)(2,1)}, u32[]{:S(2)}, u32[]{:S(2)}) collective-permute-start(bf16[384,1536]{1,0:T(8,128)(2,1)S(1)} %get-tuple-element.20.f_own), channel_id=1, source_target_pairs={{0,8},{4,12},{8,16},{12,20},{16,24},{20,28},{24,32},{28,36},{32,40... | collective-permute-start | bytes 3538952 | tf_op jit(solution)/shard_map/ppermute | solution.py:272
  16.4 5.7 %collective-permute-start.3 = (bf16[384,1536]{1,0:T(8,128)(2,1)S(1)}, bf16[384,1536]{1,0:T(8,128)(2,1)S(1)}, u32[]{:S(2)}, u32[]{:S(2)}) collective-permute-start(bf16[384,1536]{1,0:T(8,128)(2,1)S(1)} %get-tuple-element.21.b_own), channel_id=1, source_target_pairs={{8,0},{12,4},{16,8},{20,12},{24,16},{28,20},{32,24},{36,28},{40,32... | collective-permute-start | bytes 3538952 | tf_op jit(solution)/shard_map/ppermute | solution.py:272
  22.2 24.1 %collective-permute-done.wr = bf16[384,1536]{1,0:T(8,128)(2,1)} collective-permute-done((bf16[384,1536]{1,0:T(8,128)(2,1)S(1)}, bf16[384,1536]{1,0:T(8,128)(2,1)}, u32[]{:S(2)}, u32[]{:S(2)}) %collective-permute-start) | collective-permute-done | bytes 1179680 | tf_op jit(solution)/shard_map/ppermute | solution.py:272
  46.3 0.1 broadcast_select_fusion.1
  46.4 0.0 copy-start.1
  46.4 0.0 copy-start.3
  46.4 0.0 copy-start.5
  46.4 0.0 copy-start.7
  46.5 2.6 %collective-permute-start.2 = (bf16[384,1536]{1,0:T(8,128)(2,1)S(1)}, bf16[384,1536]{1,0:T(8,128)(2,1)S(1)}, u32[]{:S(2)}, u32[]{:S(2)}) collective-permute-start(bf16[384,1536]{1,0:T(8,128)(2,1)S(1)} %broadcast_select_fusion.1), channel_id=1, source_target_pairs={{0,4},{4,8},{8,12},{12,16},{16,20},{20,24},{24,28},{28,32},{32,36}... | collective-permute-start | bytes 3538952 | tf_op jit(solution)/shard_map/ppermute | solution.py:272
  49.1 0.1 collective-permute-start.1
  49.2 0.1 broadcast_select_fusion
  49.3 5.2 %collective-permute-start.5 = (bf16[384,1536]{1,0:T(8,128)(2,1)S(1)}, bf16[384,1536]{1,0:T(8,128)(2,1)S(1)}, u32[]{:S(2)}, u32[]{:S(2)}) collective-permute-start(bf16[384,1536]{1,0:T(8,128)(2,1)S(1)} %broadcast_select_fusion), channel_id=1, source_target_pairs={{4,0},{8,4},{12,8},{16,12},{20,16},{24,20},{28,24},{32,28},{36,32}... | collective-permute-start | bytes 3538952 | tf_op jit(solution)/shard_map/ppermute | solution.py:272
  54.5 0.1 collective-permute-start.4
  54.6 11.6 %collective-permute-done.2.wx = bf16[384,1536]{1,0:T(8,128)(2,1)S(1)} collective-permute-done((bf16[384,1536]{1,0:T(8,128)(2,1)S(1)}, bf16[384,1536]{1,0:T(8,128)(2,1)S(1)}, u32[]{:S(2)}, u32[]{:S(2)}) %collective-permute-start.2) | collective-permute-done | bytes 1179680 | tf_op jit(solution)/shard_map/ppermute | solution.py:272
  66.2 0.0 collective-permute-done.1.wa
  66.3 9.6 %queries.1 = (bf16[128,1536]{1,0:T(8,128)(2,1)}, bf16[128,1536]{1,0:T(8,128)(2,1)}, f32[40,128]{1,0:T(8,128)S(1)}) custom-call(s32[1]{0:T(128)} %bitcast.place, f32[8,128]{1,0:T(8,128)S(1)} %get-tuple-element.18.mr, f32[384,128]{1,0:T(8,128)S(1)} %copy-done.7, bf16[384,1536]{1,0:T(8,128)(2,1)S(1)} %get-tuple-element.20.f_own, ...), custom_call_target="tpu_custom_call" | custom-call | flops 805306368 | bytes 7864320 | tf_op jit(solution)/shard_map/queries/pallas_call | solution.py:250
  75.8 0.0 collective-permute-start.8
  75.8 1.4 %collective-permute-start.6 = (f32[40,128]{1,0:T(8,128)S(1)}, f32[40,128]{1,0:T(8,128)S(1)}, u32[]{:S(2)}, u32[]{:S(2)}) collective-permute-start(f32[40,128]{1,0:T(8,128)S(1)} %get-tuple-element.26.s0), channel_id=1, source_target_pairs={{0,252},{4,0},{8,4},{12,8},{16,12},{20,16},{24,20},{28,24},{32,28}... | collective-permute-start | bytes 61448 | tf_op jit(solution)/shard_map/ppermute | solution.py:275
  77.2 1.8 %collective-permute-done.8.s3 = f32[40,128]{1,0:T(8,128)S(1)} collective-permute-done((f32[40,128]{1,0:T(8,128)S(1)}, f32[40,128]{1,0:T(8,128)S(1)}, u32[]{:S(2)}, u32[]{:S(2)}) %collective-permute-start.8) | collective-permute-done | bytes 20512 | tf_op jit(solution)/shard_map/ppermute | solution.py:275
  79.0 0.6 collective-permute-done.7.s2
  79.7 2.0 %collective-permute-start.11 = (f32[8,128]{1,0:T(8,128)S(1)}, f32[8,128]{1,0:T(8,128)S(1)}, u32[]{:S(2)}, u32[]{:S(2)}) collective-permute-start(f32[8,128]{1,0:T(8,128)S(1)} %slice_add_fusion), channel_id=1, source_target_pairs={{0,48},{4,52},{8,56},{12,60},{16,64},{20,68},{24,72},{28,76},{32,8... | collective-permute-start | bytes 12296 | tf_op jit(solution)/shard_map/ppermute | solution.py:275
  81.7 3.5 %collective-permute-start.10 = (f32[8,128]{1,0:T(8,128)S(1)}, f32[8,128]{1,0:T(8,128)S(1)}, u32[]{:S(2)}, u32[]{:S(2)}) collective-permute-start(f32[8,128]{1,0:T(8,128)S(1)} %slice_add_fusion), channel_id=1, source_target_pairs={{0,32},{4,36},{8,40},{12,44},{16,48},{20,52},{24,56},{28,60},{32,6... | collective-permute-start | bytes 12296 | tf_op jit(solution)/shard_map/ppermute | solution.py:275
  85.2 2.0 %collective-permute-start.9 = (f32[8,128]{1,0:T(8,128)S(1)}, f32[8,128]{1,0:T(8,128)S(1)}, u32[]{:S(2)}, u32[]{:S(2)}) collective-permute-start(f32[8,128]{1,0:T(8,128)S(1)} %slice_add_fusion), channel_id=1, source_target_pairs={{0,16},{4,20},{8,24},{12,28},{16,32},{20,36},{24,40},{28,44},{32,4... | collective-permute-start | bytes 12296 | tf_op jit(solution)/shard_map/ppermute | solution.py:275
  87.2 2.9 %collective-permute-done.10 = f32[8,128]{1,0:T(8,128)S(1)} collective-permute-done((f32[8,128]{1,0:T(8,128)S(1)}, f32[8,128]{1,0:T(8,128)S(1)}, u32[]{:S(2)}, u32[]{:S(2)}) %collective-permute-start.10) | collective-permute-done | bytes 4128 | tf_op jit(solution)/shard_map/ppermute | solution.py:275
  90.1 1.7 %collective-permute-done.9 = f32[8,128]{1,0:T(8,128)S(1)} collective-permute-done((f32[8,128]{1,0:T(8,128)S(1)}, f32[8,128]{1,0:T(8,128)S(1)}, u32[]{:S(2)}, u32[]{:S(2)}) %collective-permute-start.9) | collective-permute-done | bytes 4128 | tf_op jit(solution)/shard_map/ppermute | solution.py:275
  91.8 1.7 %collective-permute-start.14 = (f32[8,128]{1,0:T(8,128)S(1)}, f32[8,128]{1,0:T(8,128)S(1)}, u32[]{:S(2)}, u32[]{:S(2)}) collective-permute-start(f32[8,128]{1,0:T(8,128)S(1)} %add_add_fusion.1), channel_id=1, source_target_pairs={{0,192},{4,196},{8,200},{12,204},{16,208},{20,212},{24,216},{28,22... | collective-permute-start | bytes 12296 | tf_op jit(solution)/shard_map/ppermute | solution.py:275
  93.4 1.4 %collective-permute-start.13 = (f32[8,128]{1,0:T(8,128)S(1)}, f32[8,128]{1,0:T(8,128)S(1)}, u32[]{:S(2)}, u32[]{:S(2)}) collective-permute-start(f32[8,128]{1,0:T(8,128)S(1)} %add_add_fusion.1), channel_id=1, source_target_pairs={{0,128},{4,132},{8,136},{12,140},{16,144},{20,148},{24,152},{28,15... | collective-permute-start | bytes 12296 | tf_op jit(solution)/shard_map/ppermute | solution.py:275
  94.8 2.4 %collective-permute-start.12 = (f32[8,128]{1,0:T(8,128)S(1)}, f32[8,128]{1,0:T(8,128)S(1)}, u32[]{:S(2)}, u32[]{:S(2)}) collective-permute-start(f32[8,128]{1,0:T(8,128)S(1)} %add_add_fusion.1), channel_id=1, source_target_pairs={{0,64},{4,68},{8,72},{12,76},{16,80},{20,84},{24,88},{28,92},{32,9... | collective-permute-start | bytes 12296 | tf_op jit(solution)/shard_map/ppermute | solution.py:275
  97.2 3.7 %lin_keys.1 = (bf16[128,1536]{1,0:T(8,128)(2,1)}, bf16[128,1536]{1,0:T(8,128)(2,1)}) custom-call(s32[1]{0:T(128)} %bitcast.place, f32[8,128]{1,0:T(8,128)S(1)} %get-tuple-element.18.mr, f32[384,128]{1,0:T(8,128)S(1)} %copy-done.7, bf16[384,1536]{1,0:T(8,128)(2,1)S(1)} %get-tuple-element.21.b_own, bf16[128,1536]{1,0:T(8,128)(2,1)S(1)} %copy-done.1, ...), custom_call_target="tpu_custom_call" | custom-call | flops 301989888 | bytes 6684672 | tf_op jit(solution)/shard_map/lin_keys/pallas_call | solution.py:250
  101.0 0.6 collective-permute-start.17
  101.6 2.4 %collective-permute-start.16 = (f32[8,128]{1,0:T(8,128)S(1)}, f32[8,128]{1,0:T(8,128)S(1)}, u32[]{:S(2)}, u32[]{:S(2)}) collective-permute-start(f32[8,128]{1,0:T(8,128)S(1)} %add_add_fusion), channel_id=1, source_target_pairs={{0,2},{1,3},{2,0},{3,1},{4,6},{5,7},{6,4},{7,5},{8,10},{9,11},{10,... | collective-permute-start | bytes 12296 | tf_op jit(solution)/shard_map/ppermute | solution.py:316
  104.0 1.8 %collective-permute-start.15 = (f32[8,128]{1,0:T(8,128)S(1)}, f32[8,128]{1,0:T(8,128)S(1)}, u32[]{:S(2)}, u32[]{:S(2)}) collective-permute-start(f32[8,128]{1,0:T(8,128)S(1)} %add_add_fusion), channel_id=1, source_target_pairs={{0,1},{1,2},{2,3},{3,0},{4,5},{5,6},{6,7},{7,4},{8,9},{9,10},{10,1... | collective-permute-start | bytes 12296 | tf_op jit(solution)/shard_map/ppermute | solution.py:316
  105.8 4.7 %soft_keys.1 = (bf16[128,1536]{1,0:T(8,128)(2,1)}, bf16[128,1536]{1,0:T(8,128)(2,1)}) custom-call(s32[1]{0:T(128)} %bitcast.place, f32[384,128]{1,0:T(8,128)S(1)} %copy-done.7, bf16[384,1536]{1,0:T(8,128)(2,1)S(1)} %get-tuple-element.20.f_own, bf16[384,1536]{1,0:T(8,128)(2,1)S(1)} %get-tuple-element.21.b_own, ...), custom_call_target="tpu_custom_call" | custom-call | flops 805306368 | bytes 6684672 | tf_op jit(solution)/shard_map/soft_keys/pallas_call | solution.py:250
  110.6 0.6 add_reduce_fusion
  (28 shorter events, 0.1 us)
Async XLA Ops:
  0.6 1.0 copy-start
  1.6 1.0 copy-start.2
  2.6 1.0 copy-start.4
  3.6 1.0 copy-start.8
  4.6 1.0 copy-start.9
  5.6 1.0 copy-start.10
  6.6 1.0 copy-start.11
  7.6 0.7 copy-start.12
  8.3 0.7 copy-start.13
  8.9 0.7 copy-start.14
  11.9 0.7 copy-start.6
  12.6 33.7 %collective-permute-start = (bf16[384,1536]{1,0:T(8,128)(2,1)S(1)}, bf16[384,1536]{1,0:T(8,128)(2,1)}, u32[]{:S(2)}, u32[]{:S(2)}) collective-permute-start(bf16[384,1536]{1,0:T(8,128)(2,1)S(1)} %get-tuple-element.20.f_own), channel_id=1, source_target_pairs={{0,8},{4,12},{8,16},{12,20},{16,24},{20,28},{24,32},{28,36},{32,40... | collective-permute-start | bytes 3538952 | tf_op jit(solution)/shard_map/ppermute | solution.py:272
  16.4 32.8 %collective-permute-start.3 = (bf16[384,1536]{1,0:T(8,128)(2,1)S(1)}, bf16[384,1536]{1,0:T(8,128)(2,1)S(1)}, u32[]{:S(2)}, u32[]{:S(2)}) collective-permute-start(bf16[384,1536]{1,0:T(8,128)(2,1)S(1)} %get-tuple-element.21.b_own), channel_id=1, source_target_pairs={{8,0},{12,4},{16,8},{20,12},{24,16},{28,20},{32,24},{36,28},{40,32... | collective-permute-start | bytes 3538952 | tf_op jit(solution)/shard_map/ppermute | solution.py:272
  46.4 19.8 %copy-start.1 = (bf16[128,1536]{1,0:T(8,128)(2,1)S(1)}, bf16[128,1536]{1,0:T(8,128)(2,1)}, u32[]{:S(2)}) copy-start(bf16[128,1536]{1,0:T(8,128)(2,1)} %lq.5) | copy-start | bytes 1179652
  46.4 19.8 %copy-start.3 = (bf16[128,1536]{1,0:T(8,128)(2,1)S(1)}, bf16[128,1536]{1,0:T(8,128)(2,1)}, u32[]{:S(2)}) copy-start(bf16[128,1536]{1,0:T(8,128)(2,1)} %lk.5) | copy-start | bytes 1179652
  46.4 19.8 %copy-start.5 = (bf16[128,1536]{1,0:T(8,128)(2,1)S(1)}, bf16[128,1536]{1,0:T(8,128)(2,1)}, u32[]{:S(2)}) copy-start(bf16[128,1536]{1,0:T(8,128)(2,1)} %lv.5) | copy-start | bytes 1179652
  46.4 19.8 %copy-start.7 = (f32[384,128]{1,0:T(8,128)S(1)}, f32[384,128]{1,0:T(8,128)}, u32[]{:S(2)}) copy-start(f32[384,128]{1,0:T(8,128)} %copy-done.6) | copy-start | bytes 589828
  46.5 19.8 %collective-permute-start.2 = (bf16[384,1536]{1,0:T(8,128)(2,1)S(1)}, bf16[384,1536]{1,0:T(8,128)(2,1)S(1)}, u32[]{:S(2)}, u32[]{:S(2)}) collective-permute-start(bf16[384,1536]{1,0:T(8,128)(2,1)S(1)} %broadcast_select_fusion.1), channel_id=1, source_target_pairs={{0,4},{4,8},{8,12},{12,16},{16,20},{20,24},{24,28},{28,32},{32,36}... | collective-permute-start | bytes 3538952 | tf_op jit(solution)/shard_map/ppermute | solution.py:272
  49.1 17.2 %collective-permute-start.1 = (bf16[384,1536]{1,0:T(8,128)(2,1)}, bf16[384,1536]{1,0:T(8,128)(2,1)S(1)}, u32[]{:S(2)}, u32[]{:S(2)}) collective-permute-start(bf16[384,1536]{1,0:T(8,128)(2,1)} %collective-permute-done.wr), channel_id=1, source_target_pairs={{0,4},{4,0},{8,12},{12,8},{16,20},{20,16},{24,28},{28,24},{32,36},... | collective-permute-start | bytes 3538952 | tf_op jit(solution)/shard_map/ppermute | solution.py:278
  49.3 47.9 %collective-permute-start.5 = (bf16[384,1536]{1,0:T(8,128)(2,1)S(1)}, bf16[384,1536]{1,0:T(8,128)(2,1)S(1)}, u32[]{:S(2)}, u32[]{:S(2)}) collective-permute-start(bf16[384,1536]{1,0:T(8,128)(2,1)S(1)} %broadcast_select_fusion), channel_id=1, source_target_pairs={{4,0},{8,4},{12,8},{16,12},{20,16},{24,20},{28,24},{32,28},{36,32}... | collective-permute-start | bytes 3538952 | tf_op jit(solution)/shard_map/ppermute | solution.py:272
  54.5 42.7 %collective-permute-start.4 = (bf16[384,1536]{1,0:T(8,128)(2,1)S(1)}, bf16[384,1536]{1,0:T(8,128)(2,1)S(1)}, u32[]{:S(2)}, u32[]{:S(2)}) collective-permute-start(bf16[384,1536]{1,0:T(8,128)(2,1)S(1)} %collective-permute-done.3.wr), channel_id=1, source_target_pairs={{0,4},{4,0},{8,12},{12,8},{16,20},{20,16},{24,28},{28,24},{32,36},... | collective-permute-start | bytes 3538952 | tf_op jit(solution)/shard_map/ppermute | solution.py:278
  75.8 3.2 %collective-permute-start.8 = (f32[40,128]{1,0:T(8,128)S(1)}, f32[40,128]{1,0:T(8,128)S(1)}, u32[]{:S(2)}, u32[]{:S(2)}) collective-permute-start(f32[40,128]{1,0:T(8,128)S(1)} %get-tuple-element.26.s0), channel_id=1, source_target_pairs={{0,244},{4,248},{8,252},{12,0},{16,4},{20,8},{24,12},{28,16},{32,2... | collective-permute-start | bytes 61448 | tf_op jit(solution)/shard_map/ppermute | solution.py:275
  75.8 3.8 %collective-permute-start.7 = (f32[40,128]{1,0:T(8,128)S(1)}, f32[40,128]{1,0:T(8,128)S(1)}, u32[]{:S(2)}, u32[]{:S(2)}) collective-permute-start(f32[40,128]{1,0:T(8,128)S(1)} %get-tuple-element.26.s0), channel_id=1, source_target_pairs={{0,248},{4,252},{8,0},{12,4},{16,8},{20,12},{24,16},{28,20},{32,24... | collective-permute-start | bytes 61448 | tf_op jit(solution)/shard_map/ppermute | solution.py:275
  75.8 3.8 %collective-permute-start.6 = (f32[40,128]{1,0:T(8,128)S(1)}, f32[40,128]{1,0:T(8,128)S(1)}, u32[]{:S(2)}, u32[]{:S(2)}) collective-permute-start(f32[40,128]{1,0:T(8,128)S(1)} %get-tuple-element.26.s0), channel_id=1, source_target_pairs={{0,252},{4,0},{8,4},{12,8},{16,12},{20,16},{24,20},{28,24},{32,28}... | collective-permute-start | bytes 61448 | tf_op jit(solution)/shard_map/ppermute | solution.py:275
  79.7 7.5 %collective-permute-start.11 = (f32[8,128]{1,0:T(8,128)S(1)}, f32[8,128]{1,0:T(8,128)S(1)}, u32[]{:S(2)}, u32[]{:S(2)}) collective-permute-start(f32[8,128]{1,0:T(8,128)S(1)} %slice_add_fusion), channel_id=1, source_target_pairs={{0,48},{4,52},{8,56},{12,60},{16,64},{20,68},{24,72},{28,76},{32,8... | collective-permute-start | bytes 12296 | tf_op jit(solution)/shard_map/ppermute | solution.py:275
  81.7 8.4 %collective-permute-start.10 = (f32[8,128]{1,0:T(8,128)S(1)}, f32[8,128]{1,0:T(8,128)S(1)}, u32[]{:S(2)}, u32[]{:S(2)}) collective-permute-start(f32[8,128]{1,0:T(8,128)S(1)} %slice_add_fusion), channel_id=1, source_target_pairs={{0,32},{4,36},{8,40},{12,44},{16,48},{20,52},{24,56},{28,60},{32,6... | collective-permute-start | bytes 12296 | tf_op jit(solution)/shard_map/ppermute | solution.py:275
  85.2 6.6 %collective-permute-start.9 = (f32[8,128]{1,0:T(8,128)S(1)}, f32[8,128]{1,0:T(8,128)S(1)}, u32[]{:S(2)}, u32[]{:S(2)}) collective-permute-start(f32[8,128]{1,0:T(8,128)S(1)} %slice_add_fusion), channel_id=1, source_target_pairs={{0,16},{4,20},{8,24},{12,28},{16,32},{20,36},{24,40},{28,44},{32,4... | collective-permute-start | bytes 12296 | tf_op jit(solution)/shard_map/ppermute | solution.py:275
  91.8 9.2 %collective-permute-start.14 = (f32[8,128]{1,0:T(8,128)S(1)}, f32[8,128]{1,0:T(8,128)S(1)}, u32[]{:S(2)}, u32[]{:S(2)}) collective-permute-start(f32[8,128]{1,0:T(8,128)S(1)} %add_add_fusion.1), channel_id=1, source_target_pairs={{0,192},{4,196},{8,200},{12,204},{16,208},{20,212},{24,216},{28,22... | collective-permute-start | bytes 12296 | tf_op jit(solution)/shard_map/ppermute | solution.py:275
  93.4 7.5 %collective-permute-start.13 = (f32[8,128]{1,0:T(8,128)S(1)}, f32[8,128]{1,0:T(8,128)S(1)}, u32[]{:S(2)}, u32[]{:S(2)}) collective-permute-start(f32[8,128]{1,0:T(8,128)S(1)} %add_add_fusion.1), channel_id=1, source_target_pairs={{0,128},{4,132},{8,136},{12,140},{16,144},{20,148},{24,152},{28,15... | collective-permute-start | bytes 12296 | tf_op jit(solution)/shard_map/ppermute | solution.py:275
  94.8 6.1 %collective-permute-start.12 = (f32[8,128]{1,0:T(8,128)S(1)}, f32[8,128]{1,0:T(8,128)S(1)}, u32[]{:S(2)}, u32[]{:S(2)}) collective-permute-start(f32[8,128]{1,0:T(8,128)S(1)} %add_add_fusion.1), channel_id=1, source_target_pairs={{0,64},{4,68},{8,72},{12,76},{16,80},{20,84},{24,88},{28,92},{32,9... | collective-permute-start | bytes 12296 | tf_op jit(solution)/shard_map/ppermute | solution.py:275
  101.0 9.6 %collective-permute-start.17 = (f32[8,128]{1,0:T(8,128)S(1)}, f32[8,128]{1,0:T(8,128)S(1)}, u32[]{:S(2)}, u32[]{:S(2)}) collective-permute-start(f32[8,128]{1,0:T(8,128)S(1)} %add_add_fusion), channel_id=1, source_target_pairs={{0,3},{1,0},{2,1},{3,2},{4,7},{5,4},{6,5},{7,6},{8,11},{9,8},{10,9... | collective-permute-start | bytes 12296 | tf_op jit(solution)/shard_map/ppermute | solution.py:316
  101.6 9.0 %collective-permute-start.16 = (f32[8,128]{1,0:T(8,128)S(1)}, f32[8,128]{1,0:T(8,128)S(1)}, u32[]{:S(2)}, u32[]{:S(2)}) collective-permute-start(f32[8,128]{1,0:T(8,128)S(1)} %add_add_fusion), channel_id=1, source_target_pairs={{0,2},{1,3},{2,0},{3,1},{4,6},{5,7},{6,4},{7,5},{8,10},{9,11},{10,... | collective-permute-start | bytes 12296 | tf_op jit(solution)/shard_map/ppermute | solution.py:316
  104.0 6.5 %collective-permute-start.15 = (f32[8,128]{1,0:T(8,128)S(1)}, f32[8,128]{1,0:T(8,128)S(1)}, u32[]{:S(2)}, u32[]{:S(2)}) collective-permute-start(f32[8,128]{1,0:T(8,128)S(1)} %add_add_fusion), channel_id=1, source_target_pairs={{0,1},{1,2},{2,3},{3,0},{4,5},{5,6},{6,7},{7,4},{8,9},{9,10},{10,1... | collective-permute-start | bytes 12296 | tf_op jit(solution)/shard_map/ppermute | solution.py:316

commit v2 on v1

v2 whole, which is shorter than its diff:
```python
import functools

import jax
import jax.numpy as jnp
from jax import lax
from jax.experimental import pallas as pl
from jax.experimental.pallas import tpu as pltpu
from jax.sharding import PartitionSpec as P

HD = 128
DOC_MOST = 384
NDOM = 8
LIN_SCALE = (HD * DOC_MOST) ** (-0.5)
SOFT_SCALE = HD ** (-0.5)
LOG2E = 1.4426950408889634
NEG = -1e30
HEADS_STEP = 4
PARTS = 1
RIDE = 4
QUERY_STEP = 4
VMEM = 16 * 1024 * 1024
PACK_VMEM = 60 * 1024 * 1024

F32 = jnp.float32
BF16 = jnp.bfloat16


def nn(a, b):
    return lax.dot_general(a, b, (((1,), (0,)), ((), ())), preferred_element_type=F32)


def nt(a, b):
    return lax.dot_general(a, b, (((1,), (1,)), ((), ())), preferred_element_type=F32)


def tn(a, b):
    return lax.dot_general(a, b, (((0,), (0,)), ((), ())), preferred_element_type=F32)


def iota(shape, dim):
    return lax.broadcasted_iota(jnp.int32, shape, dim).astype(F32)


def cols(h):
    return slice(h * HD, (h + 1) * HD)


def rows_kernel(lens, doms, wts, place, mr, mc):
    rows = mc.shape[0] // 4
    pos = place[0] * rows + lax.broadcasted_iota(jnp.int32, (1, HD), 1)
    begin = end = dom = wt = jnp.zeros((1, HD), F32)
    start = jnp.int32(0)
    for i in range(lens.shape[0]):
        stop = start + lens[i]
        inside = (pos >= start) & (pos < stop)
        begin = jnp.where(inside, start.astype(F32), begin)
        end = jnp.where(inside, stop.astype(F32), end)
        dom = jnp.where(inside, doms[i].astype(F32), dom)
        wt = jnp.where(inside, wts[doms[i]], wt)
        start = stop
    mr[0:1, :] = begin
    mr[1:2, :] = dom
    mr[2:8, :] = jnp.zeros((6, HD), F32)
    for i, row in enumerate((begin, end, dom, wt)):
        mc[i * rows : (i + 1) * rows, :] = jnp.broadcast_to(row, (rows, HD)).T


def pack_kernel(lens, doms, wts, place, lk, lv, sk, sv, lq, sq, up, f_out, b_out, mr, mc):
    rows = lk.shape[0]

    @pl.when(pl.program_id(0) == 0)
    def _():
        rows_kernel(lens, doms, wts, place, mr, mc)

    begin_c = mc[0:rows, :]
    weight = mc[3 * rows : 4 * rows, :]
    in_last = (begin_c == begin_c[rows - 1 : rows, :]).astype(BF16)
    in_first = (begin_c == begin_c[0:1, :]).astype(BF16)
    f_out[0:rows, :] = sk[...]
    f_out[rows : 2 * rows, :] = sv[...]
    b_out[0:rows, :] = sq[...]
    for h in range(QUERY_STEP):
        c = cols(h)
        f_out[2 * rows : 3 * rows, c] = tn(lk[:, c] * in_last, lv[:, c]).astype(BF16)
        grad = (weight * up[:, c].astype(F32)).astype(BF16)
        b_out[rows : 2 * rows, c] = grad
        b_out[2 * rows : 3 * rows, c] = tn(lq[:, c] * in_first, grad).astype(BF16)


def query_kernel(part, place, mr, mc, f_own, b_own, lq, lk, lv, wr, wa, wx, *rest):
    if part > 0:
        sdq_in, ldq_in, stats_in, acc_in, *rest = rest
    sdq, ldq, stats, acc_out, *rest = rest
    bias, cm, acc = rest[-3:]
    rows = lq.shape[0]
    step = pl.program_id(0)
    base = part * QUERY_STEP * pl.num_programs(0)
    block = place[0]
    offs = offsets(block % 2, True)
    square = (rows, HD)

    @pl.when(step == 0)
    def _():
        begin = mr[0:1, :]
        sub, lane = iota(square, 0), iota(square, 1)
        for i, o in enumerate(offs):
            pos = ((block - o) * rows).astype(F32) + sub
            bias[i * rows : (i + 1) * rows, :] = jnp.where(pos >= begin, 0.0, NEG)
        own = (block * rows).astype(F32) + sub
        bias[3 * rows : 4 * rows, :] = jnp.where((own >= begin) & (sub <= lane), 0.0, NEG)
        cm[...] = jnp.where((mc[0:rows, :] == begin) & (sub <= lane), LIN_SCALE, 0.0)
        if part > 0:
            acc[...] = acc_in[...]
            stats[...] = stats_in[...]
        else:
            acc[...] = jnp.zeros(square, F32)
            stats[...] = jnp.zeros_like(stats)

    begin_c = mc[0:rows, :]
    carried = jnp.where(begin_c < (block * rows).astype(F32), LIN_SCALE, 0.0)
    begin0 = begin_c[0:1, :]
    coef = [jnp.where(begin0 < ((block - o + 1) * rows).astype(F32), 1.0, 0.0) for o in offs]
    terms, deltas = [], []
    for h in range(QUERY_STEP):
        c = cols(h)
        q = b_own[0:rows, c]
        grad = b_own[rows : 2 * rows, c]
        keys = jnp.concatenate([w[0:rows, c] for w in (wr, wa, wx, f_own)], axis=0)
        vals = jnp.concatenate([w[rows : 2 * rows, c] for w in (wr, wa, wx, f_own)], axis=0)
        s = nt(keys, q) * (SOFT_SCALE * LOG2E) + bias[...]
        gp = nt(vals, grad)
        top = jnp.max(s, axis=0, keepdims=True)
        e = jnp.exp2(s - top)
        total = jnp.sum(e, axis=0, keepdims=True)
        prob = e * (1.0 / total)
        delta = jnp.sum(prob * gp, axis=0, keepdims=True)
        ds = (prob * (gp - delta) * SOFT_SCALE).astype(BF16)
        sdq[:, c] = tn(ds, keys).astype(BF16)
        row = base + step * QUERY_STEP + h
        stats[pl.ds(row, 1), :] = top + jnp.log2(total)
        stats[pl.ds(16 + row, 1), :] = delta
        deltas.append(delta)
        prior = sum(f * w[2 * rows : 3 * rows, c].astype(F32) for f, w in zip(coef, (wr, wa, wx))).astype(BF16)
        back = (cm[...] * nt(lv[:, c], grad)).astype(BF16)
        dq = tn(back, lk[:, c]) + carried * nt(grad, prior)
        ldq[:, c] = dq.astype(BF16)
        terms.append(dq * lq[:, c].astype(F32))
    diagonal = iota(square, 0) == iota(square, 1)
    acc[...] += sum(terms) + jnp.where(diagonal, sum(deltas), 0.0)

    @pl.when(step == pl.num_programs(0) - 1)
    def _():
        acc_out[...] = acc[...]
        if part == PARTS - 1:
            tokens = jnp.sum(acc[...], axis=1, keepdims=True)
            mine = jnp.where(mc[2 * rows : 3 * rows, :] == iota(square, 1), tokens, 0.0)
            vec = jnp.sum(mine, axis=0, keepdims=True)
            stats[32:40, :] = jnp.broadcast_to(vec, (8, HD))


def offsets(odd, forward):
    near, far = (3, 1) if forward else (1, 3)
    return 2, jnp.where(odd == 1, near, far), jnp.where(odd == 1, far, near)


def lin_key_kernel(place, mr, mc, b_own, lq, lk, lv, wr, wa, wx, ldk, ldv, cm):
    rows = lq.shape[0]
    block = place[0]
    odd = block % 2
    offs = offsets(odd, False)
    square = (rows, HD)

    @pl.when(pl.program_id(0) == 0)
    def _():
        sub, lane = iota(square, 0), iota(square, 1)
        cm[...] = jnp.where((mc[0:rows, :] == mr[0:1, :]) & (sub <= lane), LIN_SCALE, 0.0)

    end_c = mc[rows : 2 * rows, :]
    extended = jnp.where(end_c > ((block + 1) * rows).astype(F32), LIN_SCALE, 0.0)
    last = end_c[rows - 1 : rows, :]
    coef = [jnp.where(last > ((block + o) * rows).astype(F32), 1.0, 0.0) for o in offs]
    for h in range(HEADS_STEP):
        c = cols(h)
        grad = b_own[rows : 2 * rows, c]
        later = (
            coef[0] * wr[2 * rows : 3 * rows, c].astype(F32)
            + coef[1] * wa[2 * rows : 3 * rows, c].astype(F32)
            + coef[2] * wx[2 * rows : 3 * rows, c].astype(F32)
        ).astype(BF16)
        k, v, q = lk[:, c], lv[:, c], lq[:, c]
        scores = (cm[...] * nt(k, q)).astype(BF16)
        back = (cm[...] * nt(v, grad)).astype(BF16)
        ldk[:, c] = (nn(back, q) + extended * nt(v, later)).astype(BF16)
        ldv[:, c] = (nn(scores, grad) + extended * nn(k, later)).astype(BF16)


def soft_key_kernel(place, mc, k0, v0, b_own, wr, wa, wx, s0, s1, s2, s3, sdk, sdv, bias):
    rows = k0.shape[0]
    step = pl.program_id(0)
    block = place[0]
    odd = block % 2
    offs = offsets(odd, False)
    square = (rows, HD)

    @pl.when(step == 0)
    def _():
        end_c = mc[rows : 2 * rows, :]
        sub, lane = iota(square, 0), iota(square, 1)
        for i, o in enumerate(offs):
            pos = ((block + o) * rows).astype(F32) + lane
            bias[:, cols(i)] = jnp.where(pos < end_c, 0.0, NEG)
        own = (block * rows).astype(F32) + lane
        bias[:, cols(3)] = jnp.where((own < end_c) & (sub <= lane), 0.0, NEG)

    def stat(row):
        near, far = s1[pl.ds(row, 1), :], s3[pl.ds(row, 1), :]
        parts = [
            s2[pl.ds(row, 1), :],
            jnp.where(odd == 1, near, far),
            jnp.where(odd == 1, far, near),
            s0[pl.ds(row, 1), :],
        ]
        return jnp.concatenate(parts, axis=1)

    for h in range(HEADS_STEP):
        c = cols(h)
        k, v = k0[:, c], v0[:, c]
        queries = jnp.concatenate([w[0:rows, c] for w in (wr, wa, wx, b_own)], axis=0)
        grads = jnp.concatenate([w[rows : 2 * rows, c] for w in (wr, wa, wx, b_own)], axis=0)
        row = step * HEADS_STEP + h
        s = nt(k, queries) * (SOFT_SCALE * LOG2E) + bias[...]
        prob = jnp.exp2(s - stat(row))
        gp = nt(v, grads)
        ds = (prob * (gp - stat(16 + row)) * SOFT_SCALE).astype(BF16)
        sdk[:, c] = nn(ds, queries).astype(BF16)
        sdv[:, c] = nn(prob.astype(BF16), grads).astype(BF16)


def on_device(lin_query, lin_key, lin_value, soft_query, soft_key, soft_value, upstream, doc_lengths, doc_domain, domain_weight):
    rows, feats = lin_query.shape
    count, heads = lax.axis_size("ctx"), lax.axis_size("head")
    block = lax.axis_index("ctx")
    place = block.astype(jnp.int32).reshape(1)

    smem = pl.BlockSpec(memory_space=pltpu.SMEM)
    left = pl.BlockSpec(memory_space=pl.ANY)

    def tall(n, step=HEADS_STEP, first=0):
        return pl.BlockSpec((n * rows, step * HD), lambda i: (0, first + i))

    def whole(n):
        return pl.BlockSpec((n, HD), lambda i: (0, 0))

    def array(n, width=feats):
        return jax.ShapeDtypeStruct((n * rows, width), BF16)

    def small(n):
        return jax.ShapeDtypeStruct((n, HD), F32)

    unit = rows * feats * 2
    mm = 2 * rows * HD * feats

    def call(kernel, name, steps, in_specs, out_specs, out_shape, scratch, flops, traffic, args, vmem=VMEM, aliases=None):
        return pl.pallas_call(
            kernel,
            name=name,
            grid=(steps,),
            in_specs=in_specs,
            out_specs=out_specs,
            out_shape=out_shape,
            scratch_shapes=[pltpu.VMEM(s, F32) for s in scratch],
            input_output_aliases=aliases or {},
            compiler_params=pltpu.CompilerParams(dimension_semantics=("arbitrary",), vmem_limit_bytes=vmem),
            cost_estimate=pl.CostEstimate(flops=flops, bytes_accessed=traffic, transcendentals=0),
        )(*args)

    part_steps = feats // HD // PARTS // QUERY_STEP
    part_feats = feats // PARTS
    fwd, bwd, mr, mc = call(
        pack_kernel, "pack", PARTS * part_steps, [smem] * 4 + [tall(1, QUERY_STEP)] * 7,
        [tall(3, QUERY_STEP)] * 2 + [whole(8), whole(4 * rows)],
        [array(3)] * 2 + [small(8), small(4 * rows)],
        [], 2 * mm, 13 * unit,
        (doc_lengths, doc_domain, domain_weight, place,
         lin_key, lin_value, soft_key, soft_value, lin_query, soft_query, upstream),
        PACK_VMEM,
    )

    def shift(x, by):
        return lax.ppermute(x, "ctx", [(i, i + by) for i in range(count) if 0 <= i + by < count])

    def swap(x):
        return lax.ppermute(x, "ctx", [(i, i ^ 1) for i in range(count)])

    odd = block % 2 == 1

    fwd_first = shift(fwd, 2)
    bwd_first = shift(bwd, -2)

    def heads_of(x, p):
        return lax.slice_in_dim(x, p * part_feats, (p + 1) * part_feats, axis=1)

    fwd_far = [shift(jnp.where(odd, heads_of(fwd_first, p), heads_of(fwd, p)), 1) for p in range(PARTS)]
    fwd_swap = swap(fwd_first)
    bwds = bwd_first, swap(bwd_first), shift(jnp.where(odd, bwd, bwd_first), -1)

    results = ()
    for p in range(PARTS):
        one = tall(1, QUERY_STEP, p * part_steps)
        three = tall(3, QUERY_STEP, p * part_steps)
        held = tall(3, QUERY_STEP)
        fixed = 12
        results = call(
            functools.partial(query_kernel, p), "queries", part_steps,
            [smem, whole(8), whole(4 * rows), three, three] + [one] * 3 + [three, three, held]
            + ([left, left, whole(40), whole(rows)] if p > 0 else []),
            [one, one, whole(40), whole(rows)],
            [array(1), array(1), small(40), small(rows)],
            [(4 * rows, HD), (rows, HD), (rows, HD)],
            16 * mm // PARTS, 20 * unit // PARTS,
            (place, mr, mc, fwd, bwd, lin_query, lin_key, lin_value, fwd_first, fwd_swap, fwd_far[p], *results),
            aliases={fixed - 1: 0, fixed: 1} if p > 0 else None,
        )
    soft_dq, lin_dq, stats, _ = results
    s1, s2, s3 = (
        lax.ppermute(stats, "ctx", [(i, (i - o) % count) for i in range(count)]) for o in range(1, RIDE)
    )

    def lin_keys_side(*bwds):
        return call(
            lin_key_kernel, "lin_keys", feats // HD // HEADS_STEP,
            [smem, whole(8), whole(4 * rows), tall(3)] + [tall(1)] * 3 + [tall(3)] * 3,
            [tall(1), tall(1)], [array(1)] * 2, [(rows, HD)],
            6 * mm, 17 * unit,
            (place, mr, mc, bwd, lin_query, lin_key, lin_value, *bwds),
        )

    def soft_keys_side(*stats_rows):
        return call(
            soft_key_kernel, "soft_keys", feats // HD // HEADS_STEP,
            [smem, whole(4 * rows), tall(1), tall(1), tall(3)] + [tall(3)] * 3 + [whole(40)] * 4,
            [tall(1), tall(1)], [array(1)] * 2, [(rows, 4 * HD)],
            16 * mm, 17 * unit,
            (place, mc, soft_key, soft_value, bwd, *bwds, stats, *stats_rows),
        )

    slots = count // RIDE * heads
    groups = [[(g * RIDE + i) * heads + h for g in range(count // RIDE) for h in range(heads)] for i in range(RIDE)]
    lin_dk, lin_dv = lin_keys_side(*bwds)
    s1, s2, s3, lin_dk, lin_dv = lax.optimization_barrier((s1, s2, s3, lin_dk, lin_dv))
    vec = stats[32:33] + s1[32:33] + s2[32:33] + s3[32:33]
    vec, s1, s2, s3 = lax.optimization_barrier((vec, s1, s2, s3))
    got = lax.all_to_all(
        jnp.broadcast_to(vec, (slots, HD)), ("ctx", "head"), 0, 0, tiled=True, axis_index_groups=groups
    )
    soft_dk, soft_dv = soft_keys_side(s1, s2, s3)
    got, soft_dk, soft_dv = lax.optimization_barrier((got, soft_dk, soft_dv))
    domain_loss = jnp.sum(got, axis=0)[:NDOM]
    return (lin_dq, lin_dk, lin_dv, soft_dq, soft_dk, soft_dv, domain_loss)


def solution(mesh):
    spec = P("ctx", "head")
    return jax.shard_map(
        on_device,
        mesh=mesh,
        in_specs=(spec,) * 7 + (P(),) * 3,
        out_specs=(spec,) * 6 + (P(),),
        check_vma=False,
    )
```

time: 112 us -> 98.6 us (0.88)
  the two profiles are of different devices: /device:TPU:10 before, /device:TPU:1 now
where the time goes in v2:
time: 98.6 us; the launch traced here: 97.9 us
  waiting for transfers between devices  36.7 us (37%)
  starting transfers between devices  33.3 us (34%)
  Pallas kernels  22.2 us (23%)
  local copies, waits for them, and re-layouts  3.97 us (4%)
    ppermute x4, waiting for transfers between devices, shift(): lax.ppermute(x, 'ctx', [(i, i + by) for i in range(count) if 0 <= i + by...  33.9 us
    pallas_call x4, Pallas kernels, call(): pl.pallas_call(kernel, name=name, grid=(steps,), in_specs=in_specs, out_s...  22.2 us
    ppermute x4, starting transfers between devices, shift(): lax.ppermute(x, 'ctx', [(i, i + by) for i in range(count) if 0 <= i + by...  15 us
    ppermute x3, starting transfers between devices, on_device(): lax.ppermute(stats, 'ctx', [(i, (i - o) % count) for i in range(count)])  9.68 us
    all_to_all x1, starting transfers between devices, on_device(): lax.all_to_all(jnp.broadcast_to(vec, (slots, HD)), ('ctx', 'head'), 0, 0,...  8.51 us
    unnamed x32, local copies, waits for them, and re-layouts  3.33 us
    all_to_all x1, waiting for transfers between devices, on_device(): lax.all_to_all(jnp.broadcast_to(vec, (slots, HD)), ('ctx', 'head'), 0, 0,...  2.78 us
  transfers between devices with their start and end apart: 10, of which 3 were waited for; matrix products, arithmetic and copies ran while one was open for 0% of the time, Pallas kernels for 18%

profile of v2, /device:TPU:1, one launch (start us, length us, event | category | flops | bytes accessed | tf_op | source)
XLA Modules:
  0.0 97.9 jit_solution(17847259691564262964)
XLA Ops:
  0.6 4.8 %pack.1 = (bf16[384,1536]{1,0:T(8,128)(2,1)}, bf16[384,1536]{1,0:T(8,128)(2,1)}, f32[8,128]{1,0:T(8,128)}, f32[512,128]{1,0:T(8,128)}) custom-call(s32[42]{0:T(128)} %lens.1, s32[42]{0:T(128)} %doms.1, f32[8]{0:T(128)} %wts.1, s32[1]{0:T(128)} %bitcast.place, bf16[128,1536]{1,0:T(8,128)(2,1)} %lk.5, bf16[128,1536]{1,0:T(8,128)(2,1)} %lv.5, ...), custom_call_target="tpu_custom_call" | custom-call | flops 100663296 | bytes 5111808 | tf_op jit(solution)/shard_map/pack/pallas_call | solution.py:264
  5.4 4.4 %collective-permute-start = (bf16[384,1536]{1,0:T(8,128)(2,1)}, bf16[384,1536]{1,0:T(8,128)(2,1)S(1)}, u32[]{:S(2)}, u32[]{:S(2)}) collective-permute-start(bf16[384,1536]{1,0:T(8,128)(2,1)} %get-tuple-element.32.f_own), channel_id=1, source_target_pairs={{0,8},{4,12},{8,16},{12,20},{16,24},{20,28},{24,32},{28,36},{32,40... | collective-permute-start | bytes 3538952 | tf_op jit(solution)/shard_map/ppermute | solution.py:290
  9.9 1.3 %collective-permute-start.6 = (bf16[384,1536]{1,0:T(8,128)(2,1)}, bf16[384,1536]{1,0:T(8,128)(2,1)S(1)}, u32[]{:S(2)}, u32[]{:S(2)}) collective-permute-start(bf16[384,1536]{1,0:T(8,128)(2,1)} %get-tuple-element.33.b_own), channel_id=1, source_target_pairs={{8,0},{12,4},{16,8},{20,12},{24,16},{28,20},{32,24},{36,28},{40,32... | collective-permute-start | bytes 3538952 | tf_op jit(solution)/shard_map/ppermute | solution.py:290
  11.2 0.0 copy-start
  11.2 23.5 %collective-permute-done.wr = bf16[384,1536]{1,0:T(8,128)(2,1)S(1)} collective-permute-done((bf16[384,1536]{1,0:T(8,128)(2,1)}, bf16[384,1536]{1,0:T(8,128)(2,1)S(1)}, u32[]{:S(2)}, u32[]{:S(2)}) %collective-permute-start) | collective-permute-done | bytes 1179680 | tf_op jit(solution)/shard_map/ppermute | solution.py:290
  34.7 0.1 broadcast_select_fusion.1
  34.9 0.0 copy-start.1
  34.9 0.0 copy-start.6
  34.9 0.0 copy-start.7
  34.9 0.0 copy-start.8
  34.9 0.0 copy-start.9
  34.9 0.0 copy-start.15
  34.9 6.8 %collective-permute-start.2 = (bf16[384,1536]{1,0:T(8,128)(2,1)S(1)}, bf16[384,1536]{1,0:T(8,128)(2,1)S(1)}, u32[]{:S(2)}, u32[]{:S(2)}) collective-permute-start(bf16[384,1536]{1,0:T(8,128)(2,1)S(1)} %broadcast_select_fusion.1), channel_id=1, source_target_pairs={{0,4},{4,8},{8,12},{12,16},{16,20},{20,24},{24,28},{28,32},{32,36}... | collective-permute-start | bytes 3538952 | tf_op jit(solution)/shard_map/ppermute | solution.py:290
  41.8 0.1 collective-permute-start.1
  41.9 0.0 collective-permute-done.6.wr
  41.9 0.0 copy-done
  41.9 0.1 broadcast_select_fusion
  42.0 2.4 %collective-permute-start.8 = (bf16[384,1536]{1,0:T(8,128)(2,1)S(1)}, bf16[384,1536]{1,0:T(8,128)(2,1)S(1)}, u32[]{:S(2)}, u32[]{:S(2)}) collective-permute-start(bf16[384,1536]{1,0:T(8,128)(2,1)S(1)} %broadcast_select_fusion), channel_id=1, source_target_pairs={{4,0},{8,4},{12,8},{16,12},{20,16},{24,20},{28,24},{32,28},{36,32}... | collective-permute-start | bytes 3538952 | tf_op jit(solution)/shard_map/ppermute | solution.py:290
  44.4 0.1 collective-permute-start.7
  44.5 10.4 %collective-permute-done.2.wx = bf16[384,1536]{1,0:T(8,128)(2,1)S(1)} collective-permute-done((bf16[384,1536]{1,0:T(8,128)(2,1)S(1)}, bf16[384,1536]{1,0:T(8,128)(2,1)S(1)}, u32[]{:S(2)}, u32[]{:S(2)}) %collective-permute-start.2) | collective-permute-done | bytes 1179680 | tf_op jit(solution)/shard_map/ppermute | solution.py:290
  54.9 0.0 collective-permute-done.1.wa
  54.9 8.9 %queries.1 = (bf16[128,1536]{1,0:T(8,128)(2,1)}, bf16[128,1536]{1,0:T(8,128)(2,1)}, f32[40,128]{1,0:T(8,128)S(1)}, f32[128,128]{1,0:T(8,128)}) custom-call(s32[1]{0:T(128)} %bitcast.place, f32[8,128]{1,0:T(8,128)S(1)} %copy-done.15, f32[512,128]{1,0:T(8,128)S(1)} %copy-done.9, bf16[384,1536]{1,0:T(8,128)(2,1)S(1)} %copy-done.1, ...), custom_call_target="tpu_custom_call" | custom-call | flops 805306368 | bytes 7864320 | tf_op jit(solution)/shard_map/queries/pallas_call | solution.py:264
  63.9 0.0 copy-start.10
  63.9 0.0 copy-start.11
  63.9 0.0 copy-start.12
  63.9 8.9 %collective-permute-start.5 = (f32[40,128]{1,0:T(8,128)S(1)}, f32[40,128]{1,0:T(8,128)S(1)}, u32[]{:S(2)}, u32[]{:S(2)}) collective-permute-start(f32[40,128]{1,0:T(8,128)S(1)} %get-tuple-element.35.s0), channel_id=1, source_target_pairs={{0,244},{4,248},{8,252},{12,0},{16,4},{20,8},{24,12},{28,16},{32,2... | collective-permute-start | bytes 61448 | tf_op jit(solution)/shard_map/ppermute | solution.py:326
  72.9 0.7 collective-permute-start.4
  73.6 0.0 collective-permute-start.3
  73.6 0.0 collective-permute-done.8.wx
  73.6 0.0 collective-permute-done.7.wa
  73.6 0.0 copy-start.4
  73.6 3.7 %lin_keys.1 = (bf16[128,1536]{1,0:T(8,128)(2,1)}, bf16[128,1536]{1,0:T(8,128)(2,1)}) custom-call(s32[1]{0:T(128)} %bitcast.place, f32[8,128]{1,0:T(8,128)S(1)} %copy-done.15, f32[512,128]{1,0:T(8,128)S(1)} %copy-done.9, bf16[384,1536]{1,0:T(8,128)(2,1)S(1)} %copy-done, bf16[128,1536]{1,0:T(8,128)(2,1)S(1)} %copy-done.8, bf16[128,1536]{1,0:T(8,128)(2,1)S(1)} %copy-done.6, ...), custom_call_target="tpu_custom_call" | custom-call | flops 301989888 | bytes 6684672 | tf_op jit(solution)/shard_map/lin_keys/pallas_call | solution.py:264
  77.4 0.0 collective-permute-done.5.s3
  77.4 0.0 collective-permute-done.4.s2
  77.4 0.0 collective-permute-done.3.s1
  77.4 0.0 copy-done.13
  77.4 0.6 broadcast_in_dim.2
  78.1 8.5 %all-to-all-start = ((f32[64,1,128]{2,1,0:T(1,128)}), f32[64,1,128]{2,1,0:T(1,128)S(1)}, u32[]{:S(2)}, u32[]{:S(2)}) async-start(f32[64,1,128]{2,1,0:T(1,128)} %broadcast_in_dim.2), calls=%async_computation | async-start | bytes 65536 | tf_op jit(solution)/shard_map/all_to_all | solution.py:353
  86.6 0.0 copy-done.10
  86.6 0.0 copy-done.11
  86.6 0.0 copy-done.12
  86.6 0.0 copy-start.3
  86.6 1.3 %copy-done.3 = bf16[384,1536]{1,0:T(8,128)(2,1)S(1)} copy-done((bf16[384,1536]{1,0:T(8,128)(2,1)S(1)}, bf16[384,1536]{1,0:T(8,128)(2,1)}, u32[]{:S(2)}) %copy-start.3) | copy-done | bytes 1179672
  87.9 1.3 %copy-done.5 = bf16[384,1536]{1,0:T(8,128)(2,1)S(1)} copy-done((bf16[384,1536]{1,0:T(8,128)(2,1)S(1)}, bf16[384,1536]{1,0:T(8,128)(2,1)}, u32[]{:S(2)}) %copy-start.5) | copy-done | bytes 1179672
  89.2 0.7 copy-done.14
  89.9 4.7 %soft_keys.1 = (bf16[128,1536]{1,0:T(8,128)(2,1)}, bf16[128,1536]{1,0:T(8,128)(2,1)}) custom-call(s32[1]{0:T(128)} %bitcast.place, f32[512,128]{1,0:T(8,128)S(1)} %copy-done.10, bf16[128,1536]{1,0:T(8,128)(2,1)S(1)} %copy-done.11, bf16[128,1536]{1,0:T(8,128)(2,1)S(1)} %copy-done.12, bf16[384,1536]{1,0:T(8,128)(2,1)S(1)} %copy-done, ...), custom_call_target="tpu_custom_call" | custom-call | flops 805306368 | bytes 6684672 | tf_op jit(solution)/shard_map/soft_keys/pallas_call | solution.py:264
  94.6 2.8 %all-to-all-done = f32[64,1,128]{2,1,0:T(1,128)S(1)} async-done(((f32[64,1,128]{2,1,0:T(1,128)}), f32[64,1,128]{2,1,0:T(1,128)S(1)}, u32[]{:S(2)}, u32[]{:S(2)}) %all-to-all-start) | async-done | bytes 32800 | tf_op jit(solution)/shard_map/all_to_all | solution.py:353
  97.4 0.5 reduce_sum.9
  (13 shorter events, 0.0 us)
Async XLA Ops:
  5.4 29.3 %collective-permute-start = (bf16[384,1536]{1,0:T(8,128)(2,1)}, bf16[384,1536]{1,0:T(8,128)(2,1)S(1)}, u32[]{:S(2)}, u32[]{:S(2)}) collective-permute-start(bf16[384,1536]{1,0:T(8,128)(2,1)} %get-tuple-element.32.f_own), channel_id=1, source_target_pairs={{0,8},{4,12},{8,16},{12,20},{16,24},{20,28},{24,32},{28,36},{32,40... | collective-permute-start | bytes 3538952 | tf_op jit(solution)/shard_map/ppermute | solution.py:290
  9.9 32.0 %collective-permute-start.6 = (bf16[384,1536]{1,0:T(8,128)(2,1)}, bf16[384,1536]{1,0:T(8,128)(2,1)S(1)}, u32[]{:S(2)}, u32[]{:S(2)}) collective-permute-start(bf16[384,1536]{1,0:T(8,128)(2,1)} %get-tuple-element.33.b_own), channel_id=1, source_target_pairs={{8,0},{12,4},{16,8},{20,12},{24,16},{28,20},{32,24},{36,28},{40,32... | collective-permute-start | bytes 3538952 | tf_op jit(solution)/shard_map/ppermute | solution.py:290
  11.2 30.7 %copy-start = (bf16[384,1536]{1,0:T(8,128)(2,1)S(1)}, bf16[384,1536]{1,0:T(8,128)(2,1)}, u32[]{:S(2)}) copy-start(bf16[384,1536]{1,0:T(8,128)(2,1)} %get-tuple-element.33.b_own) | copy-start | bytes 3538948
  34.9 20.0 %copy-start.1 = (bf16[384,1536]{1,0:T(8,128)(2,1)S(1)}, bf16[384,1536]{1,0:T(8,128)(2,1)}, u32[]{:S(2)}) copy-start(bf16[384,1536]{1,0:T(8,128)(2,1)} %get-tuple-element.32.f_own) | copy-start | bytes 3538948
  34.9 20.0 %copy-start.6 = (bf16[128,1536]{1,0:T(8,128)(2,1)S(1)}, bf16[128,1536]{1,0:T(8,128)(2,1)}, u32[]{:S(2)}) copy-start(bf16[128,1536]{1,0:T(8,128)(2,1)} %lk.5) | copy-start | bytes 1179652
  34.9 20.0 %copy-start.7 = (bf16[128,1536]{1,0:T(8,128)(2,1)S(1)}, bf16[128,1536]{1,0:T(8,128)(2,1)}, u32[]{:S(2)}) copy-start(bf16[128,1536]{1,0:T(8,128)(2,1)} %lv.5) | copy-start | bytes 1179652
  34.9 20.0 %copy-start.8 = (bf16[128,1536]{1,0:T(8,128)(2,1)S(1)}, bf16[128,1536]{1,0:T(8,128)(2,1)}, u32[]{:S(2)}) copy-start(bf16[128,1536]{1,0:T(8,128)(2,1)} %lq.5) | copy-start | bytes 1179652
  34.9 20.0 %copy-start.9 = (f32[512,128]{1,0:T(8,128)S(1)}, f32[512,128]{1,0:T(8,128)}, u32[]{:S(2)}) copy-start(f32[512,128]{1,0:T(8,128)} %get-tuple-element.31.mc) | copy-start | bytes 786436
  34.9 20.0 %copy-start.15 = (f32[8,128]{1,0:T(8,128)S(1)}, f32[8,128]{1,0:T(8,128)}, u32[]{:S(2)}) copy-start(f32[8,128]{1,0:T(8,128)} %get-tuple-element.30.mr) | copy-start | bytes 12292
  34.9 20.0 %collective-permute-start.2 = (bf16[384,1536]{1,0:T(8,128)(2,1)S(1)}, bf16[384,1536]{1,0:T(8,128)(2,1)S(1)}, u32[]{:S(2)}, u32[]{:S(2)}) collective-permute-start(bf16[384,1536]{1,0:T(8,128)(2,1)S(1)} %broadcast_select_fusion.1), channel_id=1, source_target_pairs={{0,4},{4,8},{8,12},{12,16},{16,20},{20,24},{24,28},{28,32},{32,36}... | collective-permute-start | bytes 3538952 | tf_op jit(solution)/shard_map/ppermute | solution.py:290
  41.8 13.1 %collective-permute-start.1 = (bf16[384,1536]{1,0:T(8,128)(2,1)S(1)}, bf16[384,1536]{1,0:T(8,128)(2,1)S(1)}, u32[]{:S(2)}, u32[]{:S(2)}) collective-permute-start(bf16[384,1536]{1,0:T(8,128)(2,1)S(1)} %collective-permute-done.wr), channel_id=1, source_target_pairs={{0,4},{4,0},{8,12},{12,8},{16,20},{20,16},{24,28},{28,24},{32,36},... | collective-permute-start | bytes 3538952 | tf_op jit(solution)/shard_map/ppermute | solution.py:293
  42.0 31.6 %collective-permute-start.8 = (bf16[384,1536]{1,0:T(8,128)(2,1)S(1)}, bf16[384,1536]{1,0:T(8,128)(2,1)S(1)}, u32[]{:S(2)}, u32[]{:S(2)}) collective-permute-start(bf16[384,1536]{1,0:T(8,128)(2,1)S(1)} %broadcast_select_fusion), channel_id=1, source_target_pairs={{4,0},{8,4},{12,8},{16,12},{20,16},{24,20},{28,24},{32,28},{36,32}... | collective-permute-start | bytes 3538952 | tf_op jit(solution)/shard_map/ppermute | solution.py:290
  44.4 29.2 %collective-permute-start.7 = (bf16[384,1536]{1,0:T(8,128)(2,1)S(1)}, bf16[384,1536]{1,0:T(8,128)(2,1)S(1)}, u32[]{:S(2)}, u32[]{:S(2)}) collective-permute-start(bf16[384,1536]{1,0:T(8,128)(2,1)S(1)} %collective-permute-done.6.wr), channel_id=1, source_target_pairs={{0,4},{4,0},{8,12},{12,8},{16,20},{20,16},{24,28},{28,24},{32,36},... | collective-permute-start | bytes 3538952 | tf_op jit(solution)/shard_map/ppermute | solution.py:293
  63.9 13.5 %copy-start.13 = (f32[40,128]{1,0:T(8,128)}, f32[40,128]{1,0:T(8,128)S(1)}, u32[]{:S(2)}) copy-start(f32[40,128]{1,0:T(8,128)S(1)} %get-tuple-element.35.s0) | copy-start | bytes 61444
  63.9 22.7 %copy-start.10 = (f32[512,128]{1,0:T(8,128)S(1)}, f32[512,128]{1,0:T(8,128)}, u32[]{:S(2)}) copy-start(f32[512,128]{1,0:T(8,128)} %get-tuple-element.31.mc) | copy-start | bytes 786436
  63.9 22.7 %copy-start.11 = (bf16[128,1536]{1,0:T(8,128)(2,1)S(1)}, bf16[128,1536]{1,0:T(8,128)(2,1)}, u32[]{:S(2)}) copy-start(bf16[128,1536]{1,0:T(8,128)(2,1)} %k0.1) | copy-start | bytes 1179652
  63.9 22.7 %copy-start.12 = (bf16[128,1536]{1,0:T(8,128)(2,1)S(1)}, bf16[128,1536]{1,0:T(8,128)(2,1)}, u32[]{:S(2)}) copy-start(bf16[128,1536]{1,0:T(8,128)(2,1)} %v0.1) | copy-start | bytes 1179652
  63.9 13.5 %collective-permute-start.5 = (f32[40,128]{1,0:T(8,128)S(1)}, f32[40,128]{1,0:T(8,128)S(1)}, u32[]{:S(2)}, u32[]{:S(2)}) collective-permute-start(f32[40,128]{1,0:T(8,128)S(1)} %get-tuple-element.35.s0), channel_id=1, source_target_pairs={{0,244},{4,248},{8,252},{12,0},{16,4},{20,8},{24,12},{28,16},{32,2... | collective-permute-start | bytes 61448 | tf_op jit(solution)/shard_map/ppermute | solution.py:326
  72.9 4.5 %collective-permute-start.4 = (f32[40,128]{1,0:T(8,128)S(1)}, f32[40,128]{1,0:T(8,128)S(1)}, u32[]{:S(2)}, u32[]{:S(2)}) collective-permute-start(f32[40,128]{1,0:T(8,128)S(1)} %get-tuple-element.35.s0), channel_id=1, source_target_pairs={{0,248},{4,252},{8,0},{12,4},{16,8},{20,12},{24,16},{28,20},{32,24... | collective-permute-start | bytes 61448 | tf_op jit(solution)/shard_map/ppermute | solution.py:326
  73.6 3.8 %collective-permute-start.3 = (f32[40,128]{1,0:T(8,128)S(1)}, f32[40,128]{1,0:T(8,128)S(1)}, u32[]{:S(2)}, u32[]{:S(2)}) collective-permute-start(f32[40,128]{1,0:T(8,128)S(1)} %get-tuple-element.35.s0), channel_id=1, source_target_pairs={{0,252},{4,0},{8,4},{12,8},{16,12},{20,16},{24,20},{28,24},{32,28}... | collective-permute-start | bytes 61448 | tf_op jit(solution)/shard_map/ppermute | solution.py:326
  73.6 3.8 %copy-start.2 = (bf16[384,1536]{1,0:T(8,128)(2,1)}, bf16[384,1536]{1,0:T(8,128)(2,1)S(1)}, u32[]{:S(2)}) copy-start(bf16[384,1536]{1,0:T(8,128)(2,1)S(1)} %collective-permute-done.8.wx) | copy-start | bytes 3538948
  73.6 3.8 %copy-start.4 = (bf16[384,1536]{1,0:T(8,128)(2,1)}, bf16[384,1536]{1,0:T(8,128)(2,1)S(1)}, u32[]{:S(2)}) copy-start(bf16[384,1536]{1,0:T(8,128)(2,1)S(1)} %collective-permute-done.7.wa) | copy-start | bytes 3538948
  78.1 19.3 %all-to-all-start = ((f32[64,1,128]{2,1,0:T(1,128)}), f32[64,1,128]{2,1,0:T(1,128)S(1)}, u32[]{:S(2)}, u32[]{:S(2)}) async-start(f32[64,1,128]{2,1,0:T(1,128)} %broadcast_in_dim.2), calls=%async_computation | async-start | bytes 65536 | tf_op jit(solution)/shard_map/all_to_all | solution.py:353
  86.6 1.3 %copy-start.3 = (bf16[384,1536]{1,0:T(8,128)(2,1)S(1)}, bf16[384,1536]{1,0:T(8,128)(2,1)}, u32[]{:S(2)}) copy-start(bf16[384,1536]{1,0:T(8,128)(2,1)} %copy-done.2) | copy-start | bytes 3538948
  87.9 1.3 %copy-start.5 = (bf16[384,1536]{1,0:T(8,128)(2,1)S(1)}, bf16[384,1536]{1,0:T(8,128)(2,1)}, u32[]{:S(2)}) copy-start(bf16[384,1536]{1,0:T(8,128)(2,1)} %copy-done.4) | copy-start | bytes 3538948
  89.2 0.7 copy-start.14

commit v3 on v2

--- a/solution.py
+++ b/solution.py
@@ -65,33 +65,40 @@
         mc[i * rows : (i + 1) * rows, :] = jnp.broadcast_to(row, (rows, HD)).T
 
 
-def pack_kernel(lens, doms, wts, place, lk, lv, sk, sv, lq, sq, up, f_out, b_out, mr, mc):
+def pack_forward_kernel(lens, doms, wts, place, lk, lv, sk, sv, f_out, mr, mc):
     rows = lk.shape[0]
 
     @pl.when(pl.program_id(0) == 0)
     def _():
         rows_kernel(lens, doms, wts, place, mr, mc)
 
+    begin_c = mc[0:rows, :]
+    in_last = (begin_c == begin_c[rows - 1 : rows, :]).astype(BF16)
+    f_out[0:rows, :] = sk[...]
+    f_out[rows : 2 * rows, :] = sv[...]
+    for h in range(QUERY_STEP):
+        c = cols(h)
+        f_out[2 * rows : 3 * rows, c] = tn(lk[:, c] * in_last, lv[:, c]).astype(BF16)
+
+
+def pack_backward_kernel(mc, lq, sq, up, b_out):
+    rows = lq.shape[0]
     begin_c = mc[0:rows, :]
     weight = mc[3 * rows : 4 * rows, :]
-    in_last = (begin_c == begin_c[rows - 1 : rows, :]).astype(BF16)
     in_first = (begin_c == begin_c[0:1, :]).astype(BF16)
-    f_out[0:rows, :] = sk[...]
-    f_out[rows : 2 * rows, :] = sv[...]
     b_out[0:rows, :] = sq[...]
     for h in range(QUERY_STEP):
         c = cols(h)
-        f_out[2 * rows : 3 * rows, c] = tn(lk[:, c] * in_last, lv[:, c]).astype(BF16)
         grad = (weight * up[:, c].astype(F32)).astype(BF16)
         b_out[rows : 2 * rows, c] = grad
         b_out[2 * rows : 3 * rows, c] = tn(lq[:, c] * in_first, grad).astype(BF16)
 
 
-def query_kernel(part, place, mr, mc, f_own, b_own, lq, lk, lv, wr, wa, wx, *rest):
+def query_kernel(part, place, mr, mc, f_own, b_own, lq, inner, wr, wa, wx, *rest):
     if part > 0:
         sdq_in, ldq_in, stats_in, acc_in, *rest = rest
     sdq, ldq, stats, acc_out, *rest = rest
-    bias, cm, acc = rest[-3:]
+    bias, acc = rest[-2:]
     rows = lq.shape[0]
     step = pl.program_id(0)
     base = part * QUERY_STEP * pl.num_programs(0)
@@ -108,7 +115,6 @@
             bias[i * rows : (i + 1) * rows, :] = jnp.where(pos >= begin, 0.0, NEG)
         own = (block * rows).astype(F32) + sub
         bias[3 * rows : 4 * rows, :] = jnp.where((own >= begin) & (sub <= lane), 0.0, NEG)
-        cm[...] = jnp.where((mc[0:rows, :] == begin) & (sub <= lane), LIN_SCALE, 0.0)
         if part > 0:
             acc[...] = acc_in[...]
             stats[...] = stats_in[...]
@@ -141,8 +147,7 @@
         stats[pl.ds(16 + row, 1), :] = delta
         deltas.append(delta)
         prior = sum(f * w[2 * rows : 3 * rows, c].astype(F32) for f, w in zip(coef, (wr, wa, wx))).astype(BF16)
-        back = (cm[...] * nt(lv[:, c], grad)).astype(BF16)
-        dq = tn(back, lk[:, c]) + carried * nt(grad, prior)
+        dq = inner[:, c] + carried * nt(grad, prior)
         ldq[:, c] = dq.astype(BF16)
         terms.append(dq * lq[:, c].astype(F32))
     diagonal = iota(square, 0) == iota(square, 1)
@@ -163,11 +168,8 @@
     return 2, jnp.where(odd == 1, near, far), jnp.where(odd == 1, far, near)
 
 
-def lin_key_kernel(place, mr, mc, b_own, lq, lk, lv, wr, wa, wx, ldk, ldv, cm):
+def inner_kernel(mr, mc, b_own, lq, lk, lv, dq, dk, dv, cm):
     rows = lq.shape[0]
-    block = place[0]
-    odd = block % 2
-    offs = offsets(odd, False)
     square = (rows, HD)
 
     @pl.when(pl.program_id(0) == 0)
@@ -175,23 +177,29 @@
         sub, lane = iota(square, 0), iota(square, 1)
         cm[...] = jnp.where((mc[0:rows, :] == mr[0:1, :]) & (sub <= lane), LIN_SCALE, 0.0)
 
+    for h in range(HEADS_STEP):
+        c = cols(h)
+        grad = b_own[rows : 2 * rows, c]
+        k, q = lk[:, c], lq[:, c]
+        scores = (cm[...] * nt(k, q)).astype(BF16)
+        back = (cm[...] * nt(lv[:, c], grad)).astype(BF16)
+        dq[:, c] = tn(back, k)
+        dk[:, c] = nn(back, q)
+        dv[:, c] = nn(scores, grad)
+
+
+def lin_key_kernel(place, mc, lk, lv, dk, dv, wr, wa, wx, ldk, ldv):
+    rows = lk.shape[0]
+    block = place[0]
     end_c = mc[rows : 2 * rows, :]
     extended = jnp.where(end_c > ((block + 1) * rows).astype(F32), LIN_SCALE, 0.0)
     last = end_c[rows - 1 : rows, :]
-    coef = [jnp.where(last > ((block + o) * rows).astype(F32), 1.0, 0.0) for o in offs]
+    coef = [jnp.where(last > ((block + o) * rows).astype(F32), 1.0, 0.0) for o in offsets(block % 2, False)]
     for h in range(HEADS_STEP):
         c = cols(h)
-        grad = b_own[rows : 2 * rows, c]
-        later = (
-            coef[0] * wr[2 * rows : 3 * rows, c].astype(F32)
-            + coef[1] * wa[2 * rows : 3 * rows, c].astype(F32)
-            + coef[2] * wx[2 * rows : 3 * rows, c].astype(F32)
-        ).astype(BF16)
-        k, v, q = lk[:, c], lv[:, c], lq[:, c]
-        scores = (cm[...] * nt(k, q)).astype(BF16)
-        back = (cm[...] * nt(v, grad)).astype(BF16)
-        ldk[:, c] = (nn(back, q) + extended * nt(v, later)).astype(BF16)
-        ldv[:, c] = (nn(scores, grad) + extended * nn(k, later)).astype(BF16)
+        later = sum(f * w[:, c].astype(F32) for f, w in zip(coef, (wr, wa, wx))).astype(BF16)
+        ldk[:, c] = (dk[:, c] + extended * nt(lv[:, c], later)).astype(BF16)
+        ldv[:, c] = (dv[:, c] + extended * nn(lk[:, c], later)).astype(BF16)
 
 
 def soft_key_kernel(place, mc, k0, v0, b_own, wr, wa, wx, s0, s1, s2, s3, sdk, sdv, bias):
@@ -276,13 +284,18 @@
 
     part_steps = feats // HD // PARTS // QUERY_STEP
     part_feats = feats // PARTS
-    fwd, bwd, mr, mc = call(
-        pack_kernel, "pack", PARTS * part_steps, [smem] * 4 + [tall(1, QUERY_STEP)] * 7,
-        [tall(3, QUERY_STEP)] * 2 + [whole(8), whole(4 * rows)],
-        [array(3)] * 2 + [small(8), small(4 * rows)],
-        [], 2 * mm, 13 * unit,
-        (doc_lengths, doc_domain, domain_weight, place,
-         lin_key, lin_value, soft_key, soft_value, lin_query, soft_query, upstream),
+    fwd, mr, mc = call(
+        pack_forward_kernel, "pack_forward", PARTS * part_steps, [smem] * 4 + [tall(1, QUERY_STEP)] * 4,
+        [tall(3, QUERY_STEP), whole(8), whole(4 * rows)],
+        [array(3), small(8), small(4 * rows)],
+        [], mm, 7 * unit,
+        (doc_lengths, doc_domain, domain_weight, place, lin_key, lin_value, soft_key, soft_value),
+        PACK_VMEM,
+    )
+    (bwd,) = call(
+        pack_backward_kernel, "pack_backward", PARTS * part_steps, [whole(4 * rows)] + [tall(1, QUERY_STEP)] * 3,
+        [tall(3, QUERY_STEP)], [array(3)], [], mm, 6 * unit,
+        (mc, lin_query, soft_query, upstream),
         PACK_VMEM,
     )
 
@@ -304,6 +317,13 @@
     fwd_swap = swap(fwd_first)
     bwds = bwd_first, swap(bwd_first), shift(jnp.where(odd, bwd, bwd_first), -1)
 
+    wide = jax.ShapeDtypeStruct((rows, feats), F32)
+    dq_inner, dk_inner, dv_inner = call(
+        inner_kernel, "inner", feats // HD // HEADS_STEP,
+        [whole(8), whole(4 * rows), tall(3)] + [tall(1)] * 3, [tall(1)] * 3, [wide] * 3, [(rows, HD)],
+        5 * mm, 12 * unit,
+        (mr, mc, bwd, lin_query, lin_key, lin_value),
+    )
     results = ()
     for p in range(PARTS):
         one = tall(1, QUERY_STEP, p * part_steps)
@@ -312,13 +332,13 @@
         fixed = 12
         results = call(
             functools.partial(query_kernel, p), "queries", part_steps,
-            [smem, whole(8), whole(4 * rows), three, three] + [one] * 3 + [three, three, held]
+            [smem, whole(8), whole(4 * rows), three, three] + [one] * 2 + [three, three, held]
             + ([left, left, whole(40), whole(rows)] if p > 0 else []),
             [one, one, whole(40), whole(rows)],
             [array(1), array(1), small(40), small(rows)],
-            [(4 * rows, HD), (rows, HD), (rows, HD)],
+            [(4 * rows, HD), (rows, HD)],
             16 * mm // PARTS, 20 * unit // PARTS,
-            (place, mr, mc, fwd, bwd, lin_query, lin_key, lin_value, fwd_first, fwd_swap, fwd_far[p], *results),
+            (place, mr, mc, fwd, bwd, lin_query, dq_inner, fwd_first, fwd_swap, fwd_far[p], *results),
             aliases={fixed - 1: 0, fixed: 1} if p > 0 else None,
         )
     soft_dq, lin_dq, stats, _ = results
@@ -326,13 +346,15 @@
         lax.ppermute(stats, "ctx", [(i, (i - o) % count) for i in range(count)]) for o in range(1, RIDE)
     )
 
+    state = pl.BlockSpec((rows, HEADS_STEP * HD), lambda i: (2, i))
+
     def lin_keys_side(*bwds):
         return call(
             lin_key_kernel, "lin_keys", feats // HD // HEADS_STEP,
-            [smem, whole(8), whole(4 * rows), tall(3)] + [tall(1)] * 3 + [tall(3)] * 3,
-            [tall(1), tall(1)], [array(1)] * 2, [(rows, HD)],
-            6 * mm, 17 * unit,
-            (place, mr, mc, bwd, lin_query, lin_key, lin_value, *bwds),
+            [smem, whole(4 * rows)] + [tall(1)] * 4 + [state] * 3,
+            [tall(1), tall(1)], [array(1)] * 2, [],
+            2 * mm, 11 * unit,
+            (place, mc, lin_key, lin_value, dk_inner, dv_inner, *bwds),
         )
 
     def soft_keys_side(*stats_rows):

time: 98.6 us -> 96.6 us (0.980)
  waiting for transfers between devices: 36.7 us -> 28.7 us
  Pallas kernels: 22.2 us -> 26.8 us
  other arithmetic: 0.79 us -> 2.06 us
  starting transfers between devices: 33.3 us -> 34.5 us
    ppermute x4, waiting for transfers between devices: 33.9 us -> 24.2 us  [shift(): lax.ppermute(x, 'ctx', [(i, i + by) for i in range(count) if 0 <= i + by...]
    pallas_call x4 -> x6, Pallas kernels: 22.2 us -> 26.8 us  [call(): pl.pallas_call(kernel, name=name, grid=(steps,), in_specs=in_specs, out_s...]
    ppermute x4, starting transfers between devices: 15 us -> 13 us  [shift(): lax.ppermute(x, 'ctx', [(i, i + by) for i in range(count) if 0 <= i + by...]
    ppermute x2, starting transfers between devices: 0.19 us -> 1.96 us  [swap(): return lax.ppermute(x, 'ctx', [(i, i ^ 1) for i in range(count)])]
    select_n x1, other arithmetic: 0.13 us -> 1.39 us  [on_device(): jnp.where(odd, heads_of(fwd_first, p), heads_of(fwd, p))]
    all_to_all x1, starting transfers between devices: 8.51 us -> 9.56 us  [on_device(): lax.all_to_all(jnp.broadcast_to(vec, (slots, HD)), ('ctx', 'head'), 0, 0,...]
    unnamed x32 -> x28, local copies, waits for them, and re-layouts: 3.33 us -> 2.6 us
  transfers between devices with their start and end apart: 10 -> 10, of which waited for: 3 -> 5; matrix products, arithmetic and copies ran while one was open for 0% -> 2% of each run, Pallas kernels for 18% -> 24%
where the time goes in v3:
time: 96.6 us; the launch traced here: 96.1 us
  starting transfers between devices  34.5 us (36%)
  waiting for transfers between devices  28.7 us (30%)
  Pallas kernels  26.8 us (28%)
  local copies, waits for them, and re-layouts  3.23 us (3%)
  other arithmetic  2.06 us (2%)
    pallas_call x6, Pallas kernels, call(): pl.pallas_call(kernel, name=name, grid=(steps,), in_specs=in_specs, out_s...  26.8 us
    ppermute x4, waiting for transfers between devices, shift(): lax.ppermute(x, 'ctx', [(i, i + by) for i in range(count) if 0 <= i + by...  24.2 us
    ppermute x4, starting transfers between devices, shift(): lax.ppermute(x, 'ctx', [(i, i + by) for i in range(count) if 0 <= i + by...  13 us
    ppermute x3, starting transfers between devices, on_device(): lax.ppermute(stats, 'ctx', [(i, (i - o) % count) for i in range(count)])  9.96 us
    all_to_all x1, starting transfers between devices, on_device(): lax.all_to_all(jnp.broadcast_to(vec, (slots, HD)), ('ctx', 'head'), 0, 0,...  9.56 us
    all_to_all x1, waiting for transfers between devices, on_device(): lax.all_to_all(jnp.broadcast_to(vec, (slots, HD)), ('ctx', 'head'), 0, 0,...  3.52 us
    unnamed x28, local copies, waits for them, and re-layouts  2.6 us
    ppermute x2, starting transfers between devices, swap(): return lax.ppermute(x, 'ctx', [(i, i ^ 1) for i in range(count)])  1.96 us
  transfers between devices with their start and end apart: 10, of which 5 were waited for; matrix products, arithmetic and copies ran while one was open for 2% of the time, Pallas kernels for 24%

profile of v3, /device:TPU:1, one launch (start us, length us, event | category | flops | bytes accessed | tf_op | source)
XLA Modules:
  0.0 96.1 jit_solution(9682322839194228562)
XLA Ops:
  0.6 4.0 %pack_forward.1 = (bf16[384,1536]{1,0:T(8,128)(2,1)}, f32[8,128]{1,0:T(8,128)}, f32[512,128]{1,0:T(8,128)}) custom-call(s32[42]{0:T(128)} %lens.1, s32[42]{0:T(128)} %doms.1, f32[8]{0:T(128)} %wts.1, s32[1]{0:T(128)} %bitcast.place, bf16[128,1536]{1,0:T(8,128)(2,1)} %lk.5, bf16[128,1536]{1,0:T(8,128)(2,1)} %lv.5, bf16[128,1536]{1,0:T(8,128)(2,1)} %k0.1, ...), custom_call_target="tpu_custom_call" | custom-call | flops 50331648 | bytes 2752512 | tf_op jit(solution)/shard_map/pack_forward/pallas_call | solution.py:272
  4.6 5.4 %collective-permute-start = (bf16[384,1536]{1,0:T(8,128)(2,1)}, bf16[384,1536]{1,0:T(8,128)(2,1)}, u32[]{:S(2)}, u32[]{:S(2)}) collective-permute-start(bf16[384,1536]{1,0:T(8,128)(2,1)} %get-tuple-element.34.f_own), channel_id=1, source_target_pairs={{0,8},{4,12},{8,16},{12,20},{16,24},{20,28},{24,32},{28,36},{32,40... | collective-permute-start | bytes 3538952 | tf_op jit(solution)/shard_map/ppermute | solution.py:303
  10.0 3.8 %pack_backward.1.b_own = bf16[384,1536]{1,0:T(8,128)(2,1)} custom-call(f32[512,128]{1,0:T(8,128)} %get-tuple-element.33.mc, bf16[128,1536]{1,0:T(8,128)(2,1)} %lq.5, bf16[128,1536]{1,0:T(8,128)(2,1)} %sq.1, bf16[128,1536]{1,0:T(8,128)(2,1)} %up.1), custom_call_target="tpu_custom_call" | custom-call | flops 50331648 | bytes 2359296 | tf_op jit(solution)/shard_map/pack_backward/pallas_call | solution.py:272
  13.9 1.3 %collective-permute-start.6 = (bf16[384,1536]{1,0:T(8,128)(2,1)}, bf16[384,1536]{1,0:T(8,128)(2,1)S(1)}, u32[]{:S(2)}, u32[]{:S(2)}) collective-permute-start(bf16[384,1536]{1,0:T(8,128)(2,1)} %pack_backward.1.b_own), channel_id=1, source_target_pairs={{8,0},{12,4},{16,8},{20,12},{24,16},{28,20},{32,24},{36,28},{40,32... | collective-permute-start | bytes 3538952 | tf_op jit(solution)/shard_map/ppermute | solution.py:303
  15.2 0.0 copy-start
  15.2 18.8 %collective-permute-done.wr = bf16[384,1536]{1,0:T(8,128)(2,1)} collective-permute-done((bf16[384,1536]{1,0:T(8,128)(2,1)}, bf16[384,1536]{1,0:T(8,128)(2,1)}, u32[]{:S(2)}, u32[]{:S(2)}) %collective-permute-start) | collective-permute-done | bytes 1179680 | tf_op jit(solution)/shard_map/ppermute | solution.py:303
  33.9 0.0 copy-done.2
  33.9 1.4 %broadcast_select_fusion.1 = bf16[384,1536]{1,0:T(8,128)(2,1)S(1)} fusion(bf16[384,1536]{1,0:T(8,128)(2,1)} %collective-permute-done.wr, bf16[384,1536]{1,0:T(8,128)(2,1)S(1)} %copy-done.2, pred[]{:T(512)S(6)} %eq.5), kind=kLoop, calls=%fused_computation.1 | loop fusion | flops 589824 | bytes 3538945 | tf_op jit(solution)/shard_map/jit(_where)/select_n | solution.py:316
  35.3 0.0 copy-start.1
  35.4 0.0 copy-start.8
  35.4 0.0 copy-start.9
  35.4 0.0 copy-start.10
  35.4 0.0 copy-start.13
  35.4 4.4 %collective-permute-start.2 = (bf16[384,1536]{1,0:T(8,128)(2,1)S(1)}, bf16[384,1536]{1,0:T(8,128)(2,1)S(1)}, u32[]{:S(2)}, u32[]{:S(2)}) collective-permute-start(bf16[384,1536]{1,0:T(8,128)(2,1)S(1)} %broadcast_select_fusion.1), channel_id=1, source_target_pairs={{0,4},{4,8},{8,12},{12,16},{16,20},{20,24},{24,28},{28,32},{32,36}... | collective-permute-start | bytes 3538952 | tf_op jit(solution)/shard_map/ppermute | solution.py:303
  39.8 0.1 collective-permute-start.1
  39.9 2.6 %collective-permute-done.6.wr = bf16[384,1536]{1,0:T(8,128)(2,1)S(1)} collective-permute-done((bf16[384,1536]{1,0:T(8,128)(2,1)}, bf16[384,1536]{1,0:T(8,128)(2,1)S(1)}, u32[]{:S(2)}, u32[]{:S(2)}) %collective-permute-start.6) | collective-permute-done | bytes 1179680 | tf_op jit(solution)/shard_map/ppermute | solution.py:303
  42.5 1.9 %collective-permute-start.7 = (bf16[384,1536]{1,0:T(8,128)(2,1)S(1)}, bf16[384,1536]{1,0:T(8,128)(2,1)S(1)}, u32[]{:S(2)}, u32[]{:S(2)}) collective-permute-start(bf16[384,1536]{1,0:T(8,128)(2,1)S(1)} %collective-permute-done.6.wr), channel_id=1, source_target_pairs={{0,4},{4,0},{8,12},{12,8},{16,20},{20,16},{24,28},{28,24},{32,36},... | collective-permute-start | bytes 3538952 | tf_op jit(solution)/shard_map/ppermute | solution.py:306
  44.3 0.0 copy-done
  44.3 0.1 broadcast_select_fusion
  44.5 1.9 %collective-permute-start.8 = (bf16[384,1536]{1,0:T(8,128)(2,1)S(1)}, bf16[384,1536]{1,0:T(8,128)(2,1)S(1)}, u32[]{:S(2)}, u32[]{:S(2)}) collective-permute-start(bf16[384,1536]{1,0:T(8,128)(2,1)S(1)} %broadcast_select_fusion), channel_id=1, source_target_pairs={{4,0},{8,4},{12,8},{16,12},{20,16},{24,20},{28,24},{32,28},{36,32}... | collective-permute-start | bytes 3538952 | tf_op jit(solution)/shard_map/ppermute | solution.py:303
  46.4 0.0 copy-done.1
  46.5 3.5 %inner.1 = (f32[128,1536]{1,0:T(8,128)S(1)}, f32[128,1536]{1,0:T(8,128)S(1)}, f32[128,1536]{1,0:T(8,128)S(1)}) custom-call(f32[8,128]{1,0:T(8,128)S(1)} %copy-done.13, f32[512,128]{1,0:T(8,128)S(1)} %copy-done.1, bf16[384,1536]{1,0:T(8,128)(2,1)S(1)} %copy-done, bf16[128,1536]{1,0:T(8,128)(2,1)S(1)} %copy-done.8, bf16[128,1536]{1,0:T(8,128)(2,1)S(1)} %copy-done.9, ...), custom_call_target="tpu_custom_call" | custom-call | flops 251658240 | bytes 4718592 | tf_op jit(solution)/shard_map/inner/pallas_call | solution.py:272
  50.0 0.0 collective-permute-done.1.wa
  50.0 2.9 %collective-permute-done.2.wx = bf16[384,1536]{1,0:T(8,128)(2,1)S(1)} collective-permute-done((bf16[384,1536]{1,0:T(8,128)(2,1)S(1)}, bf16[384,1536]{1,0:T(8,128)(2,1)S(1)}, u32[]{:S(2)}, u32[]{:S(2)}) %collective-permute-start.2) | collective-permute-done | bytes 1179680 | tf_op jit(solution)/shard_map/ppermute | solution.py:303
  52.9 0.0 copy-done.3
  52.9 8.5 %queries.1 = (bf16[128,1536]{1,0:T(8,128)(2,1)}, bf16[128,1536]{1,0:T(8,128)(2,1)}, f32[40,128]{1,0:T(8,128)S(1)}, f32[128,128]{1,0:T(8,128)}) custom-call(s32[1]{0:T(128)} %bitcast.place, f32[8,128]{1,0:T(8,128)S(1)} %copy-done.13, f32[512,128]{1,0:T(8,128)S(1)} %copy-done.1, bf16[384,1536]{1,0:T(8,128)(2,1)S(1)} %copy-done.3, ...), custom_call_target="tpu_custom_call" | custom-call | flops 805306368 | bytes 7864320 | tf_op jit(solution)/shard_map/queries/pallas_call | solution.py:272
  61.5 0.0 collective-permute-start.3
  61.5 9.0 %collective-permute-start.4 = (f32[40,128]{1,0:T(8,128)S(1)}, f32[40,128]{1,0:T(8,128)S(1)}, u32[]{:S(2)}, u32[]{:S(2)}) collective-permute-start(f32[40,128]{1,0:T(8,128)S(1)} %get-tuple-element.37.s0), channel_id=1, source_target_pairs={{0,248},{4,252},{8,0},{12,4},{16,8},{20,12},{24,16},{28,20},{32,24... | collective-permute-start | bytes 61448 | tf_op jit(solution)/shard_map/ppermute | solution.py:346
  70.4 1.0 %collective-permute-start.5 = (f32[40,128]{1,0:T(8,128)S(1)}, f32[40,128]{1,0:T(8,128)S(1)}, u32[]{:S(2)}, u32[]{:S(2)}) collective-permute-start(f32[40,128]{1,0:T(8,128)S(1)} %get-tuple-element.37.s0), channel_id=1, source_target_pairs={{0,244},{4,248},{8,252},{12,0},{16,4},{20,8},{24,12},{28,16},{32,2... | collective-permute-start | bytes 61448 | tf_op jit(solution)/shard_map/ppermute | solution.py:346
  71.4 0.0 collective-permute-done.7.wa
  71.4 0.0 collective-permute-done.8.wx
  71.4 0.0 copy-start.6
  71.4 0.0 copy-start.11
  71.4 0.0 copy-start.12
  71.5 2.2 %lin_keys.1 = (bf16[128,1536]{1,0:T(8,128)(2,1)}, bf16[128,1536]{1,0:T(8,128)(2,1)}) custom-call(s32[1]{0:T(128)} %bitcast.place, f32[512,128]{1,0:T(8,128)S(1)} %copy-done.1, bf16[128,1536]{1,0:T(8,128)(2,1)S(1)} %copy-done.9, bf16[128,1536]{1,0:T(8,128)(2,1)S(1)} %copy-done.10, f32[128,1536]{1,0:T(8,128)S(1)} %get-tuple-element.38.dk, ...), custom_call_target="tpu_custom_call" | custom-call | flops 100663296 | bytes 4325376 | tf_op jit(solution)/shard_map/lin_keys/pallas_call | solution.py:272
  73.6 0.0 collective-permute-done.3.s1
  73.7 0.0 collective-permute-done.4.s2
  73.7 0.9 collective-permute-done.5.s3
  74.6 0.6 broadcast_in_dim.2
  75.2 9.6 %all-to-all-start = ((f32[64,1,128]{2,1,0:T(1,128)}), f32[64,1,128]{2,1,0:T(1,128)S(1)}, u32[]{:S(2)}, u32[]{:S(2)}) async-start(f32[64,1,128]{2,1,0:T(1,128)} %broadcast_in_dim.2), calls=%async_computation | async-start | bytes 65536 | tf_op jit(solution)/shard_map/all_to_all | solution.py:375
  84.8 0.0 copy-done.11
  84.8 0.0 copy-done.12
  84.8 0.0 copy-start.5
  84.8 1.3 %copy-done.5 = bf16[384,1536]{1,0:T(8,128)(2,1)S(1)} copy-done((bf16[384,1536]{1,0:T(8,128)(2,1)S(1)}, bf16[384,1536]{1,0:T(8,128)(2,1)}, u32[]{:S(2)}) %copy-start.5) | copy-done | bytes 1179672
  86.1 1.3 %copy-done.7 = bf16[384,1536]{1,0:T(8,128)(2,1)S(1)} copy-done((bf16[384,1536]{1,0:T(8,128)(2,1)S(1)}, bf16[384,1536]{1,0:T(8,128)(2,1)}, u32[]{:S(2)}) %copy-start.7) | copy-done | bytes 1179672
  87.3 4.7 %soft_keys.1 = (bf16[128,1536]{1,0:T(8,128)(2,1)}, bf16[128,1536]{1,0:T(8,128)(2,1)}) custom-call(s32[1]{0:T(128)} %bitcast.place, f32[512,128]{1,0:T(8,128)S(1)} %copy-done.1, bf16[128,1536]{1,0:T(8,128)(2,1)S(1)} %copy-done.11, bf16[128,1536]{1,0:T(8,128)(2,1)S(1)} %copy-done.12, bf16[384,1536]{1,0:T(8,128)(2,1)S(1)} %copy-done, ...), custom_call_target="tpu_custom_call" | custom-call | flops 805306368 | bytes 6684672 | tf_op jit(solution)/shard_map/soft_keys/pallas_call | solution.py:272
  92.1 3.5 %all-to-all-done = f32[64,1,128]{2,1,0:T(1,128)S(1)} async-done(((f32[64,1,128]{2,1,0:T(1,128)}), f32[64,1,128]{2,1,0:T(1,128)S(1)}, u32[]{:S(2)}, u32[]{:S(2)}) %all-to-all-start) | async-done | bytes 32800 | tf_op jit(solution)/shard_map/all_to_all | solution.py:375
  95.6 0.5 reduce_sum.9
  (11 shorter events, 0.0 us)
Async XLA Ops:
  4.6 29.3 %collective-permute-start = (bf16[384,1536]{1,0:T(8,128)(2,1)}, bf16[384,1536]{1,0:T(8,128)(2,1)}, u32[]{:S(2)}, u32[]{:S(2)}) collective-permute-start(bf16[384,1536]{1,0:T(8,128)(2,1)} %get-tuple-element.34.f_own), channel_id=1, source_target_pairs={{0,8},{4,12},{8,16},{12,20},{16,24},{20,28},{24,32},{28,36},{32,40... | collective-permute-start | bytes 3538952 | tf_op jit(solution)/shard_map/ppermute | solution.py:303
  10.0 23.9 %copy-start.2 = (bf16[384,1536]{1,0:T(8,128)(2,1)S(1)}, bf16[384,1536]{1,0:T(8,128)(2,1)}, u32[]{:S(2)}) copy-start(bf16[384,1536]{1,0:T(8,128)(2,1)} %get-tuple-element.34.f_own) | copy-start | bytes 3538948
  13.9 28.6 %collective-permute-start.6 = (bf16[384,1536]{1,0:T(8,128)(2,1)}, bf16[384,1536]{1,0:T(8,128)(2,1)S(1)}, u32[]{:S(2)}, u32[]{:S(2)}) collective-permute-start(bf16[384,1536]{1,0:T(8,128)(2,1)} %pack_backward.1.b_own), channel_id=1, source_target_pairs={{8,0},{12,4},{16,8},{20,12},{24,16},{28,20},{32,24},{36,28},{40,32... | collective-permute-start | bytes 3538952 | tf_op jit(solution)/shard_map/ppermute | solution.py:303
  15.2 29.2 %copy-start = (bf16[384,1536]{1,0:T(8,128)(2,1)S(1)}, bf16[384,1536]{1,0:T(8,128)(2,1)}, u32[]{:S(2)}) copy-start(bf16[384,1536]{1,0:T(8,128)(2,1)} %pack_backward.1.b_own) | copy-start | bytes 3538948
  35.3 11.1 %copy-start.1 = (f32[512,128]{1,0:T(8,128)S(1)}, f32[512,128]{1,0:T(8,128)}, u32[]{:S(2)}) copy-start(f32[512,128]{1,0:T(8,128)} %get-tuple-element.33.mc) | copy-start | bytes 786436
  35.4 11.1 %copy-start.8 = (bf16[128,1536]{1,0:T(8,128)(2,1)S(1)}, bf16[128,1536]{1,0:T(8,128)(2,1)}, u32[]{:S(2)}) copy-start(bf16[128,1536]{1,0:T(8,128)(2,1)} %lq.5) | copy-start | bytes 1179652
  35.4 11.1 %copy-start.9 = (bf16[128,1536]{1,0:T(8,128)(2,1)S(1)}, bf16[128,1536]{1,0:T(8,128)(2,1)}, u32[]{:S(2)}) copy-start(bf16[128,1536]{1,0:T(8,128)(2,1)} %lk.5) | copy-start | bytes 1179652
  35.4 11.1 %copy-start.10 = (bf16[128,1536]{1,0:T(8,128)(2,1)S(1)}, bf16[128,1536]{1,0:T(8,128)(2,1)}, u32[]{:S(2)}) copy-start(bf16[128,1536]{1,0:T(8,128)(2,1)} %lv.5) | copy-start | bytes 1179652
  35.4 11.1 %copy-start.13 = (f32[8,128]{1,0:T(8,128)S(1)}, f32[8,128]{1,0:T(8,128)}, u32[]{:S(2)}) copy-start(f32[8,128]{1,0:T(8,128)} %get-tuple-element.32.mr) | copy-start | bytes 12292
  35.4 17.5 %collective-permute-start.2 = (bf16[384,1536]{1,0:T(8,128)(2,1)S(1)}, bf16[384,1536]{1,0:T(8,128)(2,1)S(1)}, u32[]{:S(2)}, u32[]{:S(2)}) collective-permute-start(bf16[384,1536]{1,0:T(8,128)(2,1)S(1)} %broadcast_select_fusion.1), channel_id=1, source_target_pairs={{0,4},{4,8},{8,12},{12,16},{16,20},{20,24},{24,28},{28,32},{32,36}... | collective-permute-start | bytes 3538952 | tf_op jit(solution)/shard_map/ppermute | solution.py:303
  39.8 10.2 %collective-permute-start.1 = (bf16[384,1536]{1,0:T(8,128)(2,1)}, bf16[384,1536]{1,0:T(8,128)(2,1)S(1)}, u32[]{:S(2)}, u32[]{:S(2)}) collective-permute-start(bf16[384,1536]{1,0:T(8,128)(2,1)} %collective-permute-done.wr), channel_id=1, source_target_pairs={{0,4},{4,0},{8,12},{12,8},{16,20},{20,16},{24,28},{28,24},{32,36},... | collective-permute-start | bytes 3538952 | tf_op jit(solution)/shard_map/ppermute | solution.py:306
  42.5 28.9 %collective-permute-start.7 = (bf16[384,1536]{1,0:T(8,128)(2,1)S(1)}, bf16[384,1536]{1,0:T(8,128)(2,1)S(1)}, u32[]{:S(2)}, u32[]{:S(2)}) collective-permute-start(bf16[384,1536]{1,0:T(8,128)(2,1)S(1)} %collective-permute-done.6.wr), channel_id=1, source_target_pairs={{0,4},{4,0},{8,12},{12,8},{16,20},{20,16},{24,28},{28,24},{32,36},... | collective-permute-start | bytes 3538952 | tf_op jit(solution)/shard_map/ppermute | solution.py:306
  44.5 27.0 %collective-permute-start.8 = (bf16[384,1536]{1,0:T(8,128)(2,1)S(1)}, bf16[384,1536]{1,0:T(8,128)(2,1)S(1)}, u32[]{:S(2)}, u32[]{:S(2)}) collective-permute-start(bf16[384,1536]{1,0:T(8,128)(2,1)S(1)} %broadcast_select_fusion), channel_id=1, source_target_pairs={{4,0},{8,4},{12,8},{16,12},{20,16},{24,20},{28,24},{32,28},{36,32}... | collective-permute-start | bytes 3538952 | tf_op jit(solution)/shard_map/ppermute | solution.py:303
  46.4 6.5 %copy-start.3 = (bf16[384,1536]{1,0:T(8,128)(2,1)S(1)}, bf16[384,1536]{1,0:T(8,128)(2,1)}, u32[]{:S(2)}) copy-start(bf16[384,1536]{1,0:T(8,128)(2,1)} %get-tuple-element.34.f_own) | copy-start | bytes 3538948
  61.5 12.2 %collective-permute-start.3 = (f32[40,128]{1,0:T(8,128)S(1)}, f32[40,128]{1,0:T(8,128)S(1)}, u32[]{:S(2)}, u32[]{:S(2)}) collective-permute-start(f32[40,128]{1,0:T(8,128)S(1)} %get-tuple-element.37.s0), channel_id=1, source_target_pairs={{0,252},{4,0},{8,4},{12,8},{16,12},{20,16},{24,20},{28,24},{32,28}... | collective-permute-start | bytes 61448 | tf_op jit(solution)/shard_map/ppermute | solution.py:346
  61.5 12.2 %collective-permute-start.4 = (f32[40,128]{1,0:T(8,128)S(1)}, f32[40,128]{1,0:T(8,128)S(1)}, u32[]{:S(2)}, u32[]{:S(2)}) collective-permute-start(f32[40,128]{1,0:T(8,128)S(1)} %get-tuple-element.37.s0), channel_id=1, source_target_pairs={{0,248},{4,252},{8,0},{12,4},{16,8},{20,12},{24,16},{28,20},{32,24... | collective-permute-start | bytes 61448 | tf_op jit(solution)/shard_map/ppermute | solution.py:346
  70.4 4.1 %collective-permute-start.5 = (f32[40,128]{1,0:T(8,128)S(1)}, f32[40,128]{1,0:T(8,128)S(1)}, u32[]{:S(2)}, u32[]{:S(2)}) collective-permute-start(f32[40,128]{1,0:T(8,128)S(1)} %get-tuple-element.37.s0), channel_id=1, source_target_pairs={{0,244},{4,248},{8,252},{12,0},{16,4},{20,8},{24,12},{28,16},{32,2... | collective-permute-start | bytes 61448 | tf_op jit(solution)/shard_map/ppermute | solution.py:346
  71.4 2.2 %copy-start.4 = (bf16[384,1536]{1,0:T(8,128)(2,1)}, bf16[384,1536]{1,0:T(8,128)(2,1)S(1)}, u32[]{:S(2)}) copy-start(bf16[384,1536]{1,0:T(8,128)(2,1)S(1)} %collective-permute-done.7.wa) | copy-start | bytes 3538948
  71.4 2.2 %copy-start.6 = (bf16[384,1536]{1,0:T(8,128)(2,1)}, bf16[384,1536]{1,0:T(8,128)(2,1)S(1)}, u32[]{:S(2)}) copy-start(bf16[384,1536]{1,0:T(8,128)(2,1)S(1)} %collective-permute-done.8.wx) | copy-start | bytes 3538948
  71.4 13.3 %copy-start.11 = (bf16[128,1536]{1,0:T(8,128)(2,1)S(1)}, bf16[128,1536]{1,0:T(8,128)(2,1)}, u32[]{:S(2)}) copy-start(bf16[128,1536]{1,0:T(8,128)(2,1)} %k0.1) | copy-start | bytes 1179652
  71.4 13.3 %copy-start.12 = (bf16[128,1536]{1,0:T(8,128)(2,1)S(1)}, bf16[128,1536]{1,0:T(8,128)(2,1)}, u32[]{:S(2)}) copy-start(bf16[128,1536]{1,0:T(8,128)(2,1)} %v0.1) | copy-start | bytes 1179652
  75.2 20.4 %all-to-all-start = ((f32[64,1,128]{2,1,0:T(1,128)}), f32[64,1,128]{2,1,0:T(1,128)S(1)}, u32[]{:S(2)}, u32[]{:S(2)}) async-start(f32[64,1,128]{2,1,0:T(1,128)} %broadcast_in_dim.2), calls=%async_computation | async-start | bytes 65536 | tf_op jit(solution)/shard_map/all_to_all | solution.py:375
  84.8 1.3 %copy-start.5 = (bf16[384,1536]{1,0:T(8,128)(2,1)S(1)}, bf16[384,1536]{1,0:T(8,128)(2,1)}, u32[]{:S(2)}) copy-start(bf16[384,1536]{1,0:T(8,128)(2,1)} %copy-done.4) | copy-start | bytes 3538948
  86.1 1.3 %copy-start.7 = (bf16[384,1536]{1,0:T(8,128)(2,1)S(1)}, bf16[384,1536]{1,0:T(8,128)(2,1)}, u32[]{:S(2)}) copy-start(bf16[384,1536]{1,0:T(8,128)(2,1)} %copy-done.6) | copy-start | bytes 3538948

commit v4 on v3

--- a/solution.py
+++ b/solution.py
@@ -14,10 +14,10 @@
 SOFT_SCALE = HD ** (-0.5)
 LOG2E = 1.4426950408889634
 NEG = -1e30
-HEADS_STEP = 4
+HEADS_STEP = 6
 PARTS = 1
 RIDE = 4
-QUERY_STEP = 4
+QUERY_STEP = 6
 VMEM = 16 * 1024 * 1024
 PACK_VMEM = 60 * 1024 * 1024
 
@@ -140,8 +140,8 @@
         total = jnp.sum(e, axis=0, keepdims=True)
         prob = e * (1.0 / total)
         delta = jnp.sum(prob * gp, axis=0, keepdims=True)
-        ds = (prob * (gp - delta) * SOFT_SCALE).astype(BF16)
-        sdq[:, c] = tn(ds, keys).astype(BF16)
+        ds = (prob * (gp - delta)).astype(BF16)
+        sdq[:, c] = (tn(ds, keys) * SOFT_SCALE).astype(BF16)
         row = base + step * QUERY_STEP + h
         stats[pl.ds(row, 1), :] = top + jnp.log2(total)
         stats[pl.ds(16 + row, 1), :] = delta
@@ -239,8 +239,8 @@
         s = nt(k, queries) * (SOFT_SCALE * LOG2E) + bias[...]
         prob = jnp.exp2(s - stat(row))
         gp = nt(v, grads)
-        ds = (prob * (gp - stat(16 + row)) * SOFT_SCALE).astype(BF16)
-        sdk[:, c] = nn(ds, queries).astype(BF16)
+        ds = (prob * (gp - stat(16 + row))).astype(BF16)
+        sdk[:, c] = (nn(ds, queries) * SOFT_SCALE).astype(BF16)
         sdv[:, c] = nn(prob.astype(BF16), grads).astype(BF16)
 
 
@@ -363,7 +363,7 @@
             [smem, whole(4 * rows), tall(1), tall(1), tall(3)] + [tall(3)] * 3 + [whole(40)] * 4,
             [tall(1), tall(1)], [array(1)] * 2, [(rows, 4 * HD)],
             16 * mm, 17 * unit,
-            (place, mc, soft_key, soft_value, bwd, *bwds, stats, *stats_rows),
+            (place, mc, soft_key, soft_value, bwd, *bwds, stats, *stats_rows), PACK_VMEM,
         )
 
     slots = count // RIDE * heads

time: 96.6 us -> 95 us (0.983)
  waiting for transfers between devices: 28.7 us -> 31.3 us
  local copies, waits for them, and re-layouts: 3.23 us -> 0.7 us
  Pallas kernels: 26.8 us -> 25.2 us
    unnamed x28 -> x30, local copies, waits for them, and re-layouts: 2.6 us -> 0.07 us
    pallas_call x6, Pallas kernels: 26.8 us -> 25.2 us  [call(): pl.pallas_call(kernel, name=name, grid=(steps,), in_specs=in_specs, out_s...]
    ppermute x4, waiting for transfers between devices: 24.2 us -> 25.4 us  [shift(): lax.ppermute(x, 'ctx', [(i, i + by) for i in range(count) if 0 <= i + by...]
    all_to_all x1, waiting for transfers between devices: 3.52 us -> 4.53 us  [on_device(): lax.all_to_all(jnp.broadcast_to(vec, (slots, HD)), ('ctx', 'head'), 0, 0,...]
where the time goes in v4:
time: 95 us; the launch traced here: 94.7 us
  starting transfers between devices  34.6 us (36%)
  waiting for transfers between devices  31.3 us (33%)
  Pallas kernels  25.2 us (27%)
  other arithmetic  2.06 us (2%)
    ppermute x4, waiting for transfers between devices, shift(): lax.ppermute(x, 'ctx', [(i, i + by) for i in range(count) if 0 <= i + by...  25.4 us
    pallas_call x6, Pallas kernels, call(): pl.pallas_call(kernel, name=name, grid=(steps,), in_specs=in_specs, out_s...  25.2 us
    ppermute x4, starting transfers between devices, shift(): lax.ppermute(x, 'ctx', [(i, i + by) for i in range(count) if 0 <= i + by...  13 us
    ppermute x3, starting transfers between devices, on_device(): lax.ppermute(stats, 'ctx', [(i, (i - o) % count) for i in range(count)])  10 us
    all_to_all x1, starting transfers between devices, on_device(): lax.all_to_all(jnp.broadcast_to(vec, (slots, HD)), ('ctx', 'head'), 0, 0,...  9.57 us
    all_to_all x1, waiting for transfers between devices, on_device(): lax.all_to_all(jnp.broadcast_to(vec, (slots, HD)), ('ctx', 'head'), 0, 0,...  4.53 us
    ppermute x2, starting transfers between devices, swap(): return lax.ppermute(x, 'ctx', [(i, i ^ 1) for i in range(count)])  1.96 us
  transfers between devices with their start and end apart: 10, of which 5 were waited for; matrix products, arithmetic and copies ran while one was open for 2% of the time, Pallas kernels for 24%

profile of v4, /device:TPU:1, one launch (start us, length us, event | category | flops | bytes accessed | tf_op | source)
XLA Modules:
  0.0 94.7 jit_solution(5202114330741527219)
XLA Ops:
  0.6 2.9 %pack_forward.1 = (bf16[384,1536]{1,0:T(8,128)(2,1)}, f32[8,128]{1,0:T(8,128)}, f32[512,128]{1,0:T(8,128)}) custom-call(s32[42]{0:T(128)} %lens.1, s32[42]{0:T(128)} %doms.1, f32[8]{0:T(128)} %wts.1, s32[1]{0:T(128)} %bitcast.place, bf16[128,1536]{1,0:T(8,128)(2,1)} %lk.5, bf16[128,1536]{1,0:T(8,128)(2,1)} %lv.5, bf16[128,1536]{1,0:T(8,128)(2,1)} %k0.1, ...), custom_call_target="tpu_custom_call" | custom-call | flops 50331648 | bytes 2752512 | tf_op jit(solution)/shard_map/pack_forward/pallas_call | solution.py:272
  3.5 5.4 %collective-permute-start = (bf16[384,1536]{1,0:T(8,128)(2,1)}, bf16[384,1536]{1,0:T(8,128)(2,1)}, u32[]{:S(2)}, u32[]{:S(2)}) collective-permute-start(bf16[384,1536]{1,0:T(8,128)(2,1)} %get-tuple-element.34.f_own), channel_id=1, source_target_pairs={{0,8},{4,12},{8,16},{12,20},{16,24},{20,28},{24,32},{28,36},{32,40... | collective-permute-start | bytes 3538952 | tf_op jit(solution)/shard_map/ppermute | solution.py:303
  8.9 2.8 %pack_backward.1.b_own = bf16[384,1536]{1,0:T(8,128)(2,1)} custom-call(f32[512,128]{1,0:T(8,128)} %get-tuple-element.33.mc, bf16[128,1536]{1,0:T(8,128)(2,1)} %lq.5, bf16[128,1536]{1,0:T(8,128)(2,1)} %sq.1, bf16[128,1536]{1,0:T(8,128)(2,1)} %up.1), custom_call_target="tpu_custom_call" | custom-call | flops 50331648 | bytes 2359296 | tf_op jit(solution)/shard_map/pack_backward/pallas_call | solution.py:272
  11.7 1.3 %collective-permute-start.6 = (bf16[384,1536]{1,0:T(8,128)(2,1)}, bf16[384,1536]{1,0:T(8,128)(2,1)S(1)}, u32[]{:S(2)}, u32[]{:S(2)}) collective-permute-start(bf16[384,1536]{1,0:T(8,128)(2,1)} %pack_backward.1.b_own), channel_id=1, source_target_pairs={{8,0},{12,4},{16,8},{20,12},{24,16},{28,20},{32,24},{36,28},{40,32... | collective-permute-start | bytes 3538952 | tf_op jit(solution)/shard_map/ppermute | solution.py:303
  13.0 0.0 copy-start
  13.0 19.8 %collective-permute-done.wr = bf16[384,1536]{1,0:T(8,128)(2,1)} collective-permute-done((bf16[384,1536]{1,0:T(8,128)(2,1)}, bf16[384,1536]{1,0:T(8,128)(2,1)}, u32[]{:S(2)}, u32[]{:S(2)}) %collective-permute-start) | collective-permute-done | bytes 1179680 | tf_op jit(solution)/shard_map/ppermute | solution.py:303
  32.8 0.0 copy-done.3
  32.8 1.4 %broadcast_select_fusion.1 = bf16[384,1536]{1,0:T(8,128)(2,1)S(1)} fusion(bf16[384,1536]{1,0:T(8,128)(2,1)} %collective-permute-done.wr, bf16[384,1536]{1,0:T(8,128)(2,1)S(1)} %copy-done.3, pred[]{:T(512)S(6)} %eq.5), kind=kLoop, calls=%fused_computation.1 | loop fusion | flops 589824 | bytes 3538945 | tf_op jit(solution)/shard_map/jit(_where)/select_n | solution.py:316
  34.2 0.0 copy-start.2
  34.2 0.0 copy-start.7
  34.2 0.0 copy-start.8
  34.2 0.0 copy-start.9
  34.2 0.0 copy-start.11
  34.2 4.4 %collective-permute-start.2 = (bf16[384,1536]{1,0:T(8,128)(2,1)S(1)}, bf16[384,1536]{1,0:T(8,128)(2,1)S(1)}, u32[]{:S(2)}, u32[]{:S(2)}) collective-permute-start(bf16[384,1536]{1,0:T(8,128)(2,1)S(1)} %broadcast_select_fusion.1), channel_id=1, source_target_pairs={{0,4},{4,8},{8,12},{12,16},{16,20},{20,24},{24,28},{28,32},{32,36}... | collective-permute-start | bytes 3538952 | tf_op jit(solution)/shard_map/ppermute | solution.py:303
  38.7 0.1 collective-permute-start.1
  38.8 1.5 %collective-permute-done.6.wr = bf16[384,1536]{1,0:T(8,128)(2,1)S(1)} collective-permute-done((bf16[384,1536]{1,0:T(8,128)(2,1)}, bf16[384,1536]{1,0:T(8,128)(2,1)S(1)}, u32[]{:S(2)}, u32[]{:S(2)}) %collective-permute-start.6) | collective-permute-done | bytes 1179680 | tf_op jit(solution)/shard_map/ppermute | solution.py:303
  40.3 1.9 %collective-permute-start.7 = (bf16[384,1536]{1,0:T(8,128)(2,1)S(1)}, bf16[384,1536]{1,0:T(8,128)(2,1)S(1)}, u32[]{:S(2)}, u32[]{:S(2)}) collective-permute-start(bf16[384,1536]{1,0:T(8,128)(2,1)S(1)} %collective-permute-done.6.wr), channel_id=1, source_target_pairs={{0,4},{4,0},{8,12},{12,8},{16,20},{20,16},{24,28},{28,24},{32,36},... | collective-permute-start | bytes 3538952 | tf_op jit(solution)/shard_map/ppermute | solution.py:306
  42.2 0.0 copy-done
  42.2 0.1 broadcast_select_fusion
  42.3 1.9 %collective-permute-start.8 = (bf16[384,1536]{1,0:T(8,128)(2,1)S(1)}, bf16[384,1536]{1,0:T(8,128)(2,1)S(1)}, u32[]{:S(2)}, u32[]{:S(2)}) collective-permute-start(bf16[384,1536]{1,0:T(8,128)(2,1)S(1)} %broadcast_select_fusion), channel_id=1, source_target_pairs={{4,0},{8,4},{12,8},{16,12},{20,16},{24,20},{28,24},{32,28},{36,32}... | collective-permute-start | bytes 3538952 | tf_op jit(solution)/shard_map/ppermute | solution.py:303
  44.2 0.0 copy-done.2
  44.2 0.0 copy-done.7
  44.2 0.0 copy-done.8
  44.3 0.0 copy-done.9
  44.3 0.0 copy-done.11
  44.3 0.0 copy-start.4
  44.3 3.4 %inner.1 = (f32[128,1536]{1,0:T(8,128)S(1)}, f32[128,1536]{1,0:T(8,128)S(1)}, f32[128,1536]{1,0:T(8,128)S(1)}) custom-call(f32[8,128]{1,0:T(8,128)S(1)} %copy-done.11, f32[512,128]{1,0:T(8,128)S(1)} %copy-done.2, bf16[384,1536]{1,0:T(8,128)(2,1)S(1)} %copy-done, bf16[128,1536]{1,0:T(8,128)(2,1)S(1)} %copy-done.7, bf16[128,1536]{1,0:T(8,128)(2,1)S(1)} %copy-done.8, ...), custom_call_target="tpu_custom_call" | custom-call | flops 251658240 | bytes 4718592 | tf_op jit(solution)/shard_map/inner/pallas_call | solution.py:272
  47.7 0.0 collective-permute-done.1.wa
  47.7 4.1 %collective-permute-done.2.wx = bf16[384,1536]{1,0:T(8,128)(2,1)S(1)} collective-permute-done((bf16[384,1536]{1,0:T(8,128)(2,1)S(1)}, bf16[384,1536]{1,0:T(8,128)(2,1)S(1)}, u32[]{:S(2)}, u32[]{:S(2)}) %collective-permute-start.2) | collective-permute-done | bytes 1179680 | tf_op jit(solution)/shard_map/ppermute | solution.py:303
  51.8 0.0 copy-done.4
  51.8 8.1 %queries.1 = (bf16[128,1536]{1,0:T(8,128)(2,1)}, bf16[128,1536]{1,0:T(8,128)(2,1)}, f32[40,128]{1,0:T(8,128)S(1)}, f32[128,128]{1,0:T(8,128)}) custom-call(s32[1]{0:T(128)} %bitcast.place, f32[8,128]{1,0:T(8,128)S(1)} %copy-done.11, f32[512,128]{1,0:T(8,128)S(1)} %copy-done.2, bf16[384,1536]{1,0:T(8,128)(2,1)S(1)} %copy-done.4, ...), custom_call_target="tpu_custom_call" | custom-call | flops 805306368 | bytes 7864320 | tf_op jit(solution)/shard_map/queries/pallas_call | solution.py:272
  59.9 0.1 collective-permute-start.3
  60.0 9.0 %collective-permute-start.4 = (f32[40,128]{1,0:T(8,128)S(1)}, f32[40,128]{1,0:T(8,128)S(1)}, u32[]{:S(2)}, u32[]{:S(2)}) collective-permute-start(f32[40,128]{1,0:T(8,128)S(1)} %get-tuple-element.37.s0), channel_id=1, source_target_pairs={{0,248},{4,252},{8,0},{12,4},{16,8},{20,12},{24,16},{28,20},{32,24... | collective-permute-start | bytes 61448 | tf_op jit(solution)/shard_map/ppermute | solution.py:346
  69.0 1.0 %collective-permute-start.5 = (f32[40,128]{1,0:T(8,128)S(1)}, f32[40,128]{1,0:T(8,128)S(1)}, u32[]{:S(2)}, u32[]{:S(2)}) collective-permute-start(f32[40,128]{1,0:T(8,128)S(1)} %get-tuple-element.37.s0), channel_id=1, source_target_pairs={{0,244},{4,248},{8,252},{12,0},{16,4},{20,8},{24,12},{28,16},{32,2... | collective-permute-start | bytes 61448 | tf_op jit(solution)/shard_map/ppermute | solution.py:346
  70.0 0.0 collective-permute-done.7.wa
  70.0 0.0 collective-permute-done.8.wx
  70.0 1.7 %lin_keys.1 = (bf16[128,1536]{1,0:T(8,128)(2,1)}, bf16[128,1536]{1,0:T(8,128)(2,1)}) custom-call(s32[1]{0:T(128)} %bitcast.place, f32[512,128]{1,0:T(8,128)S(1)} %copy-done.2, bf16[128,1536]{1,0:T(8,128)(2,1)S(1)} %copy-done.8, bf16[128,1536]{1,0:T(8,128)(2,1)S(1)} %copy-done.9, f32[128,1536]{1,0:T(8,128)S(1)} %get-tuple-element.38.dk, ...), custom_call_target="tpu_custom_call" | custom-call | flops 100663296 | bytes 4325376 | tf_op jit(solution)/shard_map/lin_keys/pallas_call | solution.py:272
  71.8 0.0 collective-permute-done.3.s1
  71.8 0.0 collective-permute-done.4.s2
  71.8 1.3 %collective-permute-done.5.s3 = f32[40,128]{1,0:T(8,128)S(1)} collective-permute-done((f32[40,128]{1,0:T(8,128)S(1)}, f32[40,128]{1,0:T(8,128)S(1)}, u32[]{:S(2)}, u32[]{:S(2)}) %collective-permute-start.5) | collective-permute-done | bytes 20512 | tf_op jit(solution)/shard_map/ppermute | solution.py:346
  73.1 0.6 broadcast_in_dim.2
  73.8 9.6 %all-to-all-start = ((f32[64,1,128]{2,1,0:T(1,128)}), f32[64,1,128]{2,1,0:T(1,128)S(1)}, u32[]{:S(2)}, u32[]{:S(2)}) async-start(f32[64,1,128]{2,1,0:T(1,128)} %broadcast_in_dim.2), calls=%async_computation | async-start | bytes 65536 | tf_op jit(solution)/shard_map/all_to_all | solution.py:375
  83.4 0.0 copy-done.12
  83.4 0.0 copy-done.13
  83.4 0.0 copy-done.14
  83.4 6.2 %soft_keys.1 = (bf16[128,1536]{1,0:T(8,128)(2,1)}, bf16[128,1536]{1,0:T(8,128)(2,1)}) custom-call(s32[1]{0:T(128)} %bitcast.place, f32[512,128]{1,0:T(8,128)} %get-tuple-element.33.mc, bf16[128,1536]{1,0:T(8,128)(2,1)} %k0.1, bf16[128,1536]{1,0:T(8,128)(2,1)} %v0.1, bf16[384,1536]{1,0:T(8,128)(2,1)} %pack_backward.1.b_own, bf16[384,1536]{1,0:T(8,128)(2,1)} %copy-done.1, ...), custom_call_target="tpu_custom_call" | custom-call | flops 805306368 | bytes 6684672 | tf_op jit(solution)/shard_map/soft_keys/pallas_call | solution.py:272
  89.6 4.5 %all-to-all-done = f32[64,1,128]{2,1,0:T(1,128)S(1)} async-done(((f32[64,1,128]{2,1,0:T(1,128)}), f32[64,1,128]{2,1,0:T(1,128)S(1)}, u32[]{:S(2)}, u32[]{:S(2)}) %all-to-all-start) | async-done | bytes 32800 | tf_op jit(solution)/shard_map/all_to_all | solution.py:375
  94.1 0.5 reduce_sum.9
  (13 shorter events, 0.0 us)
Async XLA Ops:
  3.5 29.3 %collective-permute-start = (bf16[384,1536]{1,0:T(8,128)(2,1)}, bf16[384,1536]{1,0:T(8,128)(2,1)}, u32[]{:S(2)}, u32[]{:S(2)}) collective-permute-start(bf16[384,1536]{1,0:T(8,128)(2,1)} %get-tuple-element.34.f_own), channel_id=1, source_target_pairs={{0,8},{4,12},{8,16},{12,20},{16,24},{20,28},{24,32},{28,36},{32,40... | collective-permute-start | bytes 3538952 | tf_op jit(solution)/shard_map/ppermute | solution.py:303
  8.9 23.9 %copy-start.3 = (bf16[384,1536]{1,0:T(8,128)(2,1)S(1)}, bf16[384,1536]{1,0:T(8,128)(2,1)}, u32[]{:S(2)}) copy-start(bf16[384,1536]{1,0:T(8,128)(2,1)} %get-tuple-element.34.f_own) | copy-start | bytes 3538948
  11.7 28.6 %collective-permute-start.6 = (bf16[384,1536]{1,0:T(8,128)(2,1)}, bf16[384,1536]{1,0:T(8,128)(2,1)S(1)}, u32[]{:S(2)}, u32[]{:S(2)}) collective-permute-start(bf16[384,1536]{1,0:T(8,128)(2,1)} %pack_backward.1.b_own), channel_id=1, source_target_pairs={{8,0},{12,4},{16,8},{20,12},{24,16},{28,20},{32,24},{36,28},{40,32... | collective-permute-start | bytes 3538952 | tf_op jit(solution)/shard_map/ppermute | solution.py:303
  13.0 29.2 %copy-start = (bf16[384,1536]{1,0:T(8,128)(2,1)S(1)}, bf16[384,1536]{1,0:T(8,128)(2,1)}, u32[]{:S(2)}) copy-start(bf16[384,1536]{1,0:T(8,128)(2,1)} %pack_backward.1.b_own) | copy-start | bytes 3538948
  34.2 10.0 %copy-start.2 = (f32[512,128]{1,0:T(8,128)S(1)}, f32[512,128]{1,0:T(8,128)}, u32[]{:S(2)}) copy-start(f32[512,128]{1,0:T(8,128)} %get-tuple-element.33.mc) | copy-start | bytes 786436
  34.2 10.0 %copy-start.7 = (bf16[128,1536]{1,0:T(8,128)(2,1)S(1)}, bf16[128,1536]{1,0:T(8,128)(2,1)}, u32[]{:S(2)}) copy-start(bf16[128,1536]{1,0:T(8,128)(2,1)} %lq.5) | copy-start | bytes 1179652
  34.2 10.0 %copy-start.8 = (bf16[128,1536]{1,0:T(8,128)(2,1)S(1)}, bf16[128,1536]{1,0:T(8,128)(2,1)}, u32[]{:S(2)}) copy-start(bf16[128,1536]{1,0:T(8,128)(2,1)} %lk.5) | copy-start | bytes 1179652
  34.2 10.0 %copy-start.9 = (bf16[128,1536]{1,0:T(8,128)(2,1)S(1)}, bf16[128,1536]{1,0:T(8,128)(2,1)}, u32[]{:S(2)}) copy-start(bf16[128,1536]{1,0:T(8,128)(2,1)} %lv.5) | copy-start | bytes 1179652
  34.2 10.0 %copy-start.11 = (f32[8,128]{1,0:T(8,128)S(1)}, f32[8,128]{1,0:T(8,128)}, u32[]{:S(2)}) copy-start(f32[8,128]{1,0:T(8,128)} %get-tuple-element.32.mr) | copy-start | bytes 12292
  34.2 17.5 %collective-permute-start.2 = (bf16[384,1536]{1,0:T(8,128)(2,1)S(1)}, bf16[384,1536]{1,0:T(8,128)(2,1)S(1)}, u32[]{:S(2)}, u32[]{:S(2)}) collective-permute-start(bf16[384,1536]{1,0:T(8,128)(2,1)S(1)} %broadcast_select_fusion.1), channel_id=1, source_target_pairs={{0,4},{4,8},{8,12},{12,16},{16,20},{20,24},{24,28},{28,32},{32,36}... | collective-permute-start | bytes 3538952 | tf_op jit(solution)/shard_map/ppermute | solution.py:303
  38.7 9.0 %collective-permute-start.1 = (bf16[384,1536]{1,0:T(8,128)(2,1)}, bf16[384,1536]{1,0:T(8,128)(2,1)S(1)}, u32[]{:S(2)}, u32[]{:S(2)}) collective-permute-start(bf16[384,1536]{1,0:T(8,128)(2,1)} %collective-permute-done.wr), channel_id=1, source_target_pairs={{0,4},{4,0},{8,12},{12,8},{16,20},{20,16},{24,28},{28,24},{32,36},... | collective-permute-start | bytes 3538952 | tf_op jit(solution)/shard_map/ppermute | solution.py:306
  40.3 29.7 %copy-start.1 = (bf16[384,1536]{1,0:T(8,128)(2,1)}, bf16[384,1536]{1,0:T(8,128)(2,1)S(1)}, u32[]{:S(2)}) copy-start(bf16[384,1536]{1,0:T(8,128)(2,1)S(1)} %collective-permute-done.6.wr) | copy-start | bytes 3538948
  40.3 29.7 %collective-permute-start.7 = (bf16[384,1536]{1,0:T(8,128)(2,1)S(1)}, bf16[384,1536]{1,0:T(8,128)(2,1)S(1)}, u32[]{:S(2)}, u32[]{:S(2)}) collective-permute-start(bf16[384,1536]{1,0:T(8,128)(2,1)S(1)} %collective-permute-done.6.wr), channel_id=1, source_target_pairs={{0,4},{4,0},{8,12},{12,8},{16,20},{20,16},{24,28},{28,24},{32,36},... | collective-permute-start | bytes 3538952 | tf_op jit(solution)/shard_map/ppermute | solution.py:306
  42.3 27.7 %collective-permute-start.8 = (bf16[384,1536]{1,0:T(8,128)(2,1)S(1)}, bf16[384,1536]{1,0:T(8,128)(2,1)S(1)}, u32[]{:S(2)}, u32[]{:S(2)}) collective-permute-start(bf16[384,1536]{1,0:T(8,128)(2,1)S(1)} %broadcast_select_fusion), channel_id=1, source_target_pairs={{4,0},{8,4},{12,8},{16,12},{20,16},{24,20},{28,24},{32,28},{36,32}... | collective-permute-start | bytes 3538952 | tf_op jit(solution)/shard_map/ppermute | solution.py:303
  44.3 7.5 %copy-start.4 = (bf16[384,1536]{1,0:T(8,128)(2,1)S(1)}, bf16[384,1536]{1,0:T(8,128)(2,1)}, u32[]{:S(2)}) copy-start(bf16[384,1536]{1,0:T(8,128)(2,1)} %get-tuple-element.34.f_own) | copy-start | bytes 3538948
  59.9 13.2 %copy-start.10 = (f32[40,128]{1,0:T(8,128)}, f32[40,128]{1,0:T(8,128)S(1)}, u32[]{:S(2)}) copy-start(f32[40,128]{1,0:T(8,128)S(1)} %get-tuple-element.37.s0) | copy-start | bytes 61444
  59.9 11.8 %collective-permute-start.3 = (f32[40,128]{1,0:T(8,128)S(1)}, f32[40,128]{1,0:T(8,128)S(1)}, u32[]{:S(2)}, u32[]{:S(2)}) collective-permute-start(f32[40,128]{1,0:T(8,128)S(1)} %get-tuple-element.37.s0), channel_id=1, source_target_pairs={{0,252},{4,0},{8,4},{12,8},{16,12},{20,16},{24,20},{28,24},{32,28}... | collective-permute-start | bytes 61448 | tf_op jit(solution)/shard_map/ppermute | solution.py:346
  60.0 11.7 %collective-permute-start.4 = (f32[40,128]{1,0:T(8,128)S(1)}, f32[40,128]{1,0:T(8,128)S(1)}, u32[]{:S(2)}, u32[]{:S(2)}) collective-permute-start(f32[40,128]{1,0:T(8,128)S(1)} %get-tuple-element.37.s0), channel_id=1, source_target_pairs={{0,248},{4,252},{8,0},{12,4},{16,8},{20,12},{24,16},{28,20},{32,24... | collective-permute-start | bytes 61448 | tf_op jit(solution)/shard_map/ppermute | solution.py:346
  69.0 4.1 %collective-permute-start.5 = (f32[40,128]{1,0:T(8,128)S(1)}, f32[40,128]{1,0:T(8,128)S(1)}, u32[]{:S(2)}, u32[]{:S(2)}) collective-permute-start(f32[40,128]{1,0:T(8,128)S(1)} %get-tuple-element.37.s0), channel_id=1, source_target_pairs={{0,244},{4,248},{8,252},{12,0},{16,4},{20,8},{24,12},{28,16},{32,2... | collective-permute-start | bytes 61448 | tf_op jit(solution)/shard_map/ppermute | solution.py:346
  70.0 1.8 %copy-start.5 = (bf16[384,1536]{1,0:T(8,128)(2,1)}, bf16[384,1536]{1,0:T(8,128)(2,1)S(1)}, u32[]{:S(2)}) copy-start(bf16[384,1536]{1,0:T(8,128)(2,1)S(1)} %collective-permute-done.7.wa) | copy-start | bytes 3538948
  70.0 1.8 %copy-start.6 = (bf16[384,1536]{1,0:T(8,128)(2,1)}, bf16[384,1536]{1,0:T(8,128)(2,1)S(1)}, u32[]{:S(2)}) copy-start(bf16[384,1536]{1,0:T(8,128)(2,1)S(1)} %collective-permute-done.8.wx) | copy-start | bytes 3538948
  71.8 11.6 %copy-start.12 = (f32[40,128]{1,0:T(8,128)}, f32[40,128]{1,0:T(8,128)S(1)}, u32[]{:S(2)}) copy-start(f32[40,128]{1,0:T(8,128)S(1)} %collective-permute-done.3.s1) | copy-start | bytes 61444
  71.8 11.6 %copy-start.13 = (f32[40,128]{1,0:T(8,128)}, f32[40,128]{1,0:T(8,128)S(1)}, u32[]{:S(2)}) copy-start(f32[40,128]{1,0:T(8,128)S(1)} %collective-permute-done.4.s2) | copy-start | bytes 61444
  73.1 10.2 %copy-start.14 = (f32[40,128]{1,0:T(8,128)}, f32[40,128]{1,0:T(8,128)S(1)}, u32[]{:S(2)}) copy-start(f32[40,128]{1,0:T(8,128)S(1)} %collective-permute-done.5.s3) | copy-start | bytes 61444
  73.8 20.4 %all-to-all-start = ((f32[64,1,128]{2,1,0:T(1,128)}), f32[64,1,128]{2,1,0:T(1,128)S(1)}, u32[]{:S(2)}, u32[]{:S(2)}) async-start(f32[64,1,128]{2,1,0:T(1,128)} %broadcast_in_dim.2), calls=%async_computation | async-start | bytes 65536 | tf_op jit(solution)/shard_map/all_to_all | solution.py:375

commit v5 on v4

--- a/solution.py
+++ b/solution.py
@@ -18,6 +18,7 @@
 PARTS = 1
 RIDE = 4
 QUERY_STEP = 6
+LIN_STEP = 12
 VMEM = 16 * 1024 * 1024
 PACK_VMEM = 60 * 1024 * 1024
 
@@ -177,7 +178,7 @@
         sub, lane = iota(square, 0), iota(square, 1)
         cm[...] = jnp.where((mc[0:rows, :] == mr[0:1, :]) & (sub <= lane), LIN_SCALE, 0.0)
 
-    for h in range(HEADS_STEP):
+    for h in range(LIN_STEP):
         c = cols(h)
         grad = b_own[rows : 2 * rows, c]
         k, q = lk[:, c], lq[:, c]
@@ -195,7 +196,7 @@
     extended = jnp.where(end_c > ((block + 1) * rows).astype(F32), LIN_SCALE, 0.0)
     last = end_c[rows - 1 : rows, :]
     coef = [jnp.where(last > ((block + o) * rows).astype(F32), 1.0, 0.0) for o in offsets(block % 2, False)]
-    for h in range(HEADS_STEP):
+    for h in range(LIN_STEP):
         c = cols(h)
         later = sum(f * w[:, c].astype(F32) for f, w in zip(coef, (wr, wa, wx))).astype(BF16)
         ldk[:, c] = (dk[:, c] + extended * nt(lv[:, c], later)).astype(BF16)
@@ -319,8 +320,8 @@
 
     wide = jax.ShapeDtypeStruct((rows, feats), F32)
     dq_inner, dk_inner, dv_inner = call(
-        inner_kernel, "inner", feats // HD // HEADS_STEP,
-        [whole(8), whole(4 * rows), tall(3)] + [tall(1)] * 3, [tall(1)] * 3, [wide] * 3, [(rows, HD)],
+        inner_kernel, "inner", feats // HD // LIN_STEP,
+        [whole(8), whole(4 * rows), tall(3, LIN_STEP)] + [tall(1, LIN_STEP)] * 3, [tall(1, LIN_STEP)] * 3, [wide] * 3, [(rows, HD)],
         5 * mm, 12 * unit,
         (mr, mc, bwd, lin_query, lin_key, lin_value),
     )
@@ -346,13 +347,13 @@
         lax.ppermute(stats, "ctx", [(i, (i - o) % count) for i in range(count)]) for o in range(1, RIDE)
     )
 
-    state = pl.BlockSpec((rows, HEADS_STEP * HD), lambda i: (2, i))
+    state = pl.BlockSpec((rows, LIN_STEP * HD), lambda i: (2, i))
 
     def lin_keys_side(*bwds):
         return call(
-            lin_key_kernel, "lin_keys", feats // HD // HEADS_STEP,
-            [smem, whole(4 * rows)] + [tall(1)] * 4 + [state] * 3,
-            [tall(1), tall(1)], [array(1)] * 2, [],
+            lin_key_kernel, "lin_keys", feats // HD // LIN_STEP,
+            [smem, whole(4 * rows)] + [tall(1, LIN_STEP)] * 4 + [state] * 3,
+            [tall(1, LIN_STEP), tall(1, LIN_STEP)], [array(1)] * 2, [],
             2 * mm, 11 * unit,
             (place, mc, lin_key, lin_value, dk_inner, dv_inner, *bwds),
         )

time: 95 us -> 95 us (level)
  transfers between devices with their start and end apart: 10 -> 10, of which waited for: 5 -> 5; matrix products, arithmetic and copies ran while one was open for 2% -> 2% of each run, Pallas kernels for 24% -> 23%
where the time goes in v5:
time: 95 us; the launch traced here: 94.7 us
  starting transfers between devices  34.6 us (36%)
  waiting for transfers between devices  31.9 us (34%)
  Pallas kernels  24.5 us (26%)
  other arithmetic  2.06 us (2%)
    ppermute x4, waiting for transfers between devices, shift(): lax.ppermute(x, 'ctx', [(i, i + by) for i in range(count) if 0 <= i + by...  25.9 us
    pallas_call x6, Pallas kernels, call(): pl.pallas_call(kernel, name=name, grid=(steps,), in_specs=in_specs, out_s...  24.5 us
    ppermute x4, starting transfers between devices, shift(): lax.ppermute(x, 'ctx', [(i, i + by) for i in range(count) if 0 <= i + by...  13 us
    ppermute x3, starting transfers between devices, on_device(): lax.ppermute(stats, 'ctx', [(i, (i - o) % count) for i in range(count)])  10 us
    all_to_all x1, starting transfers between devices, on_device(): lax.all_to_all(jnp.broadcast_to(vec, (slots, HD)), ('ctx', 'head'), 0, 0,...  9.57 us
    all_to_all x1, waiting for transfers between devices, on_device(): lax.all_to_all(jnp.broadcast_to(vec, (slots, HD)), ('ctx', 'head'), 0, 0,...  4.53 us
    ppermute x2, starting transfers between devices, swap(): return lax.ppermute(x, 'ctx', [(i, i ^ 1) for i in range(count)])  1.96 us
  transfers between devices with their start and end apart: 10, of which 5 were waited for; matrix products, arithmetic and copies ran while one was open for 2% of the time, Pallas kernels for 23%

profile of v5, /device:TPU:1, one launch (start us, length us, event | category | flops | bytes accessed | tf_op | source)
XLA Modules:
  0.0 94.7 jit_solution(17610743276225220139)
XLA Ops:
  0.6 2.9 %pack_forward.1 = (bf16[384,1536]{1,0:T(8,128)(2,1)}, f32[8,128]{1,0:T(8,128)}, f32[512,128]{1,0:T(8,128)}) custom-call(s32[42]{0:T(128)} %lens.1, s32[42]{0:T(128)} %doms.1, f32[8]{0:T(128)} %wts.1, s32[1]{0:T(128)} %bitcast.place, bf16[128,1536]{1,0:T(8,128)(2,1)} %lk.5, bf16[128,1536]{1,0:T(8,128)(2,1)} %lv.5, bf16[128,1536]{1,0:T(8,128)(2,1)} %k0.1, ...), custom_call_target="tpu_custom_call" | custom-call | flops 50331648 | bytes 2752512 | tf_op jit(solution)/shard_map/pack_forward/pallas_call | solution.py:273
  3.5 5.4 %collective-permute-start = (bf16[384,1536]{1,0:T(8,128)(2,1)}, bf16[384,1536]{1,0:T(8,128)(2,1)}, u32[]{:S(2)}, u32[]{:S(2)}) collective-permute-start(bf16[384,1536]{1,0:T(8,128)(2,1)} %get-tuple-element.34.f_own), channel_id=1, source_target_pairs={{0,8},{4,12},{8,16},{12,20},{16,24},{20,28},{24,32},{28,36},{32,40... | collective-permute-start | bytes 3538952 | tf_op jit(solution)/shard_map/ppermute | solution.py:304
  8.9 2.8 %pack_backward.1.b_own = bf16[384,1536]{1,0:T(8,128)(2,1)} custom-call(f32[512,128]{1,0:T(8,128)} %get-tuple-element.33.mc, bf16[128,1536]{1,0:T(8,128)(2,1)} %lq.5, bf16[128,1536]{1,0:T(8,128)(2,1)} %sq.1, bf16[128,1536]{1,0:T(8,128)(2,1)} %up.1), custom_call_target="tpu_custom_call" | custom-call | flops 50331648 | bytes 2359296 | tf_op jit(solution)/shard_map/pack_backward/pallas_call | solution.py:273
  11.7 1.3 %collective-permute-start.6 = (bf16[384,1536]{1,0:T(8,128)(2,1)}, bf16[384,1536]{1,0:T(8,128)(2,1)S(1)}, u32[]{:S(2)}, u32[]{:S(2)}) collective-permute-start(bf16[384,1536]{1,0:T(8,128)(2,1)} %pack_backward.1.b_own), channel_id=1, source_target_pairs={{8,0},{12,4},{16,8},{20,12},{24,16},{28,20},{32,24},{36,28},{40,32... | collective-permute-start | bytes 3538952 | tf_op jit(solution)/shard_map/ppermute | solution.py:304
  13.0 0.0 copy-start
  13.0 19.8 %collective-permute-done.wr = bf16[384,1536]{1,0:T(8,128)(2,1)} collective-permute-done((bf16[384,1536]{1,0:T(8,128)(2,1)}, bf16[384,1536]{1,0:T(8,128)(2,1)}, u32[]{:S(2)}, u32[]{:S(2)}) %collective-permute-start) | collective-permute-done | bytes 1179680 | tf_op jit(solution)/shard_map/ppermute | solution.py:304
  32.8 0.0 copy-done.3
  32.8 1.4 %broadcast_select_fusion.1 = bf16[384,1536]{1,0:T(8,128)(2,1)S(1)} fusion(bf16[384,1536]{1,0:T(8,128)(2,1)} %collective-permute-done.wr, bf16[384,1536]{1,0:T(8,128)(2,1)S(1)} %copy-done.3, pred[]{:T(512)S(6)} %eq.5), kind=kLoop, calls=%fused_computation.1 | loop fusion | flops 589824 | bytes 3538945 | tf_op jit(solution)/shard_map/jit(_where)/select_n | solution.py:317
  34.2 0.0 copy-start.2
  34.2 0.0 copy-start.7
  34.2 0.0 copy-start.8
  34.2 0.0 copy-start.9
  34.2 0.0 copy-start.11
  34.2 4.4 %collective-permute-start.2 = (bf16[384,1536]{1,0:T(8,128)(2,1)S(1)}, bf16[384,1536]{1,0:T(8,128)(2,1)S(1)}, u32[]{:S(2)}, u32[]{:S(2)}) collective-permute-start(bf16[384,1536]{1,0:T(8,128)(2,1)S(1)} %broadcast_select_fusion.1), channel_id=1, source_target_pairs={{0,4},{4,8},{8,12},{12,16},{16,20},{20,24},{24,28},{28,32},{32,36}... | collective-permute-start | bytes 3538952 | tf_op jit(solution)/shard_map/ppermute | solution.py:304
  38.7 0.1 collective-permute-start.1
  38.8 1.5 %collective-permute-done.6.wr = bf16[384,1536]{1,0:T(8,128)(2,1)S(1)} collective-permute-done((bf16[384,1536]{1,0:T(8,128)(2,1)}, bf16[384,1536]{1,0:T(8,128)(2,1)S(1)}, u32[]{:S(2)}, u32[]{:S(2)}) %collective-permute-start.6) | collective-permute-done | bytes 1179680 | tf_op jit(solution)/shard_map/ppermute | solution.py:304
  40.3 1.9 %collective-permute-start.7 = (bf16[384,1536]{1,0:T(8,128)(2,1)S(1)}, bf16[384,1536]{1,0:T(8,128)(2,1)S(1)}, u32[]{:S(2)}, u32[]{:S(2)}) collective-permute-start(bf16[384,1536]{1,0:T(8,128)(2,1)S(1)} %collective-permute-done.6.wr), channel_id=1, source_target_pairs={{0,4},{4,0},{8,12},{12,8},{16,20},{20,16},{24,28},{28,24},{32,36},... | collective-permute-start | bytes 3538952 | tf_op jit(solution)/shard_map/ppermute | solution.py:307
  42.2 0.0 copy-done
  42.2 0.1 broadcast_select_fusion
  42.3 1.9 %collective-permute-start.8 = (bf16[384,1536]{1,0:T(8,128)(2,1)S(1)}, bf16[384,1536]{1,0:T(8,128)(2,1)S(1)}, u32[]{:S(2)}, u32[]{:S(2)}) collective-permute-start(bf16[384,1536]{1,0:T(8,128)(2,1)S(1)} %broadcast_select_fusion), channel_id=1, source_target_pairs={{4,0},{8,4},{12,8},{16,12},{20,16},{24,20},{28,24},{32,28},{36,32}... | collective-permute-start | bytes 3538952 | tf_op jit(solution)/shard_map/ppermute | solution.py:304
  44.2 0.0 copy-done.2
  44.2 0.0 copy-done.7
  44.2 0.0 copy-done.8
  44.3 0.0 copy-done.9
  44.3 0.0 copy-done.11
  44.3 0.0 copy-start.4
  44.3 2.9 %inner.1 = (f32[128,1536]{1,0:T(8,128)S(1)}, f32[128,1536]{1,0:T(8,128)S(1)}, f32[128,1536]{1,0:T(8,128)S(1)}) custom-call(f32[8,128]{1,0:T(8,128)S(1)} %copy-done.11, f32[512,128]{1,0:T(8,128)S(1)} %copy-done.2, bf16[384,1536]{1,0:T(8,128)(2,1)S(1)} %copy-done, bf16[128,1536]{1,0:T(8,128)(2,1)S(1)} %copy-done.7, bf16[128,1536]{1,0:T(8,128)(2,1)S(1)} %copy-done.8, ...), custom_call_target="tpu_custom_call" | custom-call | flops 251658240 | bytes 4718592 | tf_op jit(solution)/shard_map/inner/pallas_call | solution.py:273
  47.2 0.0 collective-permute-done.1.wa
  47.2 4.6 %collective-permute-done.2.wx = bf16[384,1536]{1,0:T(8,128)(2,1)S(1)} collective-permute-done((bf16[384,1536]{1,0:T(8,128)(2,1)S(1)}, bf16[384,1536]{1,0:T(8,128)(2,1)S(1)}, u32[]{:S(2)}, u32[]{:S(2)}) %collective-permute-start.2) | collective-permute-done | bytes 1179680 | tf_op jit(solution)/shard_map/ppermute | solution.py:304
  51.8 8.1 %queries.1 = (bf16[128,1536]{1,0:T(8,128)(2,1)}, bf16[128,1536]{1,0:T(8,128)(2,1)}, f32[40,128]{1,0:T(8,128)S(1)}, f32[128,128]{1,0:T(8,128)}) custom-call(s32[1]{0:T(128)} %bitcast.place, f32[8,128]{1,0:T(8,128)S(1)} %copy-done.11, f32[512,128]{1,0:T(8,128)S(1)} %copy-done.2, bf16[384,1536]{1,0:T(8,128)(2,1)S(1)} %copy-done.4, ...), custom_call_target="tpu_custom_call" | custom-call | flops 805306368 | bytes 7864320 | tf_op jit(solution)/shard_map/queries/pallas_call | solution.py:273
  59.9 0.1 collective-permute-start.3
  60.0 9.0 %collective-permute-start.4 = (f32[40,128]{1,0:T(8,128)S(1)}, f32[40,128]{1,0:T(8,128)S(1)}, u32[]{:S(2)}, u32[]{:S(2)}) collective-permute-start(f32[40,128]{1,0:T(8,128)S(1)} %get-tuple-element.37.s0), channel_id=1, source_target_pairs={{0,248},{4,252},{8,0},{12,4},{16,8},{20,12},{24,16},{28,20},{32,24... | collective-permute-start | bytes 61448 | tf_op jit(solution)/shard_map/ppermute | solution.py:347
  69.0 1.0 %collective-permute-start.5 = (f32[40,128]{1,0:T(8,128)S(1)}, f32[40,128]{1,0:T(8,128)S(1)}, u32[]{:S(2)}, u32[]{:S(2)}) collective-permute-start(f32[40,128]{1,0:T(8,128)S(1)} %get-tuple-element.37.s0), channel_id=1, source_target_pairs={{0,244},{4,248},{8,252},{12,0},{16,4},{20,8},{24,12},{28,16},{32,2... | collective-permute-start | bytes 61448 | tf_op jit(solution)/shard_map/ppermute | solution.py:347
  70.0 0.0 collective-permute-done.7.wa
  70.0 0.0 collective-permute-done.8.wx
  70.0 1.6 %lin_keys.1 = (bf16[128,1536]{1,0:T(8,128)(2,1)}, bf16[128,1536]{1,0:T(8,128)(2,1)}) custom-call(s32[1]{0:T(128)} %bitcast.place, f32[512,128]{1,0:T(8,128)S(1)} %copy-done.2, bf16[128,1536]{1,0:T(8,128)(2,1)S(1)} %copy-done.8, bf16[128,1536]{1,0:T(8,128)(2,1)S(1)} %copy-done.9, f32[128,1536]{1,0:T(8,128)S(1)} %get-tuple-element.38.dk, ...), custom_call_target="tpu_custom_call" | custom-call | flops 100663296 | bytes 4325376 | tf_op jit(solution)/shard_map/lin_keys/pallas_call | solution.py:273
  71.6 0.0 copy-done.6
  71.7 0.0 collective-permute-done.3.s1
  71.7 0.0 collective-permute-done.4.s2
  71.7 1.4 %collective-permute-done.5.s3 = f32[40,128]{1,0:T(8,128)S(1)} collective-permute-done((f32[40,128]{1,0:T(8,128)S(1)}, f32[40,128]{1,0:T(8,128)S(1)}, u32[]{:S(2)}, u32[]{:S(2)}) %collective-permute-start.5) | collective-permute-done | bytes 20512 | tf_op jit(solution)/shard_map/ppermute | solution.py:347
  73.1 0.6 broadcast_in_dim.2
  73.8 9.6 %all-to-all-start = ((f32[64,1,128]{2,1,0:T(1,128)}), f32[64,1,128]{2,1,0:T(1,128)S(1)}, u32[]{:S(2)}, u32[]{:S(2)}) async-start(f32[64,1,128]{2,1,0:T(1,128)} %broadcast_in_dim.2), calls=%async_computation | async-start | bytes 65536 | tf_op jit(solution)/shard_map/all_to_all | solution.py:376
  83.4 0.0 copy-done.12
  83.4 0.0 copy-done.13
  83.4 0.0 copy-done.14
  83.4 6.2 %soft_keys.1 = (bf16[128,1536]{1,0:T(8,128)(2,1)}, bf16[128,1536]{1,0:T(8,128)(2,1)}) custom-call(s32[1]{0:T(128)} %bitcast.place, f32[512,128]{1,0:T(8,128)} %get-tuple-element.33.mc, bf16[128,1536]{1,0:T(8,128)(2,1)} %k0.1, bf16[128,1536]{1,0:T(8,128)(2,1)} %v0.1, bf16[384,1536]{1,0:T(8,128)(2,1)} %pack_backward.1.b_own, bf16[384,1536]{1,0:T(8,128)(2,1)} %copy-done.1, ...), custom_call_target="tpu_custom_call" | custom-call | flops 805306368 | bytes 6684672 | tf_op jit(solution)/shard_map/soft_keys/pallas_call | solution.py:273
  89.6 4.5 %all-to-all-done = f32[64,1,128]{2,1,0:T(1,128)S(1)} async-done(((f32[64,1,128]{2,1,0:T(1,128)}), f32[64,1,128]{2,1,0:T(1,128)S(1)}, u32[]{:S(2)}, u32[]{:S(2)}) %all-to-all-start) | async-done | bytes 32800 | tf_op jit(solution)/shard_map/all_to_all | solution.py:376
  94.1 0.5 reduce_sum.9
  (13 shorter events, 0.0 us)
Async XLA Ops:
  3.5 29.3 %collective-permute-start = (bf16[384,1536]{1,0:T(8,128)(2,1)}, bf16[384,1536]{1,0:T(8,128)(2,1)}, u32[]{:S(2)}, u32[]{:S(2)}) collective-permute-start(bf16[384,1536]{1,0:T(8,128)(2,1)} %get-tuple-element.34.f_own), channel_id=1, source_target_pairs={{0,8},{4,12},{8,16},{12,20},{16,24},{20,28},{24,32},{28,36},{32,40... | collective-permute-start | bytes 3538952 | tf_op jit(solution)/shard_map/ppermute | solution.py:304
  8.9 23.9 %copy-start.3 = (bf16[384,1536]{1,0:T(8,128)(2,1)S(1)}, bf16[384,1536]{1,0:T(8,128)(2,1)}, u32[]{:S(2)}) copy-start(bf16[384,1536]{1,0:T(8,128)(2,1)} %get-tuple-element.34.f_own) | copy-start | bytes 3538948
  11.7 28.6 %collective-permute-start.6 = (bf16[384,1536]{1,0:T(8,128)(2,1)}, bf16[384,1536]{1,0:T(8,128)(2,1)S(1)}, u32[]{:S(2)}, u32[]{:S(2)}) collective-permute-start(bf16[384,1536]{1,0:T(8,128)(2,1)} %pack_backward.1.b_own), channel_id=1, source_target_pairs={{8,0},{12,4},{16,8},{20,12},{24,16},{28,20},{32,24},{36,28},{40,32... | collective-permute-start | bytes 3538952 | tf_op jit(solution)/shard_map/ppermute | solution.py:304
  13.0 29.2 %copy-start = (bf16[384,1536]{1,0:T(8,128)(2,1)S(1)}, bf16[384,1536]{1,0:T(8,128)(2,1)}, u32[]{:S(2)}) copy-start(bf16[384,1536]{1,0:T(8,128)(2,1)} %pack_backward.1.b_own) | copy-start | bytes 3538948
  34.2 10.0 %copy-start.2 = (f32[512,128]{1,0:T(8,128)S(1)}, f32[512,128]{1,0:T(8,128)}, u32[]{:S(2)}) copy-start(f32[512,128]{1,0:T(8,128)} %get-tuple-element.33.mc) | copy-start | bytes 786436
  34.2 10.0 %copy-start.7 = (bf16[128,1536]{1,0:T(8,128)(2,1)S(1)}, bf16[128,1536]{1,0:T(8,128)(2,1)}, u32[]{:S(2)}) copy-start(bf16[128,1536]{1,0:T(8,128)(2,1)} %lq.5) | copy-start | bytes 1179652
  34.2 10.0 %copy-start.8 = (bf16[128,1536]{1,0:T(8,128)(2,1)S(1)}, bf16[128,1536]{1,0:T(8,128)(2,1)}, u32[]{:S(2)}) copy-start(bf16[128,1536]{1,0:T(8,128)(2,1)} %lk.5) | copy-start | bytes 1179652
  34.2 10.0 %copy-start.9 = (bf16[128,1536]{1,0:T(8,128)(2,1)S(1)}, bf16[128,1536]{1,0:T(8,128)(2,1)}, u32[]{:S(2)}) copy-start(bf16[128,1536]{1,0:T(8,128)(2,1)} %lv.5) | copy-start | bytes 1179652
  34.2 10.0 %copy-start.11 = (f32[8,128]{1,0:T(8,128)S(1)}, f32[8,128]{1,0:T(8,128)}, u32[]{:S(2)}) copy-start(f32[8,128]{1,0:T(8,128)} %get-tuple-element.32.mr) | copy-start | bytes 12292
  34.2 17.5 %collective-permute-start.2 = (bf16[384,1536]{1,0:T(8,128)(2,1)S(1)}, bf16[384,1536]{1,0:T(8,128)(2,1)S(1)}, u32[]{:S(2)}, u32[]{:S(2)}) collective-permute-start(bf16[384,1536]{1,0:T(8,128)(2,1)S(1)} %broadcast_select_fusion.1), channel_id=1, source_target_pairs={{0,4},{4,8},{8,12},{12,16},{16,20},{20,24},{24,28},{28,32},{32,36}... | collective-permute-start | bytes 3538952 | tf_op jit(solution)/shard_map/ppermute | solution.py:304
  38.7 8.5 %collective-permute-start.1 = (bf16[384,1536]{1,0:T(8,128)(2,1)}, bf16[384,1536]{1,0:T(8,128)(2,1)S(1)}, u32[]{:S(2)}, u32[]{:S(2)}) collective-permute-start(bf16[384,1536]{1,0:T(8,128)(2,1)} %collective-permute-done.wr), channel_id=1, source_target_pairs={{0,4},{4,0},{8,12},{12,8},{16,20},{20,16},{24,28},{28,24},{32,36},... | collective-permute-start | bytes 3538952 | tf_op jit(solution)/shard_map/ppermute | solution.py:307
  40.3 29.7 %copy-start.1 = (bf16[384,1536]{1,0:T(8,128)(2,1)}, bf16[384,1536]{1,0:T(8,128)(2,1)S(1)}, u32[]{:S(2)}) copy-start(bf16[384,1536]{1,0:T(8,128)(2,1)S(1)} %collective-permute-done.6.wr) | copy-start | bytes 3538948
  40.3 29.7 %collective-permute-start.7 = (bf16[384,1536]{1,0:T(8,128)(2,1)S(1)}, bf16[384,1536]{1,0:T(8,128)(2,1)S(1)}, u32[]{:S(2)}, u32[]{:S(2)}) collective-permute-start(bf16[384,1536]{1,0:T(8,128)(2,1)S(1)} %collective-permute-done.6.wr), channel_id=1, source_target_pairs={{0,4},{4,0},{8,12},{12,8},{16,20},{20,16},{24,28},{28,24},{32,36},... | collective-permute-start | bytes 3538952 | tf_op jit(solution)/shard_map/ppermute | solution.py:307
  42.3 27.7 %collective-permute-start.8 = (bf16[384,1536]{1,0:T(8,128)(2,1)S(1)}, bf16[384,1536]{1,0:T(8,128)(2,1)S(1)}, u32[]{:S(2)}, u32[]{:S(2)}) collective-permute-start(bf16[384,1536]{1,0:T(8,128)(2,1)S(1)} %broadcast_select_fusion), channel_id=1, source_target_pairs={{4,0},{8,4},{12,8},{16,12},{20,16},{24,20},{28,24},{32,28},{36,32}... | collective-permute-start | bytes 3538952 | tf_op jit(solution)/shard_map/ppermute | solution.py:304
  44.3 7.5 %copy-start.4 = (bf16[384,1536]{1,0:T(8,128)(2,1)S(1)}, bf16[384,1536]{1,0:T(8,128)(2,1)}, u32[]{:S(2)}) copy-start(bf16[384,1536]{1,0:T(8,128)(2,1)} %get-tuple-element.34.f_own) | copy-start | bytes 3538948
  59.9 13.2 %copy-start.10 = (f32[40,128]{1,0:T(8,128)}, f32[40,128]{1,0:T(8,128)S(1)}, u32[]{:S(2)}) copy-start(f32[40,128]{1,0:T(8,128)S(1)} %get-tuple-element.37.s0) | copy-start | bytes 61444
  59.9 11.7 %collective-permute-start.3 = (f32[40,128]{1,0:T(8,128)S(1)}, f32[40,128]{1,0:T(8,128)S(1)}, u32[]{:S(2)}, u32[]{:S(2)}) collective-permute-start(f32[40,128]{1,0:T(8,128)S(1)} %get-tuple-element.37.s0), channel_id=1, source_target_pairs={{0,252},{4,0},{8,4},{12,8},{16,12},{20,16},{24,20},{28,24},{32,28}... | collective-permute-start | bytes 61448 | tf_op jit(solution)/shard_map/ppermute | solution.py:347
  60.0 11.6 %collective-permute-start.4 = (f32[40,128]{1,0:T(8,128)S(1)}, f32[40,128]{1,0:T(8,128)S(1)}, u32[]{:S(2)}, u32[]{:S(2)}) collective-permute-start(f32[40,128]{1,0:T(8,128)S(1)} %get-tuple-element.37.s0), channel_id=1, source_target_pairs={{0,248},{4,252},{8,0},{12,4},{16,8},{20,12},{24,16},{28,20},{32,24... | collective-permute-start | bytes 61448 | tf_op jit(solution)/shard_map/ppermute | solution.py:347
  69.0 4.1 %collective-permute-start.5 = (f32[40,128]{1,0:T(8,128)S(1)}, f32[40,128]{1,0:T(8,128)S(1)}, u32[]{:S(2)}, u32[]{:S(2)}) collective-permute-start(f32[40,128]{1,0:T(8,128)S(1)} %get-tuple-element.37.s0), channel_id=1, source_target_pairs={{0,244},{4,248},{8,252},{12,0},{16,4},{20,8},{24,12},{28,16},{32,2... | collective-permute-start | bytes 61448 | tf_op jit(solution)/shard_map/ppermute | solution.py:347
  70.0 1.7 %copy-start.5 = (bf16[384,1536]{1,0:T(8,128)(2,1)}, bf16[384,1536]{1,0:T(8,128)(2,1)S(1)}, u32[]{:S(2)}) copy-start(bf16[384,1536]{1,0:T(8,128)(2,1)S(1)} %collective-permute-done.7.wa) | copy-start | bytes 3538948
  70.0 1.6 %copy-start.6 = (bf16[384,1536]{1,0:T(8,128)(2,1)}, bf16[384,1536]{1,0:T(8,128)(2,1)S(1)}, u32[]{:S(2)}) copy-start(bf16[384,1536]{1,0:T(8,128)(2,1)S(1)} %collective-permute-done.8.wx) | copy-start | bytes 3538948
  71.7 11.7 %copy-start.12 = (f32[40,128]{1,0:T(8,128)}, f32[40,128]{1,0:T(8,128)S(1)}, u32[]{:S(2)}) copy-start(f32[40,128]{1,0:T(8,128)S(1)} %collective-permute-done.3.s1) | copy-start | bytes 61444
  71.7 11.7 %copy-start.13 = (f32[40,128]{1,0:T(8,128)}, f32[40,128]{1,0:T(8,128)S(1)}, u32[]{:S(2)}) copy-start(f32[40,128]{1,0:T(8,128)S(1)} %collective-permute-done.4.s2) | copy-start | bytes 61444
  73.1 10.2 %copy-start.14 = (f32[40,128]{1,0:T(8,128)}, f32[40,128]{1,0:T(8,128)S(1)}, u32[]{:S(2)}) copy-start(f32[40,128]{1,0:T(8,128)S(1)} %collective-permute-done.5.s3) | copy-start | bytes 61444
  73.8 20.4 %all-to-all-start = ((f32[64,1,128]{2,1,0:T(1,128)}), f32[64,1,128]{2,1,0:T(1,128)S(1)}, u32[]{:S(2)}, u32[]{:S(2)}) async-start(f32[64,1,128]{2,1,0:T(1,128)} %broadcast_in_dim.2), calls=%async_computation | async-start | bytes 65536 | tf_op jit(solution)/shard_map/all_to_all | solution.py:376
